TPU v7x, 128 devices: a whole 4x4x4 slice. The times are simulated.
128 devices in a mesh: seq: 16 (over y, x), exp: 8 (over z, core).
Axes of the slice: x: 4, y: 4, z: 4, core: 2. Of those that a mesh axis runs over, the one named last changes fastest.
Arguments:
- queries: bfloat16 [512, 64, 576], P(('seq', 'exp')), may hold values from -68 to 68
- own_latent: bfloat16 [512, 576], P(('seq', 'exp')), may hold values from -4 to 4
- snapshots: bfloat16 [2, 8192, 576], P(None, 'seq'), may hold values from -12 to 12
- leaf_snapshot: int32 [512], P(('seq', 'exp')), may hold values from 0 to 1
- moe_input: bfloat16 [512, 7168], P(('seq', 'exp')), may hold values from -6 to 6
- expert_ids: int32 [512, 8], P(('seq', 'exp')), may hold values from 0 to 7, all different within a row; in each aligned block of 4 rows (0 to 3, 4 to 7, ...) at most 4 rows name the same one
- gate_weights: float32 [512, 8], P(('seq', 'exp')), may hold values from 0.05 to 0.5
- w_gate: bfloat16 [8, 7168, 2048], P('exp', None, 'seq'), may hold values from -0.0625 to 0.0625
- w_up: bfloat16 [8, 7168, 2048], P('exp', None, 'seq'), may hold values from -0.0625 to 0.0625
- w_down: bfloat16 [8, 2048, 7168], P('exp', 'seq'), may hold values from -0.125 to 0.125
Outputs:
- attn_latent: bfloat16 [512, 64, 512], P(('seq', 'exp'))
- moe_output: bfloat16 [512, 7168], P(('seq', 'exp'))
Inputs may be any that keep to these rules, and one draw needn't show every extreme that they name: `expert_ids`: each row names 8 different experts; among the 4 rows of one device, no expert is named more than 4 times.
All inputs are finite; a program needn't handle non-finite values.
Results may differ from a plain program's by a relative error of at most 0.02.
Values may be sent and summed in bfloat16 or wider, within the bound.
No kernel may reach another device: no remote copies, remote signals or barrier semaphores. Data moves between devices by JAX's collectives and lax.ppermute only.
A program may use at most 192 MiB of HBM per device.

v0:
```python
import jax
import jax.numpy as jnp
from jax import lax
from jax.sharding import PartitionSpec as P

LAT = 512
TOP = 8


qk_scale = 192.0 ** (-0.5)


def expert_partial(slot_rows, w_gate, w_up, w_down):
    flat_rows = slot_rows.reshape(-1, slot_rows.shape[-1])
    gate_proj = jnp.dot(flat_rows, w_gate[0], preferred_element_type=jnp.float32)
    up_proj = jnp.dot(flat_rows, w_up[0], preferred_element_type=jnp.float32)
    hidden = (jax.nn.silu(gate_proj) * up_proj).astype(jnp.bfloat16)
    partial_out = jnp.dot(hidden, w_down[0], preferred_element_type=jnp.float32)
    return partial_out.reshape(slot_rows.shape)


def body(
    queries,
    own_latent,
    snapshots,
    leaf_snapshot,
    moe_input,
    expert_ids,
    gate_weights,
    w_gate,
    w_up,
    w_down,
):
    leaf_rows = queries.shape[0]
    width = moe_input.shape[1]
    experts = lax.axis_size("exp")
    capacity = min(leaf_rows, 2 * ((leaf_rows * TOP + experts - 1) // experts))
    expert_hits = (expert_ids[:, :, None] == jnp.arange(experts, dtype=jnp.int32)).astype(jnp.int32)
    per_row = jnp.sum(expert_hits, axis=1)
    earlier = jnp.cumsum(per_row, axis=0) - per_row
    slot_rank = jnp.take_along_axis(earlier, expert_ids, axis=1)
    flat_slot = expert_ids * capacity + slot_rank
    placing = jnp.sum(
        (flat_slot[:, :, None] == jnp.arange(experts * capacity, dtype=jnp.int32)).astype(
            jnp.bfloat16
        ),
        axis=1,
    )
    send_rows = jnp.einsum("rs,rd->sd", placing, moe_input, preferred_element_type=jnp.float32)
    send_rows = send_rows.astype(jnp.bfloat16).reshape(1, experts, capacity, width)
    chosen_snapshot = leaf_snapshot.astype(jnp.bfloat16)
    query_all, own_all, chosen_all = (
        lax.all_gather(queries, "seq", axis=0, tiled=True),
        lax.all_gather(own_latent, "seq", axis=0, tiled=True),
        lax.all_gather(chosen_snapshot, "seq", axis=0, tiled=True),
    )
    arrived = lax.all_to_all(send_rows[0], "exp", split_axis=0, concat_axis=0, tiled=True)
    slices = expert_partial(
        lax.all_gather(arrived[None], "seq", axis=0, tiled=True), w_gate, w_up, w_down
    )
    snapshot_index = chosen_all.astype(jnp.int32)
    snapshot_rows = jnp.take(snapshots, snapshot_index, axis=0)
    scores = qk_scale * jnp.einsum(
        "ghk,gpk->ghp", query_all, snapshot_rows, preferred_element_type=jnp.float32
    )
    own_score = qk_scale * jnp.einsum(
        "ghk,gk->gh", query_all, own_all, preferred_element_type=jnp.float32
    )
    row_max = lax.pmax(jnp.maximum(jnp.max(scores, axis=2), own_score), "seq")
    weights = jnp.exp(scores - row_max[:, :, None]).astype(jnp.bfloat16)
    mass_part = jnp.sum(weights.astype(jnp.float32), axis=2)
    value_part = jnp.einsum(
        "ghp,gpl->ghl", weights, snapshot_rows[:, :, :LAT], preferred_element_type=jnp.float32
    )
    slice_sum, mass_sum, value_sum = (
        lax.psum_scatter(
            slices.astype(jnp.bfloat16), "seq", scatter_dimension=0, tiled=True
        ).astype(jnp.float32),
        lax.psum_scatter(
            mass_part.astype(jnp.bfloat16), "seq", scatter_dimension=0, tiled=True
        ).astype(jnp.float32),
        lax.psum_scatter(
            value_part.astype(jnp.bfloat16), "seq", scatter_dimension=0, tiled=True
        ).astype(jnp.float32),
    )
    expert_out = lax.all_to_all(
        slice_sum.astype(jnp.bfloat16), "exp", split_axis=1, concat_axis=1, tiled=True
    )[0]
    expert_flat = expert_out.reshape(experts * capacity, width)
    picked = jnp.take(expert_flat, flat_slot, axis=0)
    moe_output = jnp.sum(gate_weights[:, :, None] * picked.astype(jnp.float32), axis=1).astype(
        jnp.bfloat16
    )
    start_row = lax.axis_index("seq") * leaf_rows
    home_max = lax.dynamic_slice_in_dim(row_max, start_row, leaf_rows, 0)
    home_score = lax.dynamic_slice_in_dim(own_score, start_row, leaf_rows, 0)
    own_weight = jnp.exp(home_score - home_max)
    numerator = value_sum + own_weight[:, :, None] * own_latent[:, None, :LAT].astype(jnp.float32)
    denominator = mass_sum + own_weight
    attn_latent = (numerator / denominator[:, :, None]).astype(jnp.bfloat16)
    return (attn_latent, moe_output)


def solution(mesh):
    in_specs = (
        P(("seq", "exp"), None, None),
        P(("seq", "exp"), None),
        P(None, "seq", None),
        P(("seq", "exp")),
        P(("seq", "exp"), None),
        P(("seq", "exp"), None),
        P(("seq", "exp"), None),
        P("exp", None, "seq"),
        P("exp", None, "seq"),
        P("exp", "seq", None),
    )
    out_specs = (P(("seq", "exp"), None, None), P(("seq", "exp"), None))
    return jax.shard_map(body, mesh=mesh, in_specs=in_specs, out_specs=out_specs, check_vma=False)
```

profile of v0, /device:TPU:0, one launch (start us, length us, event | category | flops | bytes accessed | tf_op | source)
XLA Modules:
  0.0 484.0 jit_solution(1091249641909766644)
XLA Ops:
  7.2 0.9 convert_reduce_fusion
  10.6 1.1 convolution_convert_fusion.1
  11.9 15.0 %all_to_all.10 = bf16[8,4,7168]{2,1,0:T(4,128)(2,1)} all-to-all(bf16[8,4,7168]{2,1,0:T(4,128)(2,1)S(1)} %squeeze_reshape.3), channel_id=1, replica_groups=mesh['seq'=16,'exp'=8] {'exp'}, dimensions={0} | all-to-all | bytes 917504 | tf_op jit(solution)/shard_map/all_to_all | solution.py:57
  27.7 64.8 %all-gather.7.cloned.1.call-done = bf16[128,4,7168]{2,1,0:T(4,128)(2,1)} async-done(((bf16[8,4,7168]{2,1,0:T(4,128)(2,1)}), bf16[128,4,7168]{2,1,0:T(4,128)(2,1)}) %all-gather.7.cloned.1.call-update) | async-done | bytes 7340048 | tf_op jit(solution)/shard_map/all_gather | solution.py:59
  92.5 12.1 %reshape.37 = bf16[512,7168]{1,0:T(8,128)(2,1)} reshape(bf16[128,4,7168]{2,1,0:T(4,128)(2,1)} %all-gather.7.cloned.1.call-done) | data formatting | bytes 14680064 | tf_op jit(solution)/shard_map/reshape | solution.py:14
  104.6 5.9 %fusion.10 = f32[512,128]{1,0:T(8,128)S(1)} fusion(bf16[512,7168]{1,0:T(8,128)(2,1)} %reshape.37, bf16[1,7168,128]{2,1,0:T(8,128)(2,1)} %param.17), kind=kOutput, calls=%fused_computation.16 | convolution fusion | flops 939524096 | bytes 9437184 | tf_op jit(solution)/shard_map/dot_general | solution.py:15
  111.0 2.1 fusion.15
  113.1 5.1 %convolution_convert_fusion = bf16[16,8,4,7168]{3,1,2,0:T(8,128)(2,1)} fusion(bf16[1,128,7168]{2,1,0:T(8,128)(2,1)S(1)} %copy-done, bf16[16,8,4,128]{3,2,1,0:T(4,128)(2,1)S(1)} %bitcast.51), kind=kOutput, calls=%fused_computation.6 | convolution fusion | flops 943194112 | bytes 9306112 | tf_op jit(solution)/shard_map/dot_general | solution.py:18
  119.8 39.2 %all-reduce = bf16[64]{0:T(256)(128)(2,1)S(1)} all-reduce(bf16[64]{0:T(256)(128)(2,1)S(1)} %dynamic-update-slice), channel_id=1, replica_groups=mesh['seq'=16,'exp'=8] {'seq'}, use_global_device_ids=true, to_apply=%add | all-reduce | flops 64 | bytes 256
  159.0 13.8 %gather_fusion = bf16[64,512,576]{1,2,0:T(8,128)(2,1)} fusion(bf16[2,512,576]{1,2,0:T(8,128)(2,1)S(1)} %copy-done.2, s32[1024]{0:T(1024)S(1)} %pad_clamp_fusion.1), kind=kCustom, calls=%fused_computation | custom fusion | bytes 75497728 | tf_op jit(solution)/shard_map/jit(_take)/gather | solution.py:62
  172.8 53.6 %copy.22 = bf16[64,512,576]{2,1,0:T(8,128)(2,1)} copy(bf16[64,512,576]{1,2,0:T(8,128)(2,1)} %gather_fusion) | data formatting | bytes 75497472 | tf_op jit(solution)/shard_map/jit(_take)/gather | solution.py:62
  226.4 20.6 %all-gather.1 = bf16[16,4,576]{2,1,0:T(4,128)(2,1)S(1)} all-gather(bf16[1,4,576]{2,1,0:T(4,128)(2,1)S(1)} %bitcast.53), channel_id=1, replica_groups=mesh['seq'=16,'exp'=8] {'seq'}, dimensions={0}, use_global_device_ids=true | all-gather | bytes 78336 | tf_op jit(solution)/shard_map/all_gather | solution.py:54
  247.1 28.3 %broadcast_select_fusion = bf16[64,512,576]{2,1,0:T(8,128)(2,1)} fusion(bf16[64,512,576]{2,1,0:T(8,128)(2,1)} %copy.22, pred[64]{0:T(512)(128)(4,1)S(1)} %compare_and_fusion.1), kind=kLoop, calls=%fused_computation.3 | loop fusion | flops 18874368 | bytes 75497536 | tf_op jit(solution)/shard_map/jit(_take)/select_n | solution.py:62
  275.4 4.2 fusion.26
  279.6 22.5 %bitcast_reduce_fusion = (f32[64,64]{1,0:T(8,128)S(1)}, f32[64,512,64]{1,2,0:T(8,128)}) fusion(bf16[64,512,576]{2,1,0:T(8,128)(2,1)} %broadcast_select_fusion, bf16[64,64,576]{2,1,0:T(8,128)(2,1)} %all-gather.5.cloned.1.call-done), kind=kOutput, calls=%fused_computation.8 | convolution fusion | flops 2420109312 | bytes 50872320 | tf_op jit(solution)/shard_map/ghk,gpk->ghp/dot_general | solution.py:63
  302.1 72.1 %pmax.7 = f32[64,64]{1,0:T(8,128)S(1)} all-reduce(f32[64,64]{1,0:T(8,128)S(1)} %get-tuple-element.7), channel_id=1, replica_groups=mesh['seq'=16,'exp'=8] {'seq'}, use_global_device_ids=true, to_apply=%region_1.0 | all-reduce | flops 4096 | bytes 32768 | tf_op jit(solution)/shard_map/pmax | solution.py:69
  374.2 17.6 %fusion.4 = bf16[64,64,512]{2,1,0:T(8,128)(2,1)} fusion(bf16[64,512,576]{2,1,0:T(8,128)(2,1)} %broadcast_select_fusion, f32[64,512,64]{1,2,0:T(8,128)} %get-tuple-element.11, f32[64,64]{1,0:T(8,128)S(1)} %pmax.7), kind=kOutput, calls=%fused_computation.12 | convolution fusion | flops 2155872256 | bytes 46153728 | tf_op jit(solution)/shard_map/ghp,gpl->ghl/dot_general | solution.py:72
  392.7 2.2 copy.25
  394.9 4.4 all-to-all-start.1
  399.3 4.5 fusion.18
  403.8 69.9 %all-reduce.1 = bf16[64,64]{1,0:T(8,128)(2,1)S(1)} all-reduce(bf16[64,64]{1,0:T(8,128)(2,1)S(1)} %fusion.18), channel_id=4, replica_groups=mesh['seq'=16,'exp'=8] {'seq'}, use_global_device_ids=true, to_apply=%region_4.5.clone | all-reduce | flops 4096 | bytes 16384
  473.7 1.8 divide_convert_fusion
  475.6 0.8 gather_fusion.1
  476.5 1.0 multiply_reduce_fusion
  (54 shorter events, 5.2 us)
Async XLA Ops:
  7.2 105.9 %copy-start = (bf16[1,128,7168]{2,1,0:T(8,128)(2,1)S(1)}, bf16[1,128,7168]{2,1,0:T(8,128)(2,1)}, u32[]{:S(2)}) copy-start(bf16[1,128,7168]{2,1,0:T(8,128)(2,1)} %param.19) | copy-start | bytes 5505028
  7.2 85.4 %all-gather.7.cloned.1.call-start = ((), (), s32[]{:S(2)}) async-start(), calls=%async_computation.6 | async-start | bytes 7798784 | tf_op jit(solution)/shard_map/all_gather | solution.py:59
  26.9 248.5 %all-gather.5.cloned.1.call-start = ((), (), s32[]{:S(2)}) async-start(), calls=%async_computation.4 | async-start | bytes 5570560 | tf_op jit(solution)/shard_map/all_gather | solution.py:53
  27.7 365.0 %reduce-scatter.7.cloned.1.call-start = ((), (), s32[]{:S(2)}) async-start(), calls=%async_computation.7 | async-start | bytes 7798784
  104.6 5.9 %copy-start.3 = (bf16[512,7168]{1,0:T(8,128)(2,1)S(1)}, bf16[512,7168]{1,0:T(8,128)(2,1)}, u32[]{:S(2)}) copy-start(bf16[512,7168]{1,0:T(8,128)(2,1)} %reshape.37) | copy-start | bytes 22020100
  104.6 6.3 %copy-start.7 = (bf16[1,7168,128]{2,1,0:T(8,128)(2,1)S(1)}, bf16[1,7168,128]{2,1,0:T(8,128)(2,1)}, u32[]{:S(2)}) copy-start(bf16[1,7168,128]{2,1,0:T(8,128)(2,1)} %param.18) | copy-start | bytes 5505028
  113.0 5.2 %copy-start.8 = (s32[4]{0:T(128)S(1)}, s32[4]{0:T(128)}, u32[]{:S(2)}) copy-start(s32[4]{0:T(128)} %param.13) | copy-start | bytes 52
  113.0 5.2 %copy-start.6 = (u32[128]{0:T(128)S(1)}, u32[128]{0:T(128)}, u32[]{:S(2)}) copy-start(u32[128]{0:T(128)} %constant.97) | copy-start | bytes 1540
  113.1 46.0 %copy-start.2 = (bf16[2,512,576]{1,2,0:T(8,128)(2,1)S(1)}, bf16[2,512,576]{1,2,0:T(8,128)(2,1)}, u32[]{:S(2)}) copy-start(bf16[2,512,576]{1,2,0:T(8,128)(2,1)} %param.12) | copy-start | bytes 3538948
  118.2 355.5 %reduce-scatter.5.cloned.1.call-start = ((), (), s32[]{:S(2)}) async-start(), calls=%async_computation.5 | async-start | bytes 4456448 | tf_op jit(solution)/shard_map/reduce_scatter | solution.py:82
  172.8 53.6 %copy-start.4 = (bf16[4,576]{1,0:T(4,128)(2,1)S(1)}, bf16[4,576]{1,0:T(4,128)(2,1)}, u32[]{:S(2)}) copy-start(bf16[4,576]{1,0:T(4,128)(2,1)} %param.11) | copy-start | bytes 13828
  391.8 84.7 %copy-start.5 = (f32[4,8]{1,0:T(4,128)S(1)}, f32[4,8]{1,0:T(4,128)}, u32[]{:S(2)}) copy-start(f32[4,8]{1,0:T(4,128)} %param.16) | copy-start | bytes 388
  391.8 85.7 %copy-start.1 = (bf16[1,128,7168]{2,1,0:T(8,128)(2,1)S(1)}, bf16[1,128,7168]{2,1,0:T(8,128)(2,1)}, u32[]{:S(2)}) copy-start(bf16[1,128,7168]{2,1,0:T(8,128)(2,1)} %param.19) | copy-start | bytes 5505028
  394.9 80.7 %all-to-all-start.1 = ((bf16[1,8,4,7168]{3,2,0,1:T(4,128)(2,1)}), bf16[1,8,4,7168]{3,2,0,1:T(4,128)(2,1)S(1)}, u32[]{:S(2)}, u32[]{:S(2)}) async-start(bf16[1,8,4,7168]{3,2,0,1:T(4,128)(2,1)} %copy.25), calls=%async_computation.2 | async-start | bytes 917504 | tf_op jit(solution)/shard_map/all_to_all | solution.py:86
Sparse Core Ops, SparseCore 0:
  27.0 65.4 all-gather.6
  94.7 56.4 all-gather.4
  154.7 82.6 reduce-scatter.6
  391.9 74.0 reduce-scatter.4
where the time goes:
time: 486 us; the launch traced here: 484 us
  blocking collectives  217 us (45%)
  local copies, waits for them, and re-layouts  85.1 us (18%)
  waiting for transfers between devices  65.6 us (13%)
  matrix products  58.4 us (12%)
  other arithmetic  38.1 us (8%)
  between operations  15.4 us (3%)
    unnamed x2, blocking collectives  109 us
    pmax x1, blocking collectives, body(): row_max = lax.pmax(jnp.maximum(jnp.max(scores, axis=2), own_score), 'seq')  72.1 us
    gather x2, local copies, waits for them, and re-layouts, body(): snapshot_rows = jnp.take(snapshots, snapshot_index, axis=0)  67.4 us
    all_gather x1, waiting for transfers between devices, body(): lax.all_gather(arrived[None], 'seq', axis=0, tiled=True)  64.8 us
    select_n x2, other arithmetic, body(): snapshot_rows = jnp.take(snapshots, snapshot_index, axis=0)  28.3 us
    dot_general x1, matrix products, body(): jnp.einsum('ghk,gpk->ghp', query_all, snapshot_rows, preferred_element_ty...  22.5 us
    all_gather x1, blocking collectives, body(): lax.all_gather(own_latent, 'seq', axis=0, tiled=True)  20.6 us
    dot_general x1, matrix products, body(): jnp.einsum('ghp,gpl->ghl', weights, snapshot_rows[:, :, :LAT], preferred_...  17.6 us
  transfers between devices with their start and end apart: 5, of which 1 were waited for; matrix products, arithmetic and copies ran while one was open for 36% of the time, Pallas kernels for 0%

commit v1 on v0

v1 whole, which is shorter than its diff:
```python
import math

import jax
import jax.numpy as jnp
from jax import lax
from jax.experimental import pallas as pl
from jax.experimental.pallas import tpu as pltpu
from jax.sharding import PartitionSpec as P

LAT = 512
KDIM = 576
QW = 640
D = 7168
XW = D + 128
C1 = 4608
C2 = XW - C1
E1 = 3584
E2 = D - E1
KC = 1536
SCALE2 = 192.0 ** (-0.5) * math.log2(math.e)
AXES = ("seq", "exp")
bf16 = jnp.bfloat16
f32 = jnp.float32


def shift(a, axis, s):
    pairs = []
    for y in range(4):
        for x in range(4):
            for z in range(4):
                for c in range(2):
                    to = dict(y=y, x=x, z=z, c=c)
                    to[axis] = (to[axis] + s) % (2 if axis == "c" else 4)
                    src = ((y * 4 + x) * 4 + z) * 2 + c
                    dst = ((to["y"] * 4 + to["x"]) * 4 + to["z"]) * 2 + to["c"]
                    pairs.append((src, dst))
    return lax.ppermute(a, AXES, pairs)


def spread(a, axis):
    return [a] + [shift(a, axis, s) for s in (1, 2, 3)]


def fold(chunks, axis):
    got = [shift(chunks[s], axis, -s) for s in (1, 2, 3)]
    return chunks[0].astype(f32) + got[0].astype(f32) + got[1].astype(f32) + got[2].astype(f32)


def attend_kernel(core_ref, *refs):
    qs, own, near, far = refs[0:4], refs[4], refs[5:8], refs[8:11]
    outs, s_ref = refs[11:15], refs[15]
    core = core_ref[0]
    coref = core.astype(f32)
    tiles_a = [own.at[core]] + list(near)
    tiles_b = [own.at[1 - core]] + list(far)
    tiles = tiles_a + tiles_b
    lane = lax.broadcasted_iota(jnp.int32, (256, QW - LAT), 1)
    for q_ref, o_ref in zip(qs, outs):
        q = q_ref[:, 0:KDIM]
        is_a = q_ref[:, KDIM : KDIM + 1].astype(f32) == coref
        best = []
        for group in range(2):
            m = None
            for t in range(4):
                i = group * 4 + t
                s = lax.dot_general(
                    q, tiles[i][...], (((1,), (1,)), ((), ())), preferred_element_type=f32
                )
                s_ref[i] = s
                ms = jnp.max(s, axis=1, keepdims=True)
                m = ms if m is None else jnp.maximum(m, ms)
            best.append(m)
        mu = jnp.where(is_a, best[0], best[1]) * SCALE2
        hi = mu.astype(bf16).astype(f32)
        lo = (mu - hi).astype(bf16).astype(f32)
        top = hi + lo
        total = jnp.zeros((256, 1), f32)
        acc = jnp.zeros((256, LAT), f32)
        for i in range(8):
            off = jnp.where(is_a if i < 4 else jnp.logical_not(is_a), -top, -1e30)
            w = jnp.exp2(s_ref[i] * SCALE2 + off).astype(bf16)
            total = total + jnp.sum(w.astype(f32), axis=1, keepdims=True)
            acc = acc + jnp.dot(w, tiles[i][:, 0:LAT], preferred_element_type=f32)
        o_ref[:, 0:LAT] = acc.astype(bf16)
        l_hi = total.astype(bf16).astype(f32)
        l_lo = total - l_hi
        tail = jnp.where(
            lane == 0,
            hi,
            jnp.where(lane == 1, lo, jnp.where(lane == 2, l_hi, jnp.where(lane == 3, l_lo, 0.0))),
        )
        o_ref[:, LAT:QW] = tail.astype(bf16)


def attend(core, qs, own, near, far):
    vmem = pl.BlockSpec(memory_space=pltpu.VMEM)
    return pl.pallas_call(
        attend_kernel,
        out_shape=[jax.ShapeDtypeStruct((256, QW), bf16)] * 4,
        in_specs=[pl.BlockSpec(memory_space=pltpu.SMEM)] + [vmem] * 11,
        out_specs=[vmem] * 4,
        scratch_shapes=[pltpu.VMEM((8, 256, 512), f32)],
        compiler_params=pltpu.CompilerParams(vmem_limit_bytes=40 << 20),
        name="attend",
    )(core, *qs, own, *near, *far)


def merge_kernel(q_ref, lat_ref, *refs):
    parts, out_ref = refs[0:4], refs[4]
    for leaf in range(4):
        r = slice(leaf * 64, leaf * 64 + 64)
        lat = lat_ref[leaf : leaf + 1, :].astype(f32)
        own = jnp.sum(q_ref[r, 0:KDIM].astype(f32) * lat, axis=1, keepdims=True) * SCALE2
        tails = [p[r, LAT:QW].astype(f32) for p in parts]
        tops = [t[:, 0:1] + t[:, 1:2] for t in tails]
        m = own
        for t in tops:
            m = jnp.maximum(m, t)
        w = jnp.exp2(own - m)
        num = w * lat[:, 0:LAT]
        den = w
        for p, t, top in zip(parts, tails, tops):
            w = jnp.exp2(top - m)
            num = num + w * p[r, 0:LAT].astype(f32)
            den = den + w * (t[:, 2:3] + t[:, 3:4])
        out_ref[r, :] = (num / den).astype(bf16)


def merge(q, lat, parts):
    vmem = pl.BlockSpec(memory_space=pltpu.VMEM)
    return pl.pallas_call(
        merge_kernel,
        out_shape=jax.ShapeDtypeStruct((256, LAT), bf16),
        in_specs=[vmem] * 6,
        out_specs=vmem,
        name="merge",
    )(q, lat, *parts)


def expert_kernel(e_ref, *refs):
    x1, x2 = refs[0:4], refs[4:8]
    wg, wu, wd, wg2, wu2, wd2 = refs[8:14]
    outs = refs[14:22]
    x_ref, w_ref, d_ref, acc_ref, sems = refs[22:27]
    bounds = [(k, min(k + KC, C1)) for k in range(0, C1, KC)] + [(C1, D)]
    count = [0]

    def copy(src, dst):
        cp = pltpu.make_async_copy(src, dst, sems.at[count[0]])
        count[0] += 1
        cp.start()
        return cp

    steps = []
    for k0, k1 in bounds:
        cps = []
        for j, w in enumerate((wg, wu, wg2, wu2)):
            cps.append(copy(w.at[k0:k1, :], w_ref.at[k0:k1, j * 128 : j * 128 + 128]))
        if k0 < C1:
            for z in range(4):
                cps.append(copy(x1[z].at[:, k0:k1], x_ref.at[z * 64 : z * 64 + 64, k0:k1]))
        else:
            for y in range(4):
                for z in range(4):
                    cps.append(
                        copy(
                            x2[y].at[z * 16 : z * 16 + 16, :],
                            x_ref.at[z * 64 + y * 16 : z * 64 + y * 16 + 16, C1:XW],
                        )
                    )
        steps.append(cps)
    down = [copy(wd, d_ref.at[0:128, :]), copy(wd2, d_ref.at[128:256, :])]
    for i, (k0, k1) in enumerate(bounds):
        for cp in steps[i]:
            cp.wait()
        part = jnp.dot(x_ref[:, k0:k1], w_ref[k0:k1, :], preferred_element_type=f32)
        if i == 0:
            acc_ref[...] = part
        else:
            acc_ref[...] += part
    gates = x_ref[:, D:XW].astype(f32)
    lane = lax.broadcasted_iota(jnp.int32, (256, 128), 1)
    halves = []
    for j in range(2):
        e = e_ref[j]
        pick = jnp.logical_or(lane == e, lane == e + 8)
        weight = jnp.sum(jnp.where(pick, gates, 0.0), axis=1, keepdims=True)
        g = acc_ref[:, j * 256 : j * 256 + 128]
        u = acc_ref[:, j * 256 + 128 : j * 256 + 256]
        halves.append((g / (1.0 + jnp.exp(-g)) * u * weight).astype(bf16))
    hidden = jnp.concatenate(halves, axis=1)
    row = lax.broadcasted_iota(jnp.int32, (256, 256), 0)
    col = lax.broadcasted_iota(jnp.int32, (256, 256), 1)
    i0 = row & 3
    b1 = (row >> 2) & 3
    b2 = (row >> 4) & 3
    b3 = (row >> 6) & 3
    want1 = b3 * 64 + b1 * 16 + b2 * 4 + i0
    want2 = b2 * 64 + b1 * 16 + b3 * 4 + i0
    for cp in down:
        cp.wait()
    for part, (want, base, width) in enumerate(((want1, 0, E1), (want2, E1, E2))):
        place = jnp.where(col == want, 1.0, 0.0).astype(bf16)
        h = jnp.dot(place, hidden, preferred_element_type=f32).astype(bf16)
        for n in range(0, width, 512):
            y = jnp.dot(h, d_ref[:, base + n : base + n + 512], preferred_element_type=f32).astype(
                bf16
            )
            for s in range(4):
                outs[part * 4 + s][:, n : n + 512] = y[s * 64 : s * 64 + 64, :]


def experts(e, x1, x2, weights):
    vmem = pl.BlockSpec(memory_space=pltpu.VMEM)
    hbm = pl.BlockSpec(memory_space=pl.ANY)
    return pl.pallas_call(
        expert_kernel,
        out_shape=[jax.ShapeDtypeStruct((64, E1), bf16)] * 4
        + [jax.ShapeDtypeStruct((64, E2), bf16)] * 4,
        in_specs=[pl.BlockSpec(memory_space=pltpu.SMEM)] + [hbm] * 14,
        out_specs=[vmem] * 8,
        scratch_shapes=[
            pltpu.VMEM((256, XW), bf16),
            pltpu.VMEM((D, 512), bf16),
            pltpu.VMEM((256, D), bf16),
            pltpu.VMEM((256, 512), f32),
            pltpu.SemaphoreType.DMA((64,)),
        ],
        compiler_params=pltpu.CompilerParams(vmem_limit_bytes=48 << 20),
        name="experts",
    )(e, *x1, *x2, *weights)


def body(
    queries,
    own_latent,
    snapshots,
    leaf_snapshot,
    moe_input,
    expert_ids,
    gate_weights,
    w_gate,
    w_up,
    w_down,
):
    place = lax.axis_index("exp").astype(jnp.int32)
    core = place & 1

    hit = (expert_ids[:, :, None] == jnp.arange(8, dtype=jnp.int32)).astype(f32)
    gate = jnp.sum(gate_weights[:, :, None] * hit, axis=1)
    high = lax.reduce_precision(gate, 8, 7)
    tail = jnp.concatenate([high, gate - high, jnp.zeros((4, 112), f32)], axis=1).astype(bf16)
    row = jnp.concatenate([moe_input, tail], axis=1)
    rows = jnp.concatenate(spread(row, "x"), axis=0)
    rows1 = jnp.concatenate(spread(rows[:, :C1], "y"), axis=0)
    rows2 = jnp.concatenate(spread(rows[:, C1:], "z"), axis=0)
    x1 = spread(rows1, "z")
    x2 = spread(rows2, "y")
    weights = [w_gate[0], w_up[0], w_down[0]]
    weights = weights + [shift(w, "c", 1) for w in weights]

    choice = jnp.broadcast_to(leaf_snapshot.astype(bf16)[:, None, None], (4, 64, QW - KDIM))
    query = jnp.concatenate([queries, choice], axis=2).reshape(256, QW)
    query_all = spread(query, "y")
    half = lax.dynamic_index_in_dim(snapshots, core, 0, keepdims=False)
    near = [shift(half, "x", s) for s in (1, 2, 3)]
    far = [shift(a, "c", 1) for a in near]

    parts = attend(core[None], query_all, snapshots, near, far)
    back = [parts[0]] + [shift(parts[s], "y", -s) for s in (1, 2, 3)]
    attn = merge(query, own_latent, back).reshape(4, 64, LAT)

    out = experts(jnp.stack([place, place ^ 1]), x1, x2, weights)
    a1 = fold(out[0:4], "z").astype(bf16)
    a2 = fold(out[4:8], "x").astype(bf16)
    b1 = fold([a1[s * 16 : s * 16 + 16] for s in range(4)], "x").astype(bf16)
    b2 = fold([a2[s * 16 : s * 16 + 16] for s in range(4)], "z").astype(bf16)
    b = jnp.concatenate([b1, b2], axis=1)
    moe = fold([b[s * 4 : s * 4 + 4] for s in range(4)], "y").astype(bf16)
    return attn, moe


def solution(mesh):
    in_specs = (
        P(AXES, None, None),
        P(AXES, None),
        P(None, "seq", None),
        P(AXES),
        P(AXES, None),
        P(AXES, None),
        P(AXES, None),
        P("exp", None, "seq"),
        P("exp", None, "seq"),
        P("exp", "seq", None),
    )
    out_specs = (P(AXES, None, None), P(AXES, None))
    return jax.shard_map(body, mesh=mesh, in_specs=in_specs, out_specs=out_specs, check_vma=False)
```

time: 486 us -> 213 us (0.44)
  blocking collectives: 217 us -> 0 us
  matrix products: 58.4 us -> 0 us
  local copies, waits for them, and re-layouts: 85.1 us -> 27.6 us
  starting transfers between devices: 4.6 us -> 58.4 us
  other arithmetic: 38.1 us -> 3.86 us
  waiting for transfers between devices: 65.6 us -> 94.6 us
  Pallas kernels: 0 us -> 26.4 us
  between operations: 15.4 us -> 0.93 us
    unnamed x2 -> x0, blocking collectives: 109 us -> none
    ppermute x0 -> x45, waiting for transfers between devices: none -> 94.6 us  [shift(): return lax.ppermute(a, AXES, pairs)]
    pmax x1 -> x0, blocking collectives: 72.1 us -> none  [body(): row_max = lax.pmax(jnp.maximum(jnp.max(scores, axis=2), own_score), 'seq')]
    gather x6 -> x0, local copies, waits for them, and re-layouts: 69.1 us -> none  [the longest x2 67.4 us: body(): snapshot_rows = jnp.take(snapshots, snapshot_index, axis=0)]
    all_gather x2 -> x0, waiting for transfers between devices: 64.8 us -> none  [the longest x1 64.8 us: body(): lax.all_gather(arrived[None], 'seq', axis=0, tiled=True)]
    dot_general x7 -> x0, matrix products: 58.4 us -> none  [the longest x1 22.5 us: body(): jnp.einsum('ghk,gpk->ghp', query_all, snapshot_rows, preferred_element_ty...]
    ppermute x0 -> x45, starting transfers between devices: none -> 58.4 us  [shift(): return lax.ppermute(a, AXES, pairs)]
    select_n x3 -> x0, other arithmetic: 28.3 us -> none  [the longest x2 28.3 us: body(): snapshot_rows = jnp.take(snapshots, snapshot_index, axis=0)]
  transfers between devices with their start and end apart: 5 -> 45, of which waited for: 1 -> 16; matrix products, arithmetic and copies ran while one was open for 36% -> 8% of each run, Pallas kernels for 0% -> 12%
where the time goes in v1:
time: 213 us; the launch traced here: 212 us
  waiting for transfers between devices  94.6 us (44%)
  starting transfers between devices  58.4 us (27%)
  local copies, waits for them, and re-layouts  27.6 us (13%)
  Pallas kernels  26.4 us (12%)
  other arithmetic  3.86 us (2%)
    ppermute x45, waiting for transfers between devices, shift(): return lax.ppermute(a, AXES, pairs)  94.6 us
    ppermute x45, starting transfers between devices, shift(): return lax.ppermute(a, AXES, pairs)  58.4 us
    pallas_call x1, Pallas kernels, attend(): pl.pallas_call(attend_kernel, out_shape=[jax.ShapeDtypeStruct((256, QW),...  14.8 us
    unnamed x55, local copies, waits for them, and re-layouts  14 us
    ppermute x6, local copies, waits for them, and re-layouts, shift(): return lax.ppermute(a, AXES, pairs)  11.3 us
    pallas_call x1, Pallas kernels, experts(): pl.pallas_call(expert_kernel, out_shape=[jax.ShapeDtypeStruct((64, E1), b...  8.58 us
  transfers between devices with their start and end apart: 45, of which 16 were waited for; matrix products, arithmetic and copies ran while one was open for 8% of the time, Pallas kernels for 12%

profile of v1, /device:TPU:0, one launch (start us, length us, event | category | flops | bytes accessed | tf_op | source)
XLA Modules:
  0.0 211.7 jit_solution(14197547539429635848)
XLA Ops:
  4.0 2.7 %collective-permute-start.13 = (bf16[4,7296]{1,0:T(4,128)(2,1)S(1)}, bf16[4,7296]{1,0:T(4,128)(2,1)S(1)}, u32[]{:S(2)}, u32[]{:S(2)}) collective-permute-start(bf16[4,7296]{1,0:T(4,128)(2,1)S(1)} %concatenate.22), channel_id=1, source_target_pairs={{0,16},{1,17},{2,18},{3,19},{4,20},{5,21},{6,22},{7,23},{8,24},{9,... | collective-permute-start | bytes 175112 | tf_op jit(solution)/shard_map/ppermute | solution.py:37
  12.9 3.6 %collective-permute-start.22 = (bf16[16,2688]{1,0:T(8,128)(2,1)S(1)}, bf16[16,2688]{1,0:T(8,128)(2,1)S(1)}, u32[]{:S(2)}, u32[]{:S(2)}) collective-permute-start(bf16[16,2688]{1,0:T(8,128)(2,1)S(1)} %pad_maximum_fusion.4), channel_id=1, source_target_pairs={{0,4},{1,5},{2,6},{3,7},{4,0},{5,1},{6,2},{7,3},{8,12},{9,13},{10,... | collective-permute-start | bytes 258056 | tf_op jit(solution)/shard_map/ppermute | solution.py:37
  19.4 2.9 %collective-permute-start.16 = (bf16[16,4608]{1,0:T(8,128)(2,1)S(1)}, bf16[16,4608]{1,0:T(8,128)(2,1)S(1)}, u32[]{:S(2)}, u32[]{:S(2)}) collective-permute-start(bf16[16,4608]{1,0:T(8,128)(2,1)S(1)} %slice.56), channel_id=1, source_target_pairs={{0,64},{1,65},{2,66},{3,67},{4,68},{5,69},{6,70},{7,71},{8,72},{9,... | collective-permute-start | bytes 442376 | tf_op jit(solution)/shard_map/ppermute | solution.py:37
  22.7 2.9 %collective-permute-start.25 = (bf16[64,2688]{1,0:T(8,128)(2,1)S(1)}, bf16[64,2688]{1,0:T(8,128)(2,1)S(1)}, u32[]{:S(2)}, u32[]{:S(2)}) collective-permute-start(bf16[64,2688]{1,0:T(8,128)(2,1)S(1)} %pad_maximum_fusion.1.refs_4_), channel_id=1, source_target_pairs={{0,64},{1,65},{2,66},{3,67},{4,68},{5,69},{6,70},{7,71},{8,72},{9,... | collective-permute-start | bytes 1032200 | tf_op jit(solution)/shard_map/ppermute | solution.py:37
  27.3 2.6 %collective-permute-done.16 = bf16[16,4608]{1,0:T(8,128)(2,1)S(1)} collective-permute-done((bf16[16,4608]{1,0:T(8,128)(2,1)S(1)}, bf16[16,4608]{1,0:T(8,128)(2,1)S(1)}, u32[]{:S(2)}, u32[]{:S(2)}) %collective-permute-start.16) | collective-permute-done | bytes 147488 | tf_op jit(solution)/shard_map/ppermute | solution.py:37
  30.1 13.3 %collective-permute-done.17 = bf16[16,4608]{1,0:T(8,128)(2,1)S(1)} collective-permute-done((bf16[16,4608]{1,0:T(8,128)(2,1)S(1)}, bf16[16,4608]{1,0:T(8,128)(2,1)S(1)}, u32[]{:S(2)}, u32[]{:S(2)}) %collective-permute-start.17) | collective-permute-done | bytes 147488 | tf_op jit(solution)/shard_map/ppermute | solution.py:37
  46.8 14.0 %collective-permute-done.4 = bf16[512,576]{0,1:T(8,128)(2,1)} collective-permute-done((bf16[512,576]{0,1:T(8,128)(2,1)S(1)}, bf16[512,576]{0,1:T(8,128)(2,1)}, u32[]{:S(2)}, u32[]{:S(2)}) %collective-permute-start.4) | collective-permute-done | bytes 589856 | tf_op jit(solution)/shard_map/ppermute | solution.py:37
  61.3 11.8 %collective-permute-done.5 = bf16[512,576]{0,1:T(8,128)(2,1)} collective-permute-done((bf16[512,576]{0,1:T(8,128)(2,1)S(1)}, bf16[512,576]{0,1:T(8,128)(2,1)}, u32[]{:S(2)}, u32[]{:S(2)}) %collective-permute-start.5) | collective-permute-done | bytes 589856 | tf_op jit(solution)/shard_map/ppermute | solution.py:37
  74.1 2.8 %collective-permute-done.18.refs_1_ = bf16[64,4608]{1,0:T(8,128)(2,1)S(1)} collective-permute-done((bf16[64,4608]{1,0:T(8,128)(2,1)S(1)}, bf16[64,4608]{1,0:T(8,128)(2,1)S(1)}, u32[]{:S(2)}, u32[]{:S(2)}) %collective-permute-start.18) | collective-permute-done | bytes 589856 | tf_op jit(solution)/shard_map/ppermute | solution.py:37
  76.8 12.7 %collective-permute-done.19.refs_2_ = bf16[64,4608]{1,0:T(8,128)(2,1)S(1)} collective-permute-done((bf16[64,4608]{1,0:T(8,128)(2,1)S(1)}, bf16[64,4608]{1,0:T(8,128)(2,1)S(1)}, u32[]{:S(2)}, u32[]{:S(2)}) %collective-permute-start.19) | collective-permute-done | bytes 589856 | tf_op jit(solution)/shard_map/ppermute | solution.py:37
  89.5 10.9 %collective-permute-done.20.refs_3_ = bf16[64,4608]{1,0:T(8,128)(2,1)S(1)} collective-permute-done((bf16[64,4608]{1,0:T(8,128)(2,1)S(1)}, bf16[64,4608]{1,0:T(8,128)(2,1)S(1)}, u32[]{:S(2)}, u32[]{:S(2)}) %collective-permute-start.20) | collective-permute-done | bytes 589856 | tf_op jit(solution)/shard_map/ppermute | solution.py:37
  105.5 8.6 %experts.1 = (bf16[64,3584]{1,0:T(8,128)(2,1)S(1)}, bf16[64,3584]{1,0:T(8,128)(2,1)S(1)}, bf16[64,3584]{1,0:T(8,128)(2,1)S(1)}, bf16[64,3584]{1,0:T(8,128)(2,1)S...) custom-call(s32[2]{0:T(128)S(1)} %pad_add_fusion.e_ref, ...), custom_call_target="tpu_custom_call" | custom-call | tf_op jit(solution)/shard_map/experts/pallas_call | solution.py:216
  117.2 2.7 %collective-permute-start.36 = (bf16[64,3584]{1,0:T(8,128)(2,1)}, bf16[64,3584]{1,0:T(8,128)(2,1)}, u32[]{:S(2)}, u32[]{:S(2)}) collective-permute-start(bf16[64,3584]{1,0:T(8,128)(2,1)} %get-tuple-element.23), channel_id=1, source_target_pairs={{0,24},{1,25},{2,26},{3,27},{4,28},{5,29},{6,30},{7,31},{8,0},{9,1... | collective-permute-start | bytes 1376264 | tf_op jit(solution)/shard_map/ppermute | solution.py:37
  120.9 2.3 %collective-permute-start.1 = (bf16[256,640]{1,0:T(8,128)(2,1)S(1)}, bf16[256,640]{1,0:T(8,128)(2,1)}, u32[]{:S(2)}, u32[]{:S(2)}) collective-permute-start(bf16[256,640]{1,0:T(8,128)(2,1)S(1)} %bitcast.11), channel_id=1, source_target_pairs={{0,64},{1,65},{2,66},{3,67},{4,68},{5,69},{6,70},{7,71},{8,72},{9,... | collective-permute-start | bytes 983048 | tf_op jit(solution)/shard_map/ppermute | solution.py:37
  128.8 2.2 %copy.24.refs_7_ = bf16[512,576]{1,0:T(8,128)(2,1)} copy(bf16[512,576]{0,1:T(8,128)(2,1)} %collective-permute-done.5) | data formatting | bytes 1179648 | tf_op jit(solution)/shard_map/ppermute | solution.py:37
  135.3 2.2 %copy.27.refs_10_ = bf16[512,576]{1,0:T(8,128)(2,1)} copy(bf16[512,576]{0,1:T(8,128)(2,1)} %collective-permute-done.8) | data formatting | bytes 1179648 | tf_op jit(solution)/shard_map/ppermute | solution.py:37
  142.8 14.8 %attend.1 = (bf16[256,640]{1,0:T(8,128)(2,1)S(1)}, bf16[256,640]{1,0:T(8,128)(2,1)S(1)}, bf16[256,640]{1,0:T(8,128)(2,1)S(1)}, bf16[256,640]{1,0:T(8,128)(2,1)S(1)}) custom-call(s32[1]{0:T(128)} %bitcast.1.core_ref, bf16[256,640]{1,0:T(8,128)(2,1)S(1)} %bitcast.13, bf16[256,640]{1,0:T(8,128)(2,1)S(1)} %copy-done.9, ...), custom_call_target="tpu_custom_call" | custom-call | tf_op jit(solution)/shard_map/attend/pallas_call | solution.py:97
  160.5 2.9 %collective-permute-start.30 = (bf16[64,3584]{1,0:T(8,128)(2,1)S(1)}, bf16[64,3584]{1,0:T(8,128)(2,1)S(1)}, u32[]{:S(2)}, u32[]{:S(2)}) collective-permute-start(bf16[64,3584]{1,0:T(8,128)(2,1)S(1)} %copy-done.15), channel_id=1, source_target_pairs={{0,6},{1,7},{2,0},{3,1},{4,2},{5,3},{6,4},{7,5},{8,14},{9,15},{10,... | collective-permute-start | bytes 1376264 | tf_op jit(solution)/shard_map/ppermute | solution.py:37
  167.1 16.4 %collective-permute-done.30 = bf16[64,3584]{1,0:T(8,128)(2,1)S(1)} collective-permute-done((bf16[64,3584]{1,0:T(8,128)(2,1)S(1)}, bf16[64,3584]{1,0:T(8,128)(2,1)S(1)}, u32[]{:S(2)}, u32[]{:S(2)}) %collective-permute-start.30) | collective-permute-done | bytes 458784 | tf_op jit(solution)/shard_map/ppermute | solution.py:37
  183.5 3.8 %collective-permute-start.39 = (bf16[16,3584]{1,0:T(8,128)(2,1)S(1)}, bf16[16,3584]{1,0:T(8,128)(2,1)S(1)}, u32[]{:S(2)}, u32[]{:S(2)}) collective-permute-start(bf16[16,3584]{1,0:T(8,128)(2,1)S(1)} %get-tuple-element.29), channel_id=1, source_target_pairs={{0,6},{1,7},{2,0},{3,1},{4,2},{5,3},{6,4},{7,5},{8,14},{9,15},{10,... | collective-permute-start | bytes 344072 | tf_op jit(solution)/shard_map/ppermute | solution.py:37
  188.5 2.4 %collective-permute-done.39 = bf16[16,3584]{1,0:T(8,128)(2,1)S(1)} collective-permute-done((bf16[16,3584]{1,0:T(8,128)(2,1)S(1)}, bf16[16,3584]{1,0:T(8,128)(2,1)S(1)}, u32[]{:S(2)}, u32[]{:S(2)}) %collective-permute-start.39) | collective-permute-done | bytes 114720 | tf_op jit(solution)/shard_map/ppermute | solution.py:37
  190.9 2.4 %collective-permute-start.33 = (bf16[16,3584]{1,0:T(8,128)(2,1)S(1)}, bf16[16,3584]{1,0:T(8,128)(2,1)S(1)}, u32[]{:S(2)}, u32[]{:S(2)}) collective-permute-start(bf16[16,3584]{1,0:T(8,128)(2,1)S(1)} %get-tuple-element.26), channel_id=1, source_target_pairs={{0,24},{1,25},{2,26},{3,27},{4,28},{5,29},{6,30},{7,31},{8,0},{9,1... | collective-permute-start | bytes 344072 | tf_op jit(solution)/shard_map/ppermute | solution.py:37
  193.7 2.5 %collective-permute-start.34 = (bf16[16,3584]{1,0:T(8,128)(2,1)S(1)}, bf16[16,3584]{1,0:T(8,128)(2,1)S(1)}, u32[]{:S(2)}, u32[]{:S(2)}) collective-permute-start(bf16[16,3584]{1,0:T(8,128)(2,1)S(1)} %get-tuple-element.28), channel_id=1, source_target_pairs={{0,16},{1,17},{2,18},{3,19},{4,20},{5,21},{6,22},{7,23},{8,24},{9,... | collective-permute-start | bytes 344072 | tf_op jit(solution)/shard_map/ppermute | solution.py:37
  208.0 3.0 %merge.1 = bf16[256,512]{1,0:T(8,128)(2,1)} custom-call(bf16[256,640]{1,0:T(8,128)(2,1)} %bitcast.14, bf16[4,576]{1,0:T(4,128)(2,1)} %lat_ref.1, bf16[256,640]{1,0:T(8,128)(2,1)} %copy-done.7, bf16[256,640]{1,0:T(8,128)(2,1)} %copy-done.24, bf16[256,640]{1,0:T(8,128)(2,1)} %copy-done.22, bf16[256,640]{1,0:T(8,128)(2,1)} %copy-done.23), custom_call_target="tpu_custom_call" | custom-call | tf_op jit(solution)/shard_map/merge/pallas_call | solution.py:131
  (152 shorter events, 64.5 us)
Async XLA Ops:
  9.4 36.9 %collective-permute-start.3 = (bf16[512,576]{0,1:T(8,128)(2,1)S(1)}, bf16[512,576]{0,1:T(8,128)(2,1)}, u32[]{:S(2)}, u32[]{:S(2)}) collective-permute-start(bf16[512,576]{0,1:T(8,128)(2,1)S(1)} %dynamic-slice_bitcast_fusion), channel_id=1, source_target_pairs={{0,8},{1,9},{2,10},{3,11},{4,12},{5,13},{6,14},{7,15},{8,16},{9,17... | collective-permute-start | bytes 1769480 | tf_op jit(solution)/shard_map/ppermute | solution.py:37
  22.3 21.1 %collective-permute-start.24 = (bf16[64,2688]{1,0:T(8,128)(2,1)S(1)}, bf16[64,2688]{1,0:T(8,128)(2,1)S(1)}, u32[]{:S(2)}, u32[]{:S(2)}) collective-permute-start(bf16[64,2688]{1,0:T(8,128)(2,1)S(1)} %pad_maximum_fusion.1.refs_4_), channel_id=1, source_target_pairs={{0,32},{1,33},{2,34},{3,35},{4,36},{5,37},{6,38},{7,39},{8,40},{9,... | collective-permute-start | bytes 1032200 | tf_op jit(solution)/shard_map/ppermute | solution.py:37
  22.7 22.1 %collective-permute-start.25 = (bf16[64,2688]{1,0:T(8,128)(2,1)S(1)}, bf16[64,2688]{1,0:T(8,128)(2,1)S(1)}, u32[]{:S(2)}, u32[]{:S(2)}) collective-permute-start(bf16[64,2688]{1,0:T(8,128)(2,1)S(1)} %pad_maximum_fusion.1.refs_4_), channel_id=1, source_target_pairs={{0,64},{1,65},{2,66},{3,67},{4,68},{5,69},{6,70},{7,71},{8,72},{9,... | collective-permute-start | bytes 1032200 | tf_op jit(solution)/shard_map/ppermute | solution.py:37
  26.9 19.3 %collective-permute-start.26 = (bf16[64,2688]{1,0:T(8,128)(2,1)S(1)}, bf16[64,2688]{1,0:T(8,128)(2,1)S(1)}, u32[]{:S(2)}, u32[]{:S(2)}) collective-permute-start(bf16[64,2688]{1,0:T(8,128)(2,1)S(1)} %pad_maximum_fusion.1.refs_4_), channel_id=1, source_target_pairs={{0,96},{1,97},{2,98},{3,99},{4,100},{5,101},{6,102},{7,103},{8,104... | collective-permute-start | bytes 1032200 | tf_op jit(solution)/shard_map/ppermute | solution.py:37
  43.4 57.1 %collective-permute-start.27 = (bf16[7168,128]{1,0:T(8,128)(2,1)S(1)}, bf16[7168,128]{1,0:T(8,128)(2,1)S(1)}, u32[]{:S(2)}, u32[]{:S(2)}) collective-permute-start(bf16[7168,128]{1,0:T(8,128)(2,1)S(1)} %bitcast.16), channel_id=1, source_target_pairs={{0,1},{1,0},{2,3},{3,2},{4,5},{5,4},{6,7},{7,6},{8,9},{9,8},{10,11... | collective-permute-start | bytes 5505032 | tf_op jit(solution)/shard_map/ppermute | solution.py:37
  43.4 17.4 %collective-permute-start.4 = (bf16[512,576]{0,1:T(8,128)(2,1)S(1)}, bf16[512,576]{0,1:T(8,128)(2,1)}, u32[]{:S(2)}, u32[]{:S(2)}) collective-permute-start(bf16[512,576]{0,1:T(8,128)(2,1)S(1)} %dynamic-slice_bitcast_fusion), channel_id=1, source_target_pairs={{0,16},{1,17},{2,18},{3,19},{4,20},{5,21},{6,22},{7,23},{8,24},{9,... | collective-permute-start | bytes 1769480 | tf_op jit(solution)/shard_map/ppermute | solution.py:37
  44.8 28.3 %collective-permute-start.5 = (bf16[512,576]{0,1:T(8,128)(2,1)S(1)}, bf16[512,576]{0,1:T(8,128)(2,1)}, u32[]{:S(2)}, u32[]{:S(2)}) collective-permute-start(bf16[512,576]{0,1:T(8,128)(2,1)S(1)} %dynamic-slice_bitcast_fusion), channel_id=1, source_target_pairs={{0,24},{1,25},{2,26},{3,27},{4,28},{5,29},{6,30},{7,31},{8,0},{9,1... | collective-permute-start | bytes 1769480 | tf_op jit(solution)/shard_map/ppermute | solution.py:37
  46.2 55.3 %collective-permute-start.28 = (bf16[7168,128]{1,0:T(8,128)(2,1)}, bf16[7168,128]{1,0:T(8,128)(2,1)S(1)}, u32[]{:S(2)}, u32[]{:S(2)}) collective-permute-start(bf16[7168,128]{1,0:T(8,128)(2,1)} %bitcast.17), channel_id=1, source_target_pairs={{0,1},{1,0},{2,3},{3,2},{4,5},{5,4},{6,7},{7,6},{8,9},{9,8},{10,11... | collective-permute-start | bytes 5505032 | tf_op jit(solution)/shard_map/ppermute | solution.py:37
  46.2 59.3 %collective-permute-start.29 = (bf16[128,7168]{1,0:T(8,128)(2,1)}, bf16[128,7168]{1,0:T(8,128)(2,1)}, u32[]{:S(2)}, u32[]{:S(2)}) collective-permute-start(bf16[128,7168]{1,0:T(8,128)(2,1)} %bitcast.19), channel_id=1, source_target_pairs={{0,1},{1,0},{2,3},{3,2},{4,5},{5,4},{6,7},{7,6},{8,9},{9,8},{10,11... | collective-permute-start | bytes 5505032 | tf_op jit(solution)/shard_map/ppermute | solution.py:37
  73.1 16.4 %collective-permute-start.19 = (bf16[64,4608]{1,0:T(8,128)(2,1)S(1)}, bf16[64,4608]{1,0:T(8,128)(2,1)S(1)}, u32[]{:S(2)}, u32[]{:S(2)}) collective-permute-start(bf16[64,4608]{1,0:T(8,128)(2,1)S(1)} %pad_maximum_fusion.refs_0_), channel_id=1, source_target_pairs={{0,4},{1,5},{2,6},{3,7},{4,0},{5,1},{6,2},{7,3},{8,12},{9,13},{10,... | collective-permute-start | bytes 1769480 | tf_op jit(solution)/shard_map/ppermute | solution.py:37
  76.8 23.6 %collective-permute-start.20 = (bf16[64,4608]{1,0:T(8,128)(2,1)S(1)}, bf16[64,4608]{1,0:T(8,128)(2,1)S(1)}, u32[]{:S(2)}, u32[]{:S(2)}) collective-permute-start(bf16[64,4608]{1,0:T(8,128)(2,1)S(1)} %pad_maximum_fusion.refs_0_), channel_id=1, source_target_pairs={{0,6},{1,7},{2,0},{3,1},{4,2},{5,3},{6,4},{7,5},{8,14},{9,15},{10,... | collective-permute-start | bytes 1769480 | tf_op jit(solution)/shard_map/ppermute | solution.py:37
  89.5 30.5 %collective-permute-start.6 = (bf16[512,576]{0,1:T(8,128)(2,1)}, bf16[512,576]{0,1:T(8,128)(2,1)}, u32[]{:S(2)}, u32[]{:S(2)}) collective-permute-start(bf16[512,576]{0,1:T(8,128)(2,1)} %collective-permute-done.3), channel_id=1, source_target_pairs={{0,1},{1,0},{2,3},{3,2},{4,5},{5,4},{6,7},{7,6},{8,9},{9,8},{10,11... | collective-permute-start | bytes 1769480 | tf_op jit(solution)/shard_map/ppermute | solution.py:37
  100.5 20.4 %collective-permute-start.7 = (bf16[512,576]{0,1:T(8,128)(2,1)}, bf16[512,576]{0,1:T(8,128)(2,1)}, u32[]{:S(2)}, u32[]{:S(2)}) collective-permute-start(bf16[512,576]{0,1:T(8,128)(2,1)} %collective-permute-done.4), channel_id=1, source_target_pairs={{0,1},{1,0},{2,3},{3,2},{4,5},{5,4},{6,7},{7,6},{8,9},{9,8},{10,11... | collective-permute-start | bytes 1769480 | tf_op jit(solution)/shard_map/ppermute | solution.py:37
  101.3 21.9 %collective-permute-start.8 = (bf16[512,576]{0,1:T(8,128)(2,1)}, bf16[512,576]{0,1:T(8,128)(2,1)}, u32[]{:S(2)}, u32[]{:S(2)}) collective-permute-start(bf16[512,576]{0,1:T(8,128)(2,1)} %collective-permute-done.5), channel_id=1, source_target_pairs={{0,1},{1,0},{2,3},{3,2},{4,5},{5,4},{6,7},{7,6},{8,9},{9,8},{10,11... | collective-permute-start | bytes 1769480 | tf_op jit(solution)/shard_map/ppermute | solution.py:37
  103.8 16.1 %collective-permute-start = (bf16[256,640]{1,0:T(8,128)(2,1)S(1)}, bf16[256,640]{1,0:T(8,128)(2,1)S(1)}, u32[]{:S(2)}, u32[]{:S(2)}) collective-permute-start(bf16[256,640]{1,0:T(8,128)(2,1)S(1)} %bitcast.10), channel_id=1, source_target_pairs={{0,32},{1,33},{2,34},{3,35},{4,36},{5,37},{6,38},{7,39},{8,40},{9,... | collective-permute-start | bytes 983048 | tf_op jit(solution)/shard_map/ppermute | solution.py:37
  117.2 43.3 %collective-permute-start.36 = (bf16[64,3584]{1,0:T(8,128)(2,1)}, bf16[64,3584]{1,0:T(8,128)(2,1)}, u32[]{:S(2)}, u32[]{:S(2)}) collective-permute-start(bf16[64,3584]{1,0:T(8,128)(2,1)} %get-tuple-element.23), channel_id=1, source_target_pairs={{0,24},{1,25},{2,26},{3,27},{4,28},{5,29},{6,30},{7,31},{8,0},{9,1... | collective-permute-start | bytes 1376264 | tf_op jit(solution)/shard_map/ppermute | solution.py:37
  119.9 43.5 %collective-permute-start.37 = (bf16[64,3584]{1,0:T(8,128)(2,1)}, bf16[64,3584]{1,0:T(8,128)(2,1)}, u32[]{:S(2)}, u32[]{:S(2)}) collective-permute-start(bf16[64,3584]{1,0:T(8,128)(2,1)} %get-tuple-element.24), channel_id=1, source_target_pairs={{0,16},{1,17},{2,18},{3,19},{4,20},{5,21},{6,22},{7,23},{8,24},{9,... | collective-permute-start | bytes 1376264 | tf_op jit(solution)/shard_map/ppermute | solution.py:37
  120.1 44.6 %collective-permute-start.38 = (bf16[64,3584]{1,0:T(8,128)(2,1)}, bf16[64,3584]{1,0:T(8,128)(2,1)}, u32[]{:S(2)}, u32[]{:S(2)}) collective-permute-start(bf16[64,3584]{1,0:T(8,128)(2,1)} %get-tuple-element.25), channel_id=1, source_target_pairs={{0,8},{1,9},{2,10},{3,11},{4,12},{5,13},{6,14},{7,15},{8,16},{9,17... | collective-permute-start | bytes 1376264 | tf_op jit(solution)/shard_map/ppermute | solution.py:37
  120.9 16.6 %collective-permute-start.1 = (bf16[256,640]{1,0:T(8,128)(2,1)S(1)}, bf16[256,640]{1,0:T(8,128)(2,1)}, u32[]{:S(2)}, u32[]{:S(2)}) collective-permute-start(bf16[256,640]{1,0:T(8,128)(2,1)S(1)} %bitcast.11), channel_id=1, source_target_pairs={{0,64},{1,65},{2,66},{3,67},{4,68},{5,69},{6,70},{7,71},{8,72},{9,... | collective-permute-start | bytes 983048 | tf_op jit(solution)/shard_map/ppermute | solution.py:37
  157.5 47.5 %collective-permute-start.10 = (bf16[256,640]{1,0:T(8,128)(2,1)S(1)}, bf16[256,640]{1,0:T(8,128)(2,1)S(1)}, u32[]{:S(2)}, u32[]{:S(2)}) collective-permute-start(bf16[256,640]{1,0:T(8,128)(2,1)S(1)} %get-tuple-element.16), channel_id=1, source_target_pairs={{0,64},{1,65},{2,66},{3,67},{4,68},{5,69},{6,70},{7,71},{8,72},{9,... | collective-permute-start | bytes 983048 | tf_op jit(solution)/shard_map/ppermute | solution.py:37
  159.7 45.9 %collective-permute-start.11 = (bf16[256,640]{1,0:T(8,128)(2,1)S(1)}, bf16[256,640]{1,0:T(8,128)(2,1)S(1)}, u32[]{:S(2)}, u32[]{:S(2)}) collective-permute-start(bf16[256,640]{1,0:T(8,128)(2,1)S(1)} %get-tuple-element.17), channel_id=1, source_target_pairs={{0,32},{1,33},{2,34},{3,35},{4,36},{5,37},{6,38},{7,39},{8,40},{9,... | collective-permute-start | bytes 983048 | tf_op jit(solution)/shard_map/ppermute | solution.py:37
  160.5 23.0 %collective-permute-start.30 = (bf16[64,3584]{1,0:T(8,128)(2,1)S(1)}, bf16[64,3584]{1,0:T(8,128)(2,1)S(1)}, u32[]{:S(2)}, u32[]{:S(2)}) collective-permute-start(bf16[64,3584]{1,0:T(8,128)(2,1)S(1)} %copy-done.15), channel_id=1, source_target_pairs={{0,6},{1,7},{2,0},{3,1},{4,2},{5,3},{6,4},{7,5},{8,14},{9,15},{10,... | collective-permute-start | bytes 1376264 | tf_op jit(solution)/shard_map/ppermute | solution.py:37
  163.4 23.9 %collective-permute-start.31 = (bf16[64,3584]{1,0:T(8,128)(2,1)S(1)}, bf16[64,3584]{1,0:T(8,128)(2,1)S(1)}, u32[]{:S(2)}, u32[]{:S(2)}) collective-permute-start(bf16[64,3584]{1,0:T(8,128)(2,1)S(1)} %copy-done.13), channel_id=1, source_target_pairs={{0,4},{1,5},{2,6},{3,7},{4,0},{5,1},{6,2},{7,3},{8,12},{9,13},{10,... | collective-permute-start | bytes 1376264 | tf_op jit(solution)/shard_map/ppermute | solution.py:37
  164.6 23.0 %collective-permute-start.32 = (bf16[64,3584]{1,0:T(8,128)(2,1)S(1)}, bf16[64,3584]{1,0:T(8,128)(2,1)S(1)}, u32[]{:S(2)}, u32[]{:S(2)}) collective-permute-start(bf16[64,3584]{1,0:T(8,128)(2,1)S(1)} %copy-done.11), channel_id=1, source_target_pairs={{0,2},{1,3},{2,4},{3,5},{4,6},{5,7},{6,0},{7,1},{8,10},{9,11},{10,... | collective-permute-start | bytes 1376264 | tf_op jit(solution)/shard_map/ppermute | solution.py:37
  (48 other events, 567.4 us)

commit v2 on v1

v2 whole, which is shorter than its diff:
```python
import math

import jax
import jax.numpy as jnp
from jax import lax
from jax.experimental import pallas as pl
from jax.experimental.pallas import tpu as pltpu
from jax.sharding import PartitionSpec as P

LAT = 512
KDIM = 576
QW = 640
D = 7168
XW = D + 128
KC = 2560
SCALE2 = 192.0 ** (-0.5) * math.log2(math.e)
AXES = ("seq", "exp")
GROUPS_X = [[4 * y + x for x in range(4)] for y in range(4)]
bf16 = jnp.bfloat16
f32 = jnp.float32


def shift(a, axis, s):
    pairs = []
    for y in range(4):
        for x in range(4):
            for z in range(4):
                for c in range(2):
                    to = dict(y=y, x=x, z=z, c=c)
                    to[axis] = (to[axis] + s) % (2 if axis == "c" else 4)
                    src = ((y * 4 + x) * 4 + z) * 2 + c
                    dst = ((to["y"] * 4 + to["x"]) * 4 + to["z"]) * 2 + to["c"]
                    pairs.append((src, dst))
    return lax.ppermute(a, AXES, pairs)


def gather(a, axis, groups):
    wide = jnp.broadcast_to(a, (len(groups[0]),) + a.shape[1:])
    return lax.all_to_all(wide, axis, 0, 0, tiled=True, axis_index_groups=groups)


def after(*arrays):
    return lax.optimization_barrier(arrays)


def add(*parts):
    out = parts[0].astype(f32)
    for p in parts[1:]:
        out = out + p.astype(f32)
    return out.astype(bf16)


def in_hbm(*arrays):
    return [pltpu.with_memory_space_constraint(a, pltpu.HBM) for a in arrays]


def attend_kernel(core_ref, *refs):
    qs, near, far, outs = refs[0:2], refs[2], refs[3], refs[4:6]
    q_ref, k_ref, s_ref, o_ref, sems = refs[6:11]
    coref = core_ref[0].astype(f32)
    cps = []

    def load(src, dst):
        cps.append(pltpu.make_async_copy(src, dst, sems.at[len(cps) + 2]))

    load(qs[0], q_ref.at[0])
    load(qs[1], q_ref.at[1])
    load(near, k_ref.at[0])
    load(far, k_ref.at[1])
    for cp in cps:
        cp.start()
    for cp in cps:
        cp.wait()
    lane = lax.broadcasted_iota(jnp.int32, (256, QW - LAT), 1)
    stores = []
    for step in range(2):
        q = q_ref[step, :, 0:KDIM]
        is_a = q_ref[step, :, KDIM : KDIM + 1].astype(f32) == coref
        best = []
        for g in range(2):
            m = None
            for t in range(4):
                s = jnp.dot(q, k_ref[g, t], preferred_element_type=f32)
                s_ref[g * 4 + t] = s
                ms = jnp.max(s, axis=1, keepdims=True)
                m = ms if m is None else jnp.maximum(m, ms)
            best.append(m)
        mu = jnp.where(is_a, best[0], best[1]) * SCALE2
        hi = mu.astype(bf16).astype(f32)
        lo = (mu - hi).astype(bf16).astype(f32)
        top = hi + lo
        total = jnp.zeros((256, 1), f32)
        acc = jnp.zeros((256, LAT), f32)
        for g in range(2):
            off = jnp.where(is_a if g == 0 else jnp.logical_not(is_a), -top, -1e30)
            for t in range(4):
                w = jnp.exp2(s_ref[g * 4 + t] * SCALE2 + off).astype(bf16)
                total = total + jnp.sum(w.astype(f32), axis=1, keepdims=True)
                acc = acc + lax.dot_general(
                    w,
                    k_ref[g, t, 0:LAT, :],
                    (((1,), (1,)), ((), ())),
                    preferred_element_type=f32,
                )
        o_ref[step, :, 0:LAT] = acc.astype(bf16)
        l_hi = total.astype(bf16).astype(f32)
        l_lo = total - l_hi
        tail = jnp.where(
            lane == 0,
            hi,
            jnp.where(lane == 1, lo, jnp.where(lane == 2, l_hi, jnp.where(lane == 3, l_lo, 0.0))),
        )
        o_ref[step, :, LAT:QW] = tail.astype(bf16)
        cp = pltpu.make_async_copy(o_ref.at[step], outs[step], sems.at[step])
        cp.start()
        stores.append(cp)
    for cp in stores:
        cp.wait()


def attend(core, qs, near, far):
    hbm = pl.BlockSpec(memory_space=pltpu.HBM)
    return pl.pallas_call(
        attend_kernel,
        out_shape=[pltpu.HBM((256, QW), bf16)] * 2,
        in_specs=[pl.BlockSpec(memory_space=pltpu.SMEM)] + [hbm] * 4,
        out_specs=[hbm] * 2,
        scratch_shapes=[
            pltpu.VMEM((2, 256, QW), bf16),
            pltpu.VMEM((2, 4, KDIM, 512), bf16),
            pltpu.VMEM((8, 256, 512), f32),
            pltpu.VMEM((2, 256, QW), bf16),
            pltpu.SemaphoreType.DMA((6,)),
        ],
        compiler_params=pltpu.CompilerParams(vmem_limit_bytes=40 << 20),
        cost_estimate=pl.CostEstimate(
            flops=4_500_000_000, transcendentals=2_000_000, bytes_accessed=6_000_000
        ),
        name="attend",
    )(core, *in_hbm(*qs, near, far))


def merge_kernel(q_ref, lat_ref, *refs):
    parts, out_ref = refs[0:4], refs[4]
    for leaf in range(4):
        r = slice(leaf * 64, leaf * 64 + 64)
        lat = lat_ref[leaf : leaf + 1, :].astype(f32)
        own = jnp.sum(q_ref[r, 0:KDIM].astype(f32) * lat, axis=1, keepdims=True) * SCALE2
        tails = [p[r, LAT:QW].astype(f32) for p in parts]
        tops = [t[:, 0:1] + t[:, 1:2] for t in tails]
        m = own
        for t in tops:
            m = jnp.maximum(m, t)
        w = jnp.exp2(own - m)
        num = w * lat[:, 0:LAT]
        den = w
        for p, t, top in zip(parts, tails, tops):
            w = jnp.exp2(top - m)
            num = num + w * p[r, 0:LAT].astype(f32)
            den = den + w * (t[:, 2:3] + t[:, 3:4])
        out_ref[r, :] = (num / den).astype(bf16)


def merge(q, lat, parts):
    vmem = pl.BlockSpec(memory_space=pltpu.VMEM)
    return pl.pallas_call(
        merge_kernel,
        out_shape=jax.ShapeDtypeStruct((256, LAT), bf16),
        in_specs=[vmem] * 6,
        out_specs=vmem,
        name="merge",
    )(q, lat, *parts)


def expert_kernel(e_ref, *refs):
    xs, (wg, wu, wd, wg2, wu2, wd2), outs = refs[0:5], refs[5:11], refs[11:16]
    x_ref, w_ref, d_ref, acc_ref, o_ref, sems = refs[16:22]
    bounds = [(k, min(k + KC, D)) for k in range(0, D, KC)]
    count = [0]

    def copy(src, dst):
        cp = pltpu.make_async_copy(src, dst, sems.at[count[0]])
        count[0] += 1
        cp.start()
        return cp

    steps = []
    for k0, k1 in bounds:
        cps = []
        for j, w in enumerate((wg, wu, wg2, wu2)):
            cps.append(copy(w.at[k0:k1, :], w_ref.at[k0:k1, j * 128 : j * 128 + 128]))
        end = XW if k1 == D else k1
        r = 0
        for x in xs:
            cps.append(copy(x.at[:, k0:end], x_ref.at[r : r + x.shape[0], k0:end]))
            r += x.shape[0]
        steps.append(cps)
    down = [copy(wd, d_ref.at[0:128, :]), copy(wd2, d_ref.at[128:256, :])]
    for i, (k0, k1) in enumerate(bounds):
        for cp in steps[i]:
            cp.wait()
        part = jnp.dot(x_ref[:, k0:k1], w_ref[k0:k1, :], preferred_element_type=f32)
        if i == 0:
            acc_ref[...] = part
        else:
            acc_ref[...] += part
    gates = x_ref[:, D:XW].astype(f32)
    lane = lax.broadcasted_iota(jnp.int32, (256, 128), 1)
    halves = []
    for j in range(2):
        e = e_ref[j]
        pick = jnp.logical_or(lane == e, lane == e + 8)
        weight = jnp.sum(jnp.where(pick, gates, 0.0), axis=1, keepdims=True)
        g = acc_ref[:, j * 256 : j * 256 + 128]
        u = acc_ref[:, j * 256 + 128 : j * 256 + 256]
        halves.append((g / (1.0 + jnp.exp(-g)) * u * weight).astype(bf16))
    hidden = jnp.concatenate(halves, axis=1)
    for cp in down:
        cp.wait()
    stores = []
    for n in range(0, D, 1024):
        y = jnp.dot(hidden, d_ref[:, n : n + 1024], preferred_element_type=f32)
        o_ref[:, n : n + 1024] = y.astype(bf16)
        r = 0
        for out in outs:
            stores.append(
                copy(o_ref.at[r : r + out.shape[0], n : n + 1024], out.at[:, n : n + 1024])
            )
            r += out.shape[0]
    for cp in stores:
        cp.wait()


def experts(e, xs, weights):
    hbm = pl.BlockSpec(memory_space=pltpu.HBM)
    return pl.pallas_call(
        expert_kernel,
        out_shape=[pltpu.HBM((n, D), bf16) for n in (64, 64, 32, 32, 64)],
        in_specs=[pl.BlockSpec(memory_space=pltpu.SMEM)] + [hbm] * 11,
        out_specs=[hbm] * 5,
        scratch_shapes=[
            pltpu.VMEM((256, XW), bf16),
            pltpu.VMEM((D, 512), bf16),
            pltpu.VMEM((256, D), bf16),
            pltpu.VMEM((256, 512), f32),
            pltpu.VMEM((256, D), bf16),
            pltpu.SemaphoreType.DMA((72,)),
        ],
        compiler_params=pltpu.CompilerParams(vmem_limit_bytes=48 << 20),
        cost_estimate=pl.CostEstimate(
            flops=3_000_000_000, transcendentals=65_536, bytes_accessed=18_000_000
        ),
        name="experts",
    )(e, *in_hbm(*xs, *weights))


def body(
    queries,
    own_latent,
    snapshots,
    leaf_snapshot,
    moe_input,
    expert_ids,
    gate_weights,
    w_gate,
    w_up,
    w_down,
):
    place = lax.axis_index("exp").astype(jnp.int32)
    core = place & 1

    hit = (expert_ids[:, :, None] == jnp.arange(8, dtype=jnp.int32)).astype(f32)
    gate = jnp.sum(gate_weights[:, :, None] * hit, axis=1)
    high = lax.reduce_precision(gate, 8, 7)
    tail = jnp.concatenate([high, gate - high, jnp.zeros((4, 112), f32)], axis=1).astype(bf16)
    row = jnp.concatenate([moe_input, tail], axis=1)
    rows = lax.all_to_all(
        jnp.broadcast_to(row[None], (16, 4, XW)), "seq", 0, 0, tiled=True
    ).reshape(64, XW)
    weights = [w_gate[0], w_up[0], w_down[0]]
    other = [shift(w, "c", 1) for w in weights]

    choice = jnp.broadcast_to(leaf_snapshot.astype(bf16)[:, None, None], (4, 64, QW - KDIM))
    query = jnp.concatenate([queries, choice], axis=2).reshape(256, QW)
    half = lax.dynamic_index_in_dim(jnp.transpose(snapshots, (0, 2, 1)), core, 0, keepdims=True)
    rows, half, query, *other = after(rows, half, query, *other)
    weights = weights + other

    z1, z3 = shift(rows, "z", 1), shift(rows, "z", 3)
    near = gather(half, "seq", GROUPS_X)
    q1, q3, q2 = shift(query, "y", 1), shift(query, "y", 3), shift(query, "y", 2)
    z1, z3, q1, q3, q2 = after(z1, z3, q1, q3, q2)
    xs = [rows, z1, shift(z1[:32], "z", 1), shift(z3[32:], "z", 3), z3]
    xs, near, q1, q2, q3 = after(xs, near, q1, q2, q3)
    far = shift(near, "c", 1)

    out0, out1, low, high, out3 = experts(jnp.stack([place, place ^ 1]), xs, weights)
    low, high = shift(low, "z", -1), shift(high, "z", 1)
    p1, p3 = attend(core[None], (q1, q3), near, far)
    low, high, p1, p3 = after(low, high, p1, p3)
    s1 = jnp.concatenate([add(out1[:32], low), out1[32:]], axis=0)
    s3 = jnp.concatenate([out3[:32], add(out3[32:], high)], axis=0)
    s1, s3, q2, again = after(s1, s3, q2, query)
    r1, r3 = shift(s1, "z", -1), shift(s3, "z", 1)
    v1, v3 = shift(p1, "y", -1), shift(p3, "y", 1)
    p2, p0 = attend(core[None], (q2, again), near, far)
    r1, r3, p2, p0, v1, v3 = after(r1, r3, p2, p0, v1, v3)
    v2 = shift(p2, "y", 2)
    own = add(out0, r1, r3).reshape(16, 4, D)
    moe = lax.all_to_all(own, "seq", 0, 0, tiled=True)
    moe = jnp.sum(moe.astype(f32), axis=0).astype(bf16)
    attn = merge(query, own_latent, [p0, v1, v2, v3]).reshape(4, 64, LAT)
    return attn, moe


def solution(mesh):
    in_specs = (
        P(AXES, None, None),
        P(AXES, None),
        P(None, "seq", None),
        P(AXES),
        P(AXES, None),
        P(AXES, None),
        P(AXES, None),
        P("exp", None, "seq"),
        P("exp", None, "seq"),
        P("exp", "seq", None),
    )
    out_specs = (P(AXES, None, None), P(AXES, None))
    return jax.shard_map(body, mesh=mesh, in_specs=in_specs, out_specs=out_specs, check_vma=False)
```

time: 213 us -> 155 us (0.73)
  waiting for transfers between devices: 94.6 us -> 70.3 us
  starting transfers between devices: 58.4 us -> 35.7 us
  local copies, waits for them, and re-layouts: 27.6 us -> 12.2 us
  Pallas kernels: 26.4 us -> 32.1 us
    ppermute x45 -> x18, waiting for transfers between devices: 94.6 us -> 54.7 us  [shift(): return lax.ppermute(a, AXES, pairs)]
    ppermute x45 -> x18, starting transfers between devices: 58.4 us -> 19.5 us  [shift(): return lax.ppermute(a, AXES, pairs)]
    all_to_all x0 -> x3, starting transfers between devices: none -> 16.2 us  [the longest x1 7.12 us: body(): lax.all_to_all(jnp.broadcast_to(row[None], (16, 4, XW)), 'seq', 0, 0, til...]
    all_to_all x0 -> x3, waiting for transfers between devices: none -> 15.6 us  [the longest x1 15.6 us: body(): lax.all_to_all(jnp.broadcast_to(row[None], (16, 4, XW)), 'seq', 0, 0, til...]
    unnamed x55 -> x42, local copies, waits for them, and re-layouts: 14 us -> 2.46 us
    ppermute x6 -> x0, local copies, waits for them, and re-layouts: 11.3 us -> none  [shift(): return lax.ppermute(a, AXES, pairs)]
    pallas_call x2 -> x3, Pallas kernels: 23.3 us -> 29.1 us  [the longest x2 20.4 us: attend(): pl.pallas_call(attend_kernel, out_shape=[pltpu.HBM((256, QW), bf16)] * 2,...]
    broadcast_in_dim x0 -> x2, local copies, waits for them, and re-layouts: none -> 4.19 us  [the longest x1 3.01 us: gather(): wide = jnp.broadcast_to(a, (len(groups[0]),) + a.shape[1:])]
  transfers between devices with their start and end apart: 45 -> 21, of which waited for: 16 -> 11; matrix products, arithmetic and copies ran while one was open for 8% -> 4% of each run, Pallas kernels for 12% -> 21%
where the time goes in v2:
time: 155 us; the launch traced here: 154 us
  waiting for transfers between devices  70.3 us (45%)
  starting transfers between devices  35.7 us (23%)
  Pallas kernels  32.1 us (21%)
  local copies, waits for them, and re-layouts  12.2 us (8%)
  other arithmetic  2.65 us (2%)
    ppermute x18, waiting for transfers between devices, shift(): return lax.ppermute(a, AXES, pairs)  54.7 us
    pallas_call x2, Pallas kernels, attend(): pl.pallas_call(attend_kernel, out_shape=[pltpu.HBM((256, QW), bf16)] * 2,...  20.4 us
    ppermute x18, starting transfers between devices, shift(): return lax.ppermute(a, AXES, pairs)  19.5 us
    all_to_all x1, waiting for transfers between devices, body(): lax.all_to_all(jnp.broadcast_to(row[None], (16, 4, XW)), 'seq', 0, 0, til...  15.6 us
    pallas_call x1, Pallas kernels, experts(): pl.pallas_call(expert_kernel, out_shape=[pltpu.HBM((n, D), bf16) for n in...  8.67 us
    all_to_all x1, starting transfers between devices, body(): lax.all_to_all(jnp.broadcast_to(row[None], (16, 4, XW)), 'seq', 0, 0, til...  7.12 us
    all_to_all x1, starting transfers between devices, body(): moe = lax.all_to_all(own, 'seq', 0, 0, tiled=True)  4.6 us
    all_to_all x1, starting transfers between devices, gather(): lax.all_to_all(wide, axis, 0, 0, tiled=True, axis_index_groups=groups)  4.5 us
  transfers between devices with their start and end apart: 21, of which 11 were waited for; matrix products, arithmetic and copies ran while one was open for 4% of the time, Pallas kernels for 21%

profile of v2, /device:TPU:0, one launch (start us, length us, event | category | flops | bytes accessed | tf_op | source)
XLA Modules:
  0.0 154.1 jit_solution(14625211071643641234)
XLA Ops:
  4.3 7.1 %all-to-all-start = ((bf16[16,4,7296]{2,1,0:T(4,128)(2,1)}), bf16[16,4,7296]{2,1,0:T(4,128)(2,1)S(1)}, u32[]{:S(2)}, u32[]{:S(2)}) async-start(bf16[16,4,7296]{2,1,0:T(4,128)(2,1)} %broadcast_in_dim.13), calls=%async_computation | async-start | bytes 1867776 | tf_op jit(solution)/shard_map/all_to_all | solution.py:277
  12.6 15.6 %all-to-all-done = bf16[16,4,7296]{2,1,0:T(4,128)(2,1)S(1)} async-done(((bf16[16,4,7296]{2,1,0:T(4,128)(2,1)}), bf16[16,4,7296]{2,1,0:T(4,128)(2,1)S(1)}, u32[]{:S(2)}, u32[]{:S(2)}) %all-to-all-start) | async-done | bytes 933920 | tf_op jit(solution)/shard_map/all_to_all | solution.py:277
  28.4 3.0 %broadcast_in_dim.16 = bf16[4,576,512]{2,1,0:T(8,128)(2,1)} broadcast(bf16[576,512]{1,0:T(8,128)(2,1)} %bitcast.11), dimensions={1,2} | broadcast | bytes 2949120 | tf_op jit(solution)/shard_map/broadcast_in_dim | solution.py:38
  31.4 4.5 %all-to-all-start.1 = ((bf16[4,576,512]{2,1,0:T(8,128)(2,1)}), bf16[4,576,512]{2,1,0:T(8,128)(2,1)}, u32[]{:S(2)}, u32[]{:S(2)}) async-start(bf16[4,576,512]{2,1,0:T(8,128)(2,1)} %broadcast_in_dim.16), calls=%async_computation.1 | async-start | bytes 4718592 | tf_op jit(solution)/shard_map/all_to_all | solution.py:39
  35.9 4.1 %collective-permute-start.4 = (bf16[64,7296]{1,0:T(8,128)(2,1)S(1)}, bf16[64,7296]{1,0:T(8,128)(2,1)S(1)}, u32[]{:S(2)}, u32[]{:S(2)}) collective-permute-start(bf16[64,7296]{1,0:T(8,128)(2,1)S(1)} %reshape.20.refs_0_), channel_id=1, source_target_pairs={{0,6},{1,7},{2,0},{3,1},{4,2},{5,3},{6,4},{7,5},{8,14},{9,15},{10,... | collective-permute-start | bytes 2801672 | tf_op jit(solution)/shard_map/ppermute | solution.py:34
  42.9 9.3 %collective-permute-done.7.refs_0_ = bf16[256,640]{1,0:T(8,128)(2,1)S(1)} collective-permute-done((bf16[256,640]{1,0:T(8,128)(2,1)S(1)}, bf16[256,640]{1,0:T(8,128)(2,1)S(1)}, u32[]{:S(2)}, u32[]{:S(2)}) %collective-permute-start.7) | collective-permute-done | bytes 327712 | tf_op jit(solution)/shard_map/ppermute | solution.py:34
  52.2 2.8 %collective-permute-done.6.refs_1_ = bf16[256,640]{1,0:T(8,128)(2,1)S(1)} collective-permute-done((bf16[256,640]{1,0:T(8,128)(2,1)S(1)}, bf16[256,640]{1,0:T(8,128)(2,1)S(1)}, u32[]{:S(2)}, u32[]{:S(2)}) %collective-permute-start.6) | collective-permute-done | bytes 327712 | tf_op jit(solution)/shard_map/ppermute | solution.py:34
  55.0 1.8 %collective-permute-done.5.refs_0_ = bf16[256,640]{1,0:T(8,128)(2,1)S(1)} collective-permute-done((bf16[256,640]{1,0:T(8,128)(2,1)S(1)}, bf16[256,640]{1,0:T(8,128)(2,1)S(1)}, u32[]{:S(2)}, u32[]{:S(2)}) %collective-permute-start.5) | collective-permute-done | bytes 327712 | tf_op jit(solution)/shard_map/ppermute | solution.py:34
  56.8 2.3 %collective-permute-done.4.refs_4_ = bf16[64,7296]{1,0:T(8,128)(2,1)S(1)} collective-permute-done((bf16[64,7296]{1,0:T(8,128)(2,1)S(1)}, bf16[64,7296]{1,0:T(8,128)(2,1)S(1)}, u32[]{:S(2)}, u32[]{:S(2)}) %collective-permute-start.4) | collective-permute-done | bytes 933920 | tf_op jit(solution)/shard_map/ppermute | solution.py:34
  59.0 3.4 %collective-permute-done.3.refs_1_ = bf16[64,7296]{1,0:T(8,128)(2,1)S(1)} collective-permute-done((bf16[64,7296]{1,0:T(8,128)(2,1)S(1)}, bf16[64,7296]{1,0:T(8,128)(2,1)S(1)}, u32[]{:S(2)}, u32[]{:S(2)}) %collective-permute-start.3) | collective-permute-done | bytes 933920 | tf_op jit(solution)/shard_map/ppermute | solution.py:34
  63.9 1.7 %collective-permute-start.8 = (bf16[32,7296]{1,0:T(8,128)(2,1)S(1)}, bf16[32,7296]{1,0:T(8,128)(2,1)S(1)}, u32[]{:S(2)}, u32[]{:S(2)}) collective-permute-start(bf16[32,7296]{1,0:T(8,128)(2,1)S(1)} %slice.18), channel_id=1, source_target_pairs={{0,2},{1,3},{2,4},{3,5},{4,6},{5,7},{6,0},{7,1},{8,10},{9,11},{10,... | collective-permute-start | bytes 1400840 | tf_op jit(solution)/shard_map/ppermute | solution.py:34
  65.6 8.3 %collective-permute-done.9.refs_3_ = bf16[32,7296]{1,0:T(8,128)(2,1)S(1)} collective-permute-done((bf16[32,7296]{1,0:T(8,128)(2,1)S(1)}, bf16[32,7296]{1,0:T(8,128)(2,1)S(1)}, u32[]{:S(2)}, u32[]{:S(2)}) %collective-permute-start.9) | collective-permute-done | bytes 466976 | tf_op jit(solution)/shard_map/ppermute | solution.py:34
  73.9 1.6 %collective-permute-done.8.refs_2_ = bf16[32,7296]{1,0:T(8,128)(2,1)S(1)} collective-permute-done((bf16[32,7296]{1,0:T(8,128)(2,1)S(1)}, bf16[32,7296]{1,0:T(8,128)(2,1)S(1)}, u32[]{:S(2)}, u32[]{:S(2)}) %collective-permute-start.8) | collective-permute-done | bytes 466976 | tf_op jit(solution)/shard_map/ppermute | solution.py:34
  76.3 8.7 %experts.1 = (bf16[64,7168]{1,0:T(8,128)(2,1)}, bf16[64,7168]{1,0:T(8,128)(2,1)}, bf16[32,7168]{1,0:T(8,128)(2,1)}, bf16[32,7168]{1,0:T(8,128)(2,1)}, bf16[64,7168]{1,0:T(8,128)(2,1)}) custom-call(s32[2]{0:T(128)S(1)} %pad_add_fusion.e_ref, bf16[64,7296]{1,0:T(8,128)(2,1)} %copy-done.1, bf16[64,7296]{1,0:T(8,128)(2,1)} %copy-done.3, ...), custom_call_target="tpu_custom_call" | custom-call | flops 3000000000 | bytes 18000000 | tf_op jit(solution)/shard_map/experts/pallas_call | solution.py:236
  85.5 1.6 %collective-permute-start.11 = (bf16[32,7168]{1,0:T(8,128)(2,1)}, bf16[32,7168]{1,0:T(8,128)(2,1)S(1)}, u32[]{:S(2)}, u32[]{:S(2)}) collective-permute-start(bf16[32,7168]{1,0:T(8,128)(2,1)} %get-tuple-element.63), channel_id=1, source_target_pairs={{0,2},{1,3},{2,4},{3,5},{4,6},{5,7},{6,0},{7,1},{8,10},{9,11},{10,... | collective-permute-start | bytes 1376264 | tf_op jit(solution)/shard_map/ppermute | solution.py:34
  89.2 10.3 %attend.2 = (bf16[256,640]{1,0:T(8,128)(2,1)}, bf16[256,640]{1,0:T(8,128)(2,1)}) custom-call(s32[1]{0:T(128)} %bitcast.8.core_ref, bf16[256,640]{1,0:T(8,128)(2,1)} %copy-done.16, bf16[256,640]{1,0:T(8,128)(2,1)} %copy-done.15, bf16[4,576,512]{2,1,0:T(8,128)(2,1)} %all-to-all-done.1.refs_2_, bf16[4,576,512]{2,1,0:T(8,128)(2,1)} %collective-permute-done.12.refs_3_), custom_call_target="tpu_custom_call" | custom-call | flops 4499999744 | bytes 6000000 | tf_op jit(solution)/shard_map/attend/pallas_call | solution.py:123
  99.9 1.7 %collective-permute-start.13 = (bf16[64,7168]{1,0:T(8,128)(2,1)S(1)}, bf16[64,7168]{1,0:T(8,128)(2,1)S(1)}, u32[]{:S(2)}, u32[]{:S(2)}) collective-permute-start(bf16[64,7168]{1,0:T(8,128)(2,1)S(1)} %pad_maximum_fusion), channel_id=1, source_target_pairs={{0,6},{1,7},{2,0},{3,1},{4,2},{5,3},{6,4},{7,5},{8,14},{9,15},{10,... | collective-permute-start | bytes 2752520 | tf_op jit(solution)/shard_map/ppermute | solution.py:34
  104.0 10.2 %attend.3 = (bf16[256,640]{1,0:T(8,128)(2,1)}, bf16[256,640]{1,0:T(8,128)(2,1)}) custom-call(s32[1]{0:T(128)} %bitcast.8.core_ref, bf16[256,640]{1,0:T(8,128)(2,1)} %copy-done.14, bf16[256,640]{1,0:T(8,128)(2,1)} %bitcast.21, bf16[4,576,512]{2,1,0:T(8,128)(2,1)} %all-to-all-done.1.refs_2_, bf16[4,576,512]{2,1,0:T(8,128)(2,1)} %collective-permute-done.12.refs_3_), custom_call_target="tpu_custom_call" | custom-call | flops 4499999744 | bytes 6000000 | tf_op jit(solution)/shard_map/attend/pallas_call | solution.py:123
  114.2 7.2 %collective-permute-done.13 = bf16[64,7168]{1,0:T(8,128)(2,1)S(1)} collective-permute-done((bf16[64,7168]{1,0:T(8,128)(2,1)S(1)}, bf16[64,7168]{1,0:T(8,128)(2,1)S(1)}, u32[]{:S(2)}, u32[]{:S(2)}) %collective-permute-start.13) | collective-permute-done | bytes 917536 | tf_op jit(solution)/shard_map/ppermute | solution.py:34
  121.4 2.7 %collective-permute-done.14 = bf16[64,7168]{1,0:T(8,128)(2,1)S(1)} collective-permute-done((bf16[64,7168]{1,0:T(8,128)(2,1)S(1)}, bf16[64,7168]{1,0:T(8,128)(2,1)S(1)}, u32[]{:S(2)}, u32[]{:S(2)}) %collective-permute-start.14) | collective-permute-done | bytes 917536 | tf_op jit(solution)/shard_map/ppermute | solution.py:34
  125.8 4.6 %all-to-all-start.2 = ((bf16[16,4,7168]{2,1,0:T(4,128)(2,1)}), bf16[16,4,7168]{2,1,0:T(4,128)(2,1)S(1)}, u32[]{:S(2)}, u32[]{:S(2)}) async-start(bf16[16,4,7168]{2,1,0:T(4,128)(2,1)} %reshape.23), calls=%async_computation.2 | async-start | bytes 1835008 | tf_op jit(solution)/shard_map/all_to_all | solution.py:310
  130.4 3.5 %collective-permute-start.17 = (bf16[256,640]{1,0:T(8,128)(2,1)S(1)}, bf16[256,640]{1,0:T(8,128)(2,1)S(1)}, u32[]{:S(2)}, u32[]{:S(2)}) collective-permute-start(bf16[256,640]{1,0:T(8,128)(2,1)S(1)} %copy-done.19), channel_id=1, source_target_pairs={{0,64},{1,65},{2,66},{3,67},{4,68},{5,69},{6,70},{7,71},{8,72},{9,... | collective-permute-start | bytes 983048 | tf_op jit(solution)/shard_map/ppermute | solution.py:34
  133.9 15.4 %collective-permute-done.17.refs_2_ = bf16[256,640]{1,0:T(8,128)(2,1)S(1)} collective-permute-done((bf16[256,640]{1,0:T(8,128)(2,1)S(1)}, bf16[256,640]{1,0:T(8,128)(2,1)S(1)}, u32[]{:S(2)}, u32[]{:S(2)}) %collective-permute-start.17) | collective-permute-done | bytes 327712 | tf_op jit(solution)/shard_map/ppermute | solution.py:34
  150.0 3.0 %merge.1 = bf16[256,512]{1,0:T(8,128)(2,1)} custom-call(bf16[256,640]{1,0:T(8,128)(2,1)} %bitcast.22, bf16[4,576]{1,0:T(4,128)(2,1)} %lat_ref.1, bf16[256,640]{1,0:T(8,128)(2,1)} %get-tuple-element.81.refs_0_, bf16[256,640]{1,0:T(8,128)(2,1)} %copy-done.10, bf16[256,640]{1,0:T(8,128)(2,1)} %copy-done.12, bf16[256,640]{1,0:T(8,128)(2,1)} %copy-done.11), custom_call_target="tpu_custom_call" | custom-call | tf_op jit(solution)/shard_map/merge/pallas_call | solution.py:166
  (86 shorter events, 18.8 us)
Async XLA Ops:
  0.7 27.7 %collective-permute-start = (bf16[7168,128]{1,0:T(8,128)(2,1)}, bf16[7168,128]{1,0:T(8,128)(2,1)}, u32[]{:S(2)}, u32[]{:S(2)}) collective-permute-start(bf16[7168,128]{1,0:T(8,128)(2,1)} %bitcast.12), channel_id=1, source_target_pairs={{0,1},{1,0},{2,3},{3,2},{4,5},{5,4},{6,7},{7,6},{8,9},{9,8},{10,11... | collective-permute-start | bytes 5505032 | tf_op jit(solution)/shard_map/ppermute | solution.py:34
  0.8 27.6 %collective-permute-start.1 = (bf16[7168,128]{1,0:T(8,128)(2,1)}, bf16[7168,128]{1,0:T(8,128)(2,1)}, u32[]{:S(2)}, u32[]{:S(2)}) collective-permute-start(bf16[7168,128]{1,0:T(8,128)(2,1)} %bitcast.14), channel_id=1, source_target_pairs={{0,1},{1,0},{2,3},{3,2},{4,5},{5,4},{6,7},{7,6},{8,9},{9,8},{10,11... | collective-permute-start | bytes 5505032 | tf_op jit(solution)/shard_map/ppermute | solution.py:34
  1.3 27.1 %collective-permute-start.2 = (bf16[128,7168]{1,0:T(8,128)(2,1)}, bf16[128,7168]{1,0:T(8,128)(2,1)}, u32[]{:S(2)}, u32[]{:S(2)}) collective-permute-start(bf16[128,7168]{1,0:T(8,128)(2,1)} %bitcast.16), channel_id=1, source_target_pairs={{0,1},{1,0},{2,3},{3,2},{4,5},{5,4},{6,7},{7,6},{8,9},{9,8},{10,11... | collective-permute-start | bytes 5505032 | tf_op jit(solution)/shard_map/ppermute | solution.py:34
  4.3 23.9 %all-to-all-start = ((bf16[16,4,7296]{2,1,0:T(4,128)(2,1)}), bf16[16,4,7296]{2,1,0:T(4,128)(2,1)S(1)}, u32[]{:S(2)}, u32[]{:S(2)}) async-start(bf16[16,4,7296]{2,1,0:T(4,128)(2,1)} %broadcast_in_dim.13), calls=%async_computation | async-start | bytes 1867776 | tf_op jit(solution)/shard_map/all_to_all | solution.py:277
  11.6 30.4 %copy-start.4 = (bf16[4,64,640]{2,1,0:T(8,128)(2,1)}, bf16[4,64,640]{2,1,0:T(8,128)(2,1)S(1)}, u32[]{:S(2)}) copy-start(bf16[4,64,640]{2,1,0:T(8,128)(2,1)S(1)} %pad_maximum_fusion.2) | copy-start | bytes 983044
  31.4 44.1 %all-to-all-start.1 = ((bf16[4,576,512]{2,1,0:T(8,128)(2,1)}), bf16[4,576,512]{2,1,0:T(8,128)(2,1)}, u32[]{:S(2)}, u32[]{:S(2)}) async-start(bf16[4,576,512]{2,1,0:T(8,128)(2,1)} %broadcast_in_dim.16), calls=%async_computation.1 | async-start | bytes 4718592 | tf_op jit(solution)/shard_map/all_to_all | solution.py:39
  35.9 23.1 %collective-permute-start.4 = (bf16[64,7296]{1,0:T(8,128)(2,1)S(1)}, bf16[64,7296]{1,0:T(8,128)(2,1)S(1)}, u32[]{:S(2)}, u32[]{:S(2)}) collective-permute-start(bf16[64,7296]{1,0:T(8,128)(2,1)S(1)} %reshape.20.refs_0_), channel_id=1, source_target_pairs={{0,6},{1,7},{2,0},{3,1},{4,2},{5,3},{6,4},{7,5},{8,14},{9,15},{10,... | collective-permute-start | bytes 2801672 | tf_op jit(solution)/shard_map/ppermute | solution.py:34
  40.0 22.4 %collective-permute-start.3 = (bf16[64,7296]{1,0:T(8,128)(2,1)S(1)}, bf16[64,7296]{1,0:T(8,128)(2,1)S(1)}, u32[]{:S(2)}, u32[]{:S(2)}) collective-permute-start(bf16[64,7296]{1,0:T(8,128)(2,1)S(1)} %reshape.20.refs_0_), channel_id=1, source_target_pairs={{0,2},{1,3},{2,4},{3,5},{4,6},{5,7},{6,0},{7,1},{8,10},{9,11},{10,... | collective-permute-start | bytes 2801672 | tf_op jit(solution)/shard_map/ppermute | solution.py:34
  40.0 12.2 %collective-permute-start.7 = (bf16[256,640]{1,0:T(8,128)(2,1)S(1)}, bf16[256,640]{1,0:T(8,128)(2,1)S(1)}, u32[]{:S(2)}, u32[]{:S(2)}) collective-permute-start(bf16[256,640]{1,0:T(8,128)(2,1)S(1)} %bitcast.18), channel_id=1, source_target_pairs={{0,64},{1,65},{2,66},{3,67},{4,68},{5,69},{6,70},{7,71},{8,72},{9,... | collective-permute-start | bytes 983048 | tf_op jit(solution)/shard_map/ppermute | solution.py:34
  40.9 14.1 %collective-permute-start.6 = (bf16[256,640]{1,0:T(8,128)(2,1)S(1)}, bf16[256,640]{1,0:T(8,128)(2,1)S(1)}, u32[]{:S(2)}, u32[]{:S(2)}) collective-permute-start(bf16[256,640]{1,0:T(8,128)(2,1)S(1)} %bitcast.19), channel_id=1, source_target_pairs={{0,96},{1,97},{2,98},{3,99},{4,100},{5,101},{6,102},{7,103},{8,104... | collective-permute-start | bytes 983048 | tf_op jit(solution)/shard_map/ppermute | solution.py:34
  42.0 14.7 %collective-permute-start.5 = (bf16[256,640]{1,0:T(8,128)(2,1)S(1)}, bf16[256,640]{1,0:T(8,128)(2,1)S(1)}, u32[]{:S(2)}, u32[]{:S(2)}) collective-permute-start(bf16[256,640]{1,0:T(8,128)(2,1)S(1)} %bitcast.20), channel_id=1, source_target_pairs={{0,32},{1,33},{2,34},{3,35},{4,36},{5,37},{6,38},{7,39},{8,40},{9,... | collective-permute-start | bytes 983048 | tf_op jit(solution)/shard_map/ppermute | solution.py:34
  59.0 16.5 %copy-start.2 = (bf16[64,7296]{1,0:T(8,128)(2,1)}, bf16[64,7296]{1,0:T(8,128)(2,1)S(1)}, u32[]{:S(2)}) copy-start(bf16[64,7296]{1,0:T(8,128)(2,1)S(1)} %collective-permute-done.4.refs_4_) | copy-start | bytes 2801668
  63.5 10.4 %collective-permute-start.9 = (bf16[32,7296]{1,0:T(8,128)(2,1)S(1)}, bf16[32,7296]{1,0:T(8,128)(2,1)S(1)}, u32[]{:S(2)}, u32[]{:S(2)}) collective-permute-start(bf16[32,7296]{1,0:T(8,128)(2,1)S(1)} %slice.19), channel_id=1, source_target_pairs={{0,6},{1,7},{2,0},{3,1},{4,2},{5,3},{6,4},{7,5},{8,14},{9,15},{10,... | collective-permute-start | bytes 1400840 | tf_op jit(solution)/shard_map/ppermute | solution.py:34
  63.9 11.6 %collective-permute-start.8 = (bf16[32,7296]{1,0:T(8,128)(2,1)S(1)}, bf16[32,7296]{1,0:T(8,128)(2,1)S(1)}, u32[]{:S(2)}, u32[]{:S(2)}) collective-permute-start(bf16[32,7296]{1,0:T(8,128)(2,1)S(1)} %slice.18), channel_id=1, source_target_pairs={{0,2},{1,3},{2,4},{3,5},{4,6},{5,7},{6,0},{7,1},{8,10},{9,11},{10,... | collective-permute-start | bytes 1400840 | tf_op jit(solution)/shard_map/ppermute | solution.py:34
  75.5 13.7 %collective-permute-start.12 = (bf16[4,576,512]{2,1,0:T(8,128)(2,1)}, bf16[4,576,512]{2,1,0:T(8,128)(2,1)}, u32[]{:S(2)}, u32[]{:S(2)}) collective-permute-start(bf16[4,576,512]{2,1,0:T(8,128)(2,1)} %all-to-all-done.1.refs_2_), channel_id=1, source_target_pairs={{0,1},{1,0},{2,3},{3,2},{4,5},{5,4},{6,7},{7,6},{8,9},{9,8},{10,11... | collective-permute-start | bytes 7077896 | tf_op jit(solution)/shard_map/ppermute | solution.py:34
  84.9 14.5 %collective-permute-start.10 = (bf16[32,7168]{1,0:T(8,128)(2,1)}, bf16[32,7168]{1,0:T(8,128)(2,1)S(1)}, u32[]{:S(2)}, u32[]{:S(2)}) collective-permute-start(bf16[32,7168]{1,0:T(8,128)(2,1)} %get-tuple-element.62), channel_id=1, source_target_pairs={{0,6},{1,7},{2,0},{3,1},{4,2},{5,3},{6,4},{7,5},{8,14},{9,15},{10,... | collective-permute-start | bytes 1376264 | tf_op jit(solution)/shard_map/ppermute | solution.py:34
  85.5 14.0 %collective-permute-start.11 = (bf16[32,7168]{1,0:T(8,128)(2,1)}, bf16[32,7168]{1,0:T(8,128)(2,1)S(1)}, u32[]{:S(2)}, u32[]{:S(2)}) collective-permute-start(bf16[32,7168]{1,0:T(8,128)(2,1)} %get-tuple-element.63), channel_id=1, source_target_pairs={{0,2},{1,3},{2,4},{3,5},{4,6},{5,7},{6,0},{7,1},{8,10},{9,11},{10,... | collective-permute-start | bytes 1376264 | tf_op jit(solution)/shard_map/ppermute | solution.py:34
  99.9 24.3 %copy-start.5 = (bf16[64,7168]{1,0:T(8,128)(2,1)S(1)}, bf16[64,7168]{1,0:T(8,128)(2,1)}, u32[]{:S(2)}) copy-start(bf16[64,7168]{1,0:T(8,128)(2,1)} %get-tuple-element.85) | copy-start | bytes 2752516
  99.9 21.6 %collective-permute-start.13 = (bf16[64,7168]{1,0:T(8,128)(2,1)S(1)}, bf16[64,7168]{1,0:T(8,128)(2,1)S(1)}, u32[]{:S(2)}, u32[]{:S(2)}) collective-permute-start(bf16[64,7168]{1,0:T(8,128)(2,1)S(1)} %pad_maximum_fusion), channel_id=1, source_target_pairs={{0,6},{1,7},{2,0},{3,1},{4,2},{5,3},{6,4},{7,5},{8,14},{9,15},{10,... | collective-permute-start | bytes 2752520 | tf_op jit(solution)/shard_map/ppermute | solution.py:34
  101.6 22.5 %collective-permute-start.14 = (bf16[64,7168]{1,0:T(8,128)(2,1)S(1)}, bf16[64,7168]{1,0:T(8,128)(2,1)S(1)}, u32[]{:S(2)}, u32[]{:S(2)}) collective-permute-start(bf16[64,7168]{1,0:T(8,128)(2,1)S(1)} %pad_maximum_fusion.1), channel_id=1, source_target_pairs={{0,2},{1,3},{2,4},{3,5},{4,6},{5,7},{6,0},{7,1},{8,10},{9,11},{10,... | collective-permute-start | bytes 2752520 | tf_op jit(solution)/shard_map/ppermute | solution.py:34
  102.0 12.2 %collective-permute-start.15 = (bf16[256,640]{1,0:T(8,128)(2,1)S(1)}, bf16[256,640]{1,0:T(8,128)(2,1)S(1)}, u32[]{:S(2)}, u32[]{:S(2)}) collective-permute-start(bf16[256,640]{1,0:T(8,128)(2,1)S(1)} %copy-done.18), channel_id=1, source_target_pairs={{0,96},{1,97},{2,98},{3,99},{4,100},{5,101},{6,102},{7,103},{8,104... | collective-permute-start | bytes 983048 | tf_op jit(solution)/shard_map/ppermute | solution.py:34
  103.0 11.2 %collective-permute-start.16 = (bf16[256,640]{1,0:T(8,128)(2,1)S(1)}, bf16[256,640]{1,0:T(8,128)(2,1)S(1)}, u32[]{:S(2)}, u32[]{:S(2)}) collective-permute-start(bf16[256,640]{1,0:T(8,128)(2,1)S(1)} %copy-done.17), channel_id=1, source_target_pairs={{0,32},{1,33},{2,34},{3,35},{4,36},{5,37},{6,38},{7,39},{8,40},{9,... | collective-permute-start | bytes 983048 | tf_op jit(solution)/shard_map/ppermute | solution.py:34
  125.8 27.3 %all-to-all-start.2 = ((bf16[16,4,7168]{2,1,0:T(4,128)(2,1)}), bf16[16,4,7168]{2,1,0:T(4,128)(2,1)S(1)}, u32[]{:S(2)}, u32[]{:S(2)}) async-start(bf16[16,4,7168]{2,1,0:T(4,128)(2,1)} %reshape.23), calls=%async_computation.2 | async-start | bytes 1835008 | tf_op jit(solution)/shard_map/all_to_all | solution.py:310
  130.4 18.9 %collective-permute-start.17 = (bf16[256,640]{1,0:T(8,128)(2,1)S(1)}, bf16[256,640]{1,0:T(8,128)(2,1)S(1)}, u32[]{:S(2)}, u32[]{:S(2)}) collective-permute-start(bf16[256,640]{1,0:T(8,128)(2,1)S(1)} %copy-done.19), channel_id=1, source_target_pairs={{0,64},{1,65},{2,66},{3,67},{4,68},{5,69},{6,70},{7,71},{8,72},{9,... | collective-permute-start | bytes 983048 | tf_op jit(solution)/shard_map/ppermute | solution.py:34
  (18 other events, 114.0 us)

commit v3 on v2

--- a/solution.py
+++ b/solution.py
@@ -15,7 +15,6 @@
 KC = 2560
 SCALE2 = 192.0 ** (-0.5) * math.log2(math.e)
 AXES = ("seq", "exp")
-GROUPS_X = [[4 * y + x for x in range(4)] for y in range(4)]
 bf16 = jnp.bfloat16
 f32 = jnp.float32
 
@@ -34,11 +33,6 @@
     return lax.ppermute(a, AXES, pairs)
 
 
-def gather(a, axis, groups):
-    wide = jnp.broadcast_to(a, (len(groups[0]),) + a.shape[1:])
-    return lax.all_to_all(wide, axis, 0, 0, tiled=True, axis_index_groups=groups)
-
-
 def after(*arrays):
     return lax.optimization_barrier(arrays)
 
@@ -55,9 +49,10 @@
 
 
 def attend_kernel(core_ref, *refs):
-    qs, near, far, outs = refs[0:2], refs[2], refs[3], refs[4:6]
-    q_ref, k_ref, s_ref, o_ref, sems = refs[6:11]
-    coref = core_ref[0].astype(f32)
+    qs, own, near, far, outs = refs[0:2], refs[2], refs[3], refs[4], refs[5:7]
+    q_ref, k_ref, s_ref, o_ref, sems = refs[7:12]
+    core = core_ref[0]
+    coref = core.astype(f32)
     cps = []
 
     def load(src, dst):
@@ -65,8 +60,9 @@
 
     load(qs[0], q_ref.at[0])
     load(qs[1], q_ref.at[1])
-    load(near, k_ref.at[0])
-    load(far, k_ref.at[1])
+    for g, (mine, got) in enumerate(((own.at[core], near), (own.at[1 - core], far))):
+        load(mine, k_ref.at[g, 0])
+        load(got, k_ref.at[g, 1:4])
     for cp in cps:
         cp.start()
     for cp in cps:
@@ -118,26 +114,26 @@
         cp.wait()
 
 
-def attend(core, qs, near, far):
+def attend(core, qs, own, near, far):
     hbm = pl.BlockSpec(memory_space=pltpu.HBM)
     return pl.pallas_call(
         attend_kernel,
         out_shape=[pltpu.HBM((256, QW), bf16)] * 2,
-        in_specs=[pl.BlockSpec(memory_space=pltpu.SMEM)] + [hbm] * 4,
+        in_specs=[pl.BlockSpec(memory_space=pltpu.SMEM)] + [hbm] * 5,
         out_specs=[hbm] * 2,
         scratch_shapes=[
             pltpu.VMEM((2, 256, QW), bf16),
             pltpu.VMEM((2, 4, KDIM, 512), bf16),
             pltpu.VMEM((8, 256, 512), f32),
             pltpu.VMEM((2, 256, QW), bf16),
-            pltpu.SemaphoreType.DMA((6,)),
+            pltpu.SemaphoreType.DMA((8,)),
         ],
         compiler_params=pltpu.CompilerParams(vmem_limit_bytes=40 << 20),
         cost_estimate=pl.CostEstimate(
             flops=4_500_000_000, transcendentals=2_000_000, bytes_accessed=6_000_000
         ),
         name="attend",
-    )(core, *in_hbm(*qs, near, far))
+    )(core, *in_hbm(*qs, own, near.reshape(3, KDIM, 512), far.reshape(3, KDIM, 512)))
 
 
 def merge_kernel(q_ref, lat_ref, *refs):
@@ -282,30 +278,33 @@
 
     choice = jnp.broadcast_to(leaf_snapshot.astype(bf16)[:, None, None], (4, 64, QW - KDIM))
     query = jnp.concatenate([queries, choice], axis=2).reshape(256, QW)
-    half = lax.dynamic_index_in_dim(jnp.transpose(snapshots, (0, 2, 1)), core, 0, keepdims=True)
+    keys = jnp.transpose(snapshots, (0, 2, 1))
+    half = lax.dynamic_index_in_dim(keys, core, 0, keepdims=False)
     rows, half, query, *other = after(rows, half, query, *other)
     weights = weights + other
 
     z1, z3 = shift(rows, "z", 1), shift(rows, "z", 3)
-    near = gather(half, "seq", GROUPS_X)
-    q1, q3, q2 = shift(query, "y", 1), shift(query, "y", 3), shift(query, "y", 2)
-    z1, z3, q1, q3, q2 = after(z1, z3, q1, q3, q2)
+    k1, k3, q1 = shift(half, "x", 1), shift(half, "x", 3), shift(query, "y", 1)
+    z1, z3, k1, k3, q1, half, query = after(z1, z3, k1, k3, q1, half, query)
     xs = [rows, z1, shift(z1[:32], "z", 1), shift(z3[32:], "z", 3), z3]
-    xs, near, q1, q2, q3 = after(xs, near, q1, q2, q3)
+    k2, q3, q2 = shift(half, "x", 2), shift(query, "y", 3), shift(query, "y", 2)
+    xs, k2, q3 = after(xs, k2, q3)
+    near = jnp.concatenate([k1, k2, k3], axis=0)
     far = shift(near, "c", 1)
 
     out0, out1, low, high, out3 = experts(jnp.stack([place, place ^ 1]), xs, weights)
     low, high = shift(low, "z", -1), shift(high, "z", 1)
-    p1, p3 = attend(core[None], (q1, q3), near, far)
+    p1, p3 = attend(core[None], (q1, q3), keys, near, far)
     low, high, p1, p3 = after(low, high, p1, p3)
     s1 = jnp.concatenate([add(out1[:32], low), out1[32:]], axis=0)
     s3 = jnp.concatenate([out3[:32], add(out3[32:], high)], axis=0)
     s1, s3, q2, again = after(s1, s3, q2, query)
     r1, r3 = shift(s1, "z", -1), shift(s3, "z", 1)
     v1, v3 = shift(p1, "y", -1), shift(p3, "y", 1)
-    p2, p0 = attend(core[None], (q2, again), near, far)
-    r1, r3, p2, p0, v1, v3 = after(r1, r3, p2, p0, v1, v3)
+    p2, p0 = attend(core[None], (q2, again), keys, near, far)
     v2 = shift(p2, "y", 2)
+    r1, r3, p0, v1, v3 = after(r1, r3, p0, v1, v3)
+    r1, r3, v2 = after(r1, r3, v2)
     own = add(out0, r1, r3).reshape(16, 4, D)
     moe = lax.all_to_all(own, "seq", 0, 0, tiled=True)
     moe = jnp.sum(moe.astype(f32), axis=0).astype(bf16)

time: 155 us -> 145 us (0.935)
  waiting for transfers between devices: 70.3 us -> 59.1 us
  starting transfers between devices: 35.7 us -> 39.7 us
  local copies, waits for them, and re-layouts: 12.2 us -> 10.2 us
    ppermute x18 -> x21, waiting for transfers between devices: 54.7 us -> 32.8 us  [shift(): return lax.ppermute(a, AXES, pairs)]
    all_to_all x1, waiting for transfers between devices: 0.01 us -> 11 us  [body(): moe = lax.all_to_all(own, 'seq', 0, 0, tiled=True)]
    ppermute x18 -> x21, starting transfers between devices: 19.5 us -> 26.5 us  [shift(): return lax.ppermute(a, AXES, pairs)]
    all_to_all x1 -> x0, starting transfers between devices: 4.5 us -> none  [gather(): lax.all_to_all(wide, axis, 0, 0, tiled=True, axis_index_groups=groups)]
    broadcast_in_dim x1 -> x0, local copies, waits for them, and re-layouts: 3.01 us -> none  [gather(): wide = jnp.broadcast_to(a, (len(groups[0]),) + a.shape[1:])]
  transfers between devices with their start and end apart: 21 -> 23, of which waited for: 11 -> 10; matrix products, arithmetic and copies ran while one was open for 4% -> 6% of each run, Pallas kernels for 21% -> 22%
where the time goes in v3:
time: 145 us
  waiting for transfers between devices  59.1 us (41%)
  starting transfers between devices  39.7 us (27%)
  Pallas kernels  32.1 us (22%)
  local copies, waits for them, and re-layouts  10.2 us (7%)
  other arithmetic  2.66 us (2%)
    ppermute x21, waiting for transfers between devices, shift(): return lax.ppermute(a, AXES, pairs)  32.8 us
    ppermute x21, starting transfers between devices, shift(): return lax.ppermute(a, AXES, pairs)  26.5 us
    pallas_call x2, Pallas kernels, attend(): pl.pallas_call(attend_kernel, out_shape=[pltpu.HBM((256, QW), bf16)] * 2,...  20.4 us
    all_to_all x1, waiting for transfers between devices, body(): lax.all_to_all(jnp.broadcast_to(row[None], (16, 4, XW)), 'seq', 0, 0, til...  15.3 us
    all_to_all x1, waiting for transfers between devices, body(): moe = lax.all_to_all(own, 'seq', 0, 0, tiled=True)  11 us
    pallas_call x1, Pallas kernels, experts(): pl.pallas_call(expert_kernel, out_shape=[pltpu.HBM((n, D), bf16) for n in...  8.63 us
    all_to_all x1, starting transfers between devices, body(): lax.all_to_all(jnp.broadcast_to(row[None], (16, 4, XW)), 'seq', 0, 0, til...  7.12 us
    all_to_all x1, starting transfers between devices, body(): moe = lax.all_to_all(own, 'seq', 0, 0, tiled=True)  6.08 us
  transfers between devices with their start and end apart: 23, of which 10 were waited for; matrix products, arithmetic and copies ran while one was open for 6% of the time, Pallas kernels for 22%

profile of v3, /device:TPU:0, one launch (start us, length us, event | category | flops | bytes accessed | tf_op | source)
XLA Modules:
  0.0 144.8 jit_solution(11070416359180821941)
XLA Ops:
  4.2 7.1 %all-to-all-start = ((bf16[16,4,7296]{2,1,0:T(4,128)(2,1)}), bf16[16,4,7296]{2,1,0:T(4,128)(2,1)S(1)}, u32[]{:S(2)}, u32[]{:S(2)}) async-start(bf16[16,4,7296]{2,1,0:T(4,128)(2,1)} %broadcast_in_dim.9), calls=%async_computation | async-start | bytes 1867776 | tf_op jit(solution)/shard_map/all_to_all | solution.py:273
  12.8 15.3 %all-to-all-done = bf16[16,4,7296]{2,1,0:T(4,128)(2,1)S(1)} async-done(((bf16[16,4,7296]{2,1,0:T(4,128)(2,1)}), bf16[16,4,7296]{2,1,0:T(4,128)(2,1)S(1)}, u32[]{:S(2)}, u32[]{:S(2)}) %all-to-all-start) | async-done | bytes 933920 | tf_op jit(solution)/shard_map/all_to_all | solution.py:273
  28.4 2.0 %collective-permute-start.3 = (bf16[64,7296]{1,0:T(8,128)(2,1)S(1)}, bf16[64,7296]{1,0:T(8,128)(2,1)S(1)}, u32[]{:S(2)}, u32[]{:S(2)}) collective-permute-start(bf16[64,7296]{1,0:T(8,128)(2,1)S(1)} %reshape.28.refs_0_), channel_id=1, source_target_pairs={{0,2},{1,3},{2,4},{3,5},{4,6},{5,7},{6,0},{7,1},{8,10},{9,11},{10,... | collective-permute-start | bytes 2801672 | tf_op jit(solution)/shard_map/ppermute | solution.py:33
  30.3 2.2 %collective-permute-start.4 = (bf16[64,7296]{1,0:T(8,128)(2,1)S(1)}, bf16[64,7296]{1,0:T(8,128)(2,1)S(1)}, u32[]{:S(2)}, u32[]{:S(2)}) collective-permute-start(bf16[64,7296]{1,0:T(8,128)(2,1)S(1)} %reshape.28.refs_0_), channel_id=1, source_target_pairs={{0,6},{1,7},{2,0},{3,1},{4,2},{5,3},{6,4},{7,5},{8,14},{9,15},{10,... | collective-permute-start | bytes 2801672 | tf_op jit(solution)/shard_map/ppermute | solution.py:33
  32.9 2.9 %collective-permute-start.6 = (bf16[576,512]{1,0:T(8,128)(2,1)S(1)}, bf16[576,512]{1,0:T(8,128)(2,1)S(1)}, u32[]{:S(2)}, u32[]{:S(2)}) collective-permute-start(bf16[576,512]{1,0:T(8,128)(2,1)S(1)} %dynamic-slice_bitcast_fusion), channel_id=1, source_target_pairs={{0,24},{1,25},{2,26},{3,27},{4,28},{5,29},{6,30},{7,31},{8,0},{9,1... | collective-permute-start | bytes 1769480 | tf_op jit(solution)/shard_map/ppermute | solution.py:33
  35.8 8.8 %collective-permute-done.7.refs_0_ = bf16[256,640]{1,0:T(8,128)(2,1)S(1)} collective-permute-done((bf16[256,640]{1,0:T(8,128)(2,1)S(1)}, bf16[256,640]{1,0:T(8,128)(2,1)S(1)}, u32[]{:S(2)}, u32[]{:S(2)}) %collective-permute-start.7) | collective-permute-done | bytes 327712 | tf_op jit(solution)/shard_map/ppermute | solution.py:33
  44.6 2.9 %collective-permute-done.5 = bf16[576,512]{1,0:T(8,128)(2,1)S(1)} collective-permute-done((bf16[576,512]{1,0:T(8,128)(2,1)S(1)}, bf16[576,512]{1,0:T(8,128)(2,1)S(1)}, u32[]{:S(2)}, u32[]{:S(2)}) %collective-permute-start.5) | collective-permute-done | bytes 589856 | tf_op jit(solution)/shard_map/ppermute | solution.py:33
  47.6 4.6 %collective-permute-done.3.refs_1_ = bf16[64,7296]{1,0:T(8,128)(2,1)S(1)} collective-permute-done((bf16[64,7296]{1,0:T(8,128)(2,1)S(1)}, bf16[64,7296]{1,0:T(8,128)(2,1)S(1)}, u32[]{:S(2)}, u32[]{:S(2)}) %collective-permute-start.3) | collective-permute-done | bytes 933920 | tf_op jit(solution)/shard_map/ppermute | solution.py:33
  52.2 1.8 %collective-permute-start.10 = (bf16[576,512]{1,0:T(8,128)(2,1)S(1)}, bf16[576,512]{1,0:T(8,128)(2,1)S(1)}, u32[]{:S(2)}, u32[]{:S(2)}) collective-permute-start(bf16[576,512]{1,0:T(8,128)(2,1)S(1)} %dynamic-slice_bitcast_fusion), channel_id=1, source_target_pairs={{0,16},{1,17},{2,18},{3,19},{4,20},{5,21},{6,22},{7,23},{8,24},{9,... | collective-permute-start | bytes 1769480 | tf_op jit(solution)/shard_map/ppermute | solution.py:33
  55.3 2.1 %collective-permute-start.9 = (bf16[32,7296]{1,0:T(8,128)(2,1)S(1)}, bf16[32,7296]{1,0:T(8,128)(2,1)S(1)}, u32[]{:S(2)}, u32[]{:S(2)}) collective-permute-start(bf16[32,7296]{1,0:T(8,128)(2,1)S(1)} %slice.19), channel_id=1, source_target_pairs={{0,6},{1,7},{2,0},{3,1},{4,2},{5,3},{6,4},{7,5},{8,14},{9,15},{10,... | collective-permute-start | bytes 1400840 | tf_op jit(solution)/shard_map/ppermute | solution.py:33
  59.6 6.2 %collective-permute-done.11.refs_1_ = bf16[256,640]{1,0:T(8,128)(2,1)S(1)} collective-permute-done((bf16[256,640]{1,0:T(8,128)(2,1)S(1)}, bf16[256,640]{1,0:T(8,128)(2,1)S(1)}, u32[]{:S(2)}, u32[]{:S(2)}) %collective-permute-start.11) | collective-permute-done | bytes 327712 | tf_op jit(solution)/shard_map/ppermute | solution.py:33
  69.2 8.6 %experts.1 = (bf16[64,7168]{1,0:T(8,128)(2,1)}, bf16[64,7168]{1,0:T(8,128)(2,1)}, bf16[32,7168]{1,0:T(8,128)(2,1)}, bf16[32,7168]{1,0:T(8,128)(2,1)}, bf16[64,7168]{1,0:T(8,128)(2,1)}) custom-call(s32[2]{0:T(128)S(1)} %pad_add_fusion.e_ref, bf16[64,7296]{1,0:T(8,128)(2,1)} %copy-done, bf16[64,7296]{1,0:T(8,128)(2,1)} %copy-done.1, ...), custom_call_target="tpu_custom_call" | custom-call | flops 3000000000 | bytes 18000000 | tf_op jit(solution)/shard_map/experts/pallas_call | solution.py:232
  77.8 3.1 %collective-permute-start.12 = (bf16[32,7168]{1,0:T(8,128)(2,1)}, bf16[32,7168]{1,0:T(8,128)(2,1)S(1)}, u32[]{:S(2)}, u32[]{:S(2)}) collective-permute-start(bf16[32,7168]{1,0:T(8,128)(2,1)} %get-tuple-element.63), channel_id=1, source_target_pairs={{0,6},{1,7},{2,0},{3,1},{4,2},{5,3},{6,4},{7,5},{8,14},{9,15},{10,... | collective-permute-start | bytes 1376264 | tf_op jit(solution)/shard_map/ppermute | solution.py:33
  80.9 1.7 %collective-permute-start.15 = (bf16[256,640]{1,0:T(8,128)(2,1)S(1)}, bf16[256,640]{1,0:T(8,128)(2,1)S(1)}, u32[]{:S(2)}, u32[]{:S(2)}) collective-permute-start(bf16[256,640]{1,0:T(8,128)(2,1)S(1)} %bitcast.23), channel_id=1, source_target_pairs={{0,64},{1,65},{2,66},{3,67},{4,68},{5,69},{6,70},{7,71},{8,72},{9,... | collective-permute-start | bytes 983048 | tf_op jit(solution)/shard_map/ppermute | solution.py:33
  84.7 10.3 %attend.2 = (bf16[256,640]{1,0:T(8,128)(2,1)}, bf16[256,640]{1,0:T(8,128)(2,1)}) custom-call(s32[1]{0:T(128)} %bitcast.8.core_ref, bf16[256,640]{1,0:T(8,128)(2,1)} %copy-done.13, bf16[256,640]{1,0:T(8,128)(2,1)} %copy-done.14, bf16[2,576,512]{2,1,0:T(8,128)(2,1)} %bitcast.26, bf16[3,576,512]{2,1,0:T(8,128)(2,1)} %bitcast.10.refs_3_, ...), custom_call_target="tpu_custom_call" | custom-call | flops 4499999744 | bytes 6000000 | tf_op jit(solution)/shard_map/attend/pallas_call | solution.py:119
  95.4 3.3 %collective-permute-start.16 = (bf16[64,7168]{1,0:T(8,128)(2,1)S(1)}, bf16[64,7168]{1,0:T(8,128)(2,1)S(1)}, u32[]{:S(2)}, u32[]{:S(2)}) collective-permute-start(bf16[64,7168]{1,0:T(8,128)(2,1)S(1)} %pad_maximum_fusion), channel_id=1, source_target_pairs={{0,6},{1,7},{2,0},{3,1},{4,2},{5,3},{6,4},{7,5},{8,14},{9,15},{10,... | collective-permute-start | bytes 2752520 | tf_op jit(solution)/shard_map/ppermute | solution.py:33
  98.8 1.9 %collective-permute-start.18 = (bf16[256,640]{1,0:T(8,128)(2,1)S(1)}, bf16[256,640]{1,0:T(8,128)(2,1)S(1)}, u32[]{:S(2)}, u32[]{:S(2)}) collective-permute-start(bf16[256,640]{1,0:T(8,128)(2,1)S(1)} %copy-done.17), channel_id=1, source_target_pairs={{0,96},{1,97},{2,98},{3,99},{4,100},{5,101},{6,102},{7,103},{8,104... | collective-permute-start | bytes 983048 | tf_op jit(solution)/shard_map/ppermute | solution.py:33
  100.8 10.1 %attend.3 = (bf16[256,640]{1,0:T(8,128)(2,1)}, bf16[256,640]{1,0:T(8,128)(2,1)}) custom-call(s32[1]{0:T(128)} %bitcast.8.core_ref, bf16[256,640]{1,0:T(8,128)(2,1)} %copy-done.16, bf16[256,640]{1,0:T(8,128)(2,1)} %bitcast.24, bf16[2,576,512]{2,1,0:T(8,128)(2,1)} %bitcast.27, bf16[3,576,512]{2,1,0:T(8,128)(2,1)} %bitcast.10.refs_3_, ...), custom_call_target="tpu_custom_call" | custom-call | flops 4499999744 | bytes 6000000 | tf_op jit(solution)/shard_map/attend/pallas_call | solution.py:119
  110.9 1.9 %collective-permute-start.20 = (bf16[256,640]{1,0:T(8,128)(2,1)}, bf16[256,640]{1,0:T(8,128)(2,1)S(1)}, u32[]{:S(2)}, u32[]{:S(2)}) collective-permute-start(bf16[256,640]{1,0:T(8,128)(2,1)} %get-tuple-element.86), channel_id=1, source_target_pairs={{0,64},{1,65},{2,66},{3,67},{4,68},{5,69},{6,70},{7,71},{8,72},{9,... | collective-permute-start | bytes 983048 | tf_op jit(solution)/shard_map/ppermute | solution.py:33
  112.9 5.3 %collective-permute-done.16 = bf16[64,7168]{1,0:T(8,128)(2,1)S(1)} collective-permute-done((bf16[64,7168]{1,0:T(8,128)(2,1)S(1)}, bf16[64,7168]{1,0:T(8,128)(2,1)S(1)}, u32[]{:S(2)}, u32[]{:S(2)}) %collective-permute-start.16) | collective-permute-done | bytes 917536 | tf_op jit(solution)/shard_map/ppermute | solution.py:33
  118.2 3.4 %collective-permute-done.17 = bf16[64,7168]{1,0:T(8,128)(2,1)S(1)} collective-permute-done((bf16[64,7168]{1,0:T(8,128)(2,1)S(1)}, bf16[64,7168]{1,0:T(8,128)(2,1)S(1)}, u32[]{:S(2)}, u32[]{:S(2)}) %collective-permute-start.17) | collective-permute-done | bytes 917536 | tf_op jit(solution)/shard_map/ppermute | solution.py:33
  123.6 6.1 %all-to-all-start.1 = ((bf16[16,4,7168]{2,1,0:T(4,128)(2,1)}), bf16[16,4,7168]{2,1,0:T(4,128)(2,1)S(1)}, u32[]{:S(2)}, u32[]{:S(2)}) async-start(bf16[16,4,7168]{2,1,0:T(4,128)(2,1)} %reshape.33), calls=%async_computation.1 | async-start | bytes 1835008 | tf_op jit(solution)/shard_map/all_to_all | solution.py:309
  129.7 3.0 %merge.1 = bf16[256,512]{1,0:T(8,128)(2,1)} custom-call(bf16[256,640]{1,0:T(8,128)(2,1)} %bitcast.25, bf16[4,576]{1,0:T(4,128)(2,1)} %lat_ref.1, bf16[256,640]{1,0:T(8,128)(2,1)} %get-tuple-element.82.refs_0_, bf16[256,640]{1,0:T(8,128)(2,1)} %copy-done.9, bf16[256,640]{1,0:T(8,128)(2,1)} %copy-done.11, bf16[256,640]{1,0:T(8,128)(2,1)} %copy-done.10), custom_call_target="tpu_custom_call" | custom-call | tf_op jit(solution)/shard_map/merge/pallas_call | solution.py:162
  132.7 11.0 %all-to-all-done.1 = bf16[16,4,7168]{2,1,0:T(4,128)(2,1)S(1)} async-done(((bf16[16,4,7168]{2,1,0:T(4,128)(2,1)}), bf16[16,4,7168]{2,1,0:T(4,128)(2,1)S(1)}, u32[]{:S(2)}, u32[]{:S(2)}) %all-to-all-start.1) | async-done | bytes 917536 | tf_op jit(solution)/shard_map/all_to_all | solution.py:309
  (88 shorter events, 18.0 us)
Async XLA Ops:
  0.7 27.7 %collective-permute-start = (bf16[7168,128]{1,0:T(8,128)(2,1)}, bf16[7168,128]{1,0:T(8,128)(2,1)}, u32[]{:S(2)}, u32[]{:S(2)}) collective-permute-start(bf16[7168,128]{1,0:T(8,128)(2,1)} %bitcast.15), channel_id=1, source_target_pairs={{0,1},{1,0},{2,3},{3,2},{4,5},{5,4},{6,7},{7,6},{8,9},{9,8},{10,11... | collective-permute-start | bytes 5505032 | tf_op jit(solution)/shard_map/ppermute | solution.py:33
  0.7 27.6 %collective-permute-start.1 = (bf16[7168,128]{1,0:T(8,128)(2,1)}, bf16[7168,128]{1,0:T(8,128)(2,1)}, u32[]{:S(2)}, u32[]{:S(2)}) collective-permute-start(bf16[7168,128]{1,0:T(8,128)(2,1)} %bitcast.17), channel_id=1, source_target_pairs={{0,1},{1,0},{2,3},{3,2},{4,5},{5,4},{6,7},{7,6},{8,9},{9,8},{10,11... | collective-permute-start | bytes 5505032 | tf_op jit(solution)/shard_map/ppermute | solution.py:33
  1.2 27.1 %collective-permute-start.2 = (bf16[128,7168]{1,0:T(8,128)(2,1)}, bf16[128,7168]{1,0:T(8,128)(2,1)}, u32[]{:S(2)}, u32[]{:S(2)}) collective-permute-start(bf16[128,7168]{1,0:T(8,128)(2,1)} %bitcast.19), channel_id=1, source_target_pairs={{0,1},{1,0},{2,3},{3,2},{4,5},{5,4},{6,7},{7,6},{8,9},{9,8},{10,11... | collective-permute-start | bytes 5505032 | tf_op jit(solution)/shard_map/ppermute | solution.py:33
  4.2 23.9 %all-to-all-start = ((bf16[16,4,7296]{2,1,0:T(4,128)(2,1)}), bf16[16,4,7296]{2,1,0:T(4,128)(2,1)S(1)}, u32[]{:S(2)}, u32[]{:S(2)}) async-start(bf16[16,4,7296]{2,1,0:T(4,128)(2,1)} %broadcast_in_dim.9), calls=%async_computation | async-start | bytes 1867776 | tf_op jit(solution)/shard_map/all_to_all | solution.py:273
  11.6 69.3 %copy-start.3 = (bf16[4,64,640]{2,1,0:T(8,128)(2,1)}, bf16[4,64,640]{2,1,0:T(8,128)(2,1)S(1)}, u32[]{:S(2)}) copy-start(bf16[4,64,640]{2,1,0:T(8,128)(2,1)S(1)} %pad_maximum_fusion.2) | copy-start | bytes 983044
  28.4 23.8 %collective-permute-start.3 = (bf16[64,7296]{1,0:T(8,128)(2,1)S(1)}, bf16[64,7296]{1,0:T(8,128)(2,1)S(1)}, u32[]{:S(2)}, u32[]{:S(2)}) collective-permute-start(bf16[64,7296]{1,0:T(8,128)(2,1)S(1)} %reshape.28.refs_0_), channel_id=1, source_target_pairs={{0,2},{1,3},{2,4},{3,5},{4,6},{5,7},{6,0},{7,1},{8,10},{9,11},{10,... | collective-permute-start | bytes 2801672 | tf_op jit(solution)/shard_map/ppermute | solution.py:33
  30.3 21.9 %collective-permute-start.4 = (bf16[64,7296]{1,0:T(8,128)(2,1)S(1)}, bf16[64,7296]{1,0:T(8,128)(2,1)S(1)}, u32[]{:S(2)}, u32[]{:S(2)}) collective-permute-start(bf16[64,7296]{1,0:T(8,128)(2,1)S(1)} %reshape.28.refs_0_), channel_id=1, source_target_pairs={{0,6},{1,7},{2,0},{3,1},{4,2},{5,3},{6,4},{7,5},{8,14},{9,15},{10,... | collective-permute-start | bytes 2801672 | tf_op jit(solution)/shard_map/ppermute | solution.py:33
  32.5 15.0 %collective-permute-start.5 = (bf16[576,512]{1,0:T(8,128)(2,1)S(1)}, bf16[576,512]{1,0:T(8,128)(2,1)S(1)}, u32[]{:S(2)}, u32[]{:S(2)}) collective-permute-start(bf16[576,512]{1,0:T(8,128)(2,1)S(1)} %dynamic-slice_bitcast_fusion), channel_id=1, source_target_pairs={{0,8},{1,9},{2,10},{3,11},{4,12},{5,13},{6,14},{7,15},{8,16},{9,17... | collective-permute-start | bytes 1769480 | tf_op jit(solution)/shard_map/ppermute | solution.py:33
  32.9 14.7 %collective-permute-start.6 = (bf16[576,512]{1,0:T(8,128)(2,1)S(1)}, bf16[576,512]{1,0:T(8,128)(2,1)S(1)}, u32[]{:S(2)}, u32[]{:S(2)}) collective-permute-start(bf16[576,512]{1,0:T(8,128)(2,1)S(1)} %dynamic-slice_bitcast_fusion), channel_id=1, source_target_pairs={{0,24},{1,25},{2,26},{3,27},{4,28},{5,29},{6,30},{7,31},{8,0},{9,1... | collective-permute-start | bytes 1769480 | tf_op jit(solution)/shard_map/ppermute | solution.py:33
  35.8 8.8 %collective-permute-start.7 = (bf16[256,640]{1,0:T(8,128)(2,1)S(1)}, bf16[256,640]{1,0:T(8,128)(2,1)S(1)}, u32[]{:S(2)}, u32[]{:S(2)}) collective-permute-start(bf16[256,640]{1,0:T(8,128)(2,1)S(1)} %bitcast.21), channel_id=1, source_target_pairs={{0,32},{1,33},{2,34},{3,35},{4,36},{5,37},{6,38},{7,39},{8,40},{9,... | collective-permute-start | bytes 983048 | tf_op jit(solution)/shard_map/ppermute | solution.py:33
  52.2 15.0 %collective-permute-start.10 = (bf16[576,512]{1,0:T(8,128)(2,1)S(1)}, bf16[576,512]{1,0:T(8,128)(2,1)S(1)}, u32[]{:S(2)}, u32[]{:S(2)}) collective-permute-start(bf16[576,512]{1,0:T(8,128)(2,1)S(1)} %dynamic-slice_bitcast_fusion), channel_id=1, source_target_pairs={{0,16},{1,17},{2,18},{3,19},{4,20},{5,21},{6,22},{7,23},{8,24},{9,... | collective-permute-start | bytes 1769480 | tf_op jit(solution)/shard_map/ppermute | solution.py:33
  54.1 13.1 %collective-permute-start.8 = (bf16[32,7296]{1,0:T(8,128)(2,1)S(1)}, bf16[32,7296]{1,0:T(8,128)(2,1)S(1)}, u32[]{:S(2)}, u32[]{:S(2)}) collective-permute-start(bf16[32,7296]{1,0:T(8,128)(2,1)S(1)} %slice.18), channel_id=1, source_target_pairs={{0,2},{1,3},{2,4},{3,5},{4,6},{5,7},{6,0},{7,1},{8,10},{9,11},{10,... | collective-permute-start | bytes 1400840 | tf_op jit(solution)/shard_map/ppermute | solution.py:33
  55.3 11.8 %collective-permute-start.9 = (bf16[32,7296]{1,0:T(8,128)(2,1)S(1)}, bf16[32,7296]{1,0:T(8,128)(2,1)S(1)}, u32[]{:S(2)}, u32[]{:S(2)}) collective-permute-start(bf16[32,7296]{1,0:T(8,128)(2,1)S(1)} %slice.19), channel_id=1, source_target_pairs={{0,6},{1,7},{2,0},{3,1},{4,2},{5,3},{6,4},{7,5},{8,14},{9,15},{10,... | collective-permute-start | bytes 1400840 | tf_op jit(solution)/shard_map/ppermute | solution.py:33
  57.5 8.3 %collective-permute-start.11 = (bf16[256,640]{1,0:T(8,128)(2,1)S(1)}, bf16[256,640]{1,0:T(8,128)(2,1)S(1)}, u32[]{:S(2)}, u32[]{:S(2)}) collective-permute-start(bf16[256,640]{1,0:T(8,128)(2,1)S(1)} %bitcast.22), channel_id=1, source_target_pairs={{0,96},{1,97},{2,98},{3,99},{4,100},{5,101},{6,102},{7,103},{8,104... | collective-permute-start | bytes 983048 | tf_op jit(solution)/shard_map/ppermute | solution.py:33
  69.1 15.6 %collective-permute-start.14 = (bf16[1728,512]{1,0:T(8,128)(2,1)}, bf16[1728,512]{1,0:T(8,128)(2,1)}, u32[]{:S(2)}, u32[]{:S(2)}) collective-permute-start(bf16[1728,512]{1,0:T(8,128)(2,1)} %constant_dynamic-update-slice_fusion), channel_id=1, source_target_pairs={{0,1},{1,0},{2,3},{3,2},{4,5},{5,4},{6,7},{7,6},{8,9},{9,8},{10,11... | collective-permute-start | bytes 5308424 | tf_op jit(solution)/shard_map/ppermute | solution.py:33
  77.8 17.2 %collective-permute-start.12 = (bf16[32,7168]{1,0:T(8,128)(2,1)}, bf16[32,7168]{1,0:T(8,128)(2,1)S(1)}, u32[]{:S(2)}, u32[]{:S(2)}) collective-permute-start(bf16[32,7168]{1,0:T(8,128)(2,1)} %get-tuple-element.63), channel_id=1, source_target_pairs={{0,6},{1,7},{2,0},{3,1},{4,2},{5,3},{6,4},{7,5},{8,14},{9,15},{10,... | collective-permute-start | bytes 1376264 | tf_op jit(solution)/shard_map/ppermute | solution.py:33
  80.9 14.1 %collective-permute-start.13 = (bf16[32,7168]{1,0:T(8,128)(2,1)}, bf16[32,7168]{1,0:T(8,128)(2,1)S(1)}, u32[]{:S(2)}, u32[]{:S(2)}) collective-permute-start(bf16[32,7168]{1,0:T(8,128)(2,1)} %get-tuple-element.64), channel_id=1, source_target_pairs={{0,2},{1,3},{2,4},{3,5},{4,6},{5,7},{6,0},{7,1},{8,10},{9,11},{10,... | collective-permute-start | bytes 1376264 | tf_op jit(solution)/shard_map/ppermute | solution.py:33
  80.9 14.5 %collective-permute-start.15 = (bf16[256,640]{1,0:T(8,128)(2,1)S(1)}, bf16[256,640]{1,0:T(8,128)(2,1)S(1)}, u32[]{:S(2)}, u32[]{:S(2)}) collective-permute-start(bf16[256,640]{1,0:T(8,128)(2,1)S(1)} %bitcast.23), channel_id=1, source_target_pairs={{0,64},{1,65},{2,66},{3,67},{4,68},{5,69},{6,70},{7,71},{8,72},{9,... | collective-permute-start | bytes 983048 | tf_op jit(solution)/shard_map/ppermute | solution.py:33
  95.4 22.7 %collective-permute-start.16 = (bf16[64,7168]{1,0:T(8,128)(2,1)S(1)}, bf16[64,7168]{1,0:T(8,128)(2,1)S(1)}, u32[]{:S(2)}, u32[]{:S(2)}) collective-permute-start(bf16[64,7168]{1,0:T(8,128)(2,1)S(1)} %pad_maximum_fusion), channel_id=1, source_target_pairs={{0,6},{1,7},{2,0},{3,1},{4,2},{5,3},{6,4},{7,5},{8,14},{9,15},{10,... | collective-permute-start | bytes 2752520 | tf_op jit(solution)/shard_map/ppermute | solution.py:33
  98.8 22.8 %collective-permute-start.17 = (bf16[64,7168]{1,0:T(8,128)(2,1)S(1)}, bf16[64,7168]{1,0:T(8,128)(2,1)S(1)}, u32[]{:S(2)}, u32[]{:S(2)}) collective-permute-start(bf16[64,7168]{1,0:T(8,128)(2,1)S(1)} %pad_maximum_fusion.1), channel_id=1, source_target_pairs={{0,2},{1,3},{2,4},{3,5},{4,6},{5,7},{6,0},{7,1},{8,10},{9,11},{10,... | collective-permute-start | bytes 2752520 | tf_op jit(solution)/shard_map/ppermute | solution.py:33
  98.8 14.1 %collective-permute-start.18 = (bf16[256,640]{1,0:T(8,128)(2,1)S(1)}, bf16[256,640]{1,0:T(8,128)(2,1)S(1)}, u32[]{:S(2)}, u32[]{:S(2)}) collective-permute-start(bf16[256,640]{1,0:T(8,128)(2,1)S(1)} %copy-done.17), channel_id=1, source_target_pairs={{0,96},{1,97},{2,98},{3,99},{4,100},{5,101},{6,102},{7,103},{8,104... | collective-permute-start | bytes 983048 | tf_op jit(solution)/shard_map/ppermute | solution.py:33
  100.6 12.2 %collective-permute-start.19 = (bf16[256,640]{1,0:T(8,128)(2,1)S(1)}, bf16[256,640]{1,0:T(8,128)(2,1)S(1)}, u32[]{:S(2)}, u32[]{:S(2)}) collective-permute-start(bf16[256,640]{1,0:T(8,128)(2,1)S(1)} %copy-done.15), channel_id=1, source_target_pairs={{0,32},{1,33},{2,34},{3,35},{4,36},{5,37},{6,38},{7,39},{8,40},{9,... | collective-permute-start | bytes 983048 | tf_op jit(solution)/shard_map/ppermute | solution.py:33
  110.9 10.7 %collective-permute-start.20 = (bf16[256,640]{1,0:T(8,128)(2,1)}, bf16[256,640]{1,0:T(8,128)(2,1)S(1)}, u32[]{:S(2)}, u32[]{:S(2)}) collective-permute-start(bf16[256,640]{1,0:T(8,128)(2,1)} %get-tuple-element.86), channel_id=1, source_target_pairs={{0,64},{1,65},{2,66},{3,67},{4,68},{5,69},{6,70},{7,71},{8,72},{9,... | collective-permute-start | bytes 983048 | tf_op jit(solution)/shard_map/ppermute | solution.py:33
  123.6 20.2 %all-to-all-start.1 = ((bf16[16,4,7168]{2,1,0:T(4,128)(2,1)}), bf16[16,4,7168]{2,1,0:T(4,128)(2,1)S(1)}, u32[]{:S(2)}, u32[]{:S(2)}) async-start(bf16[16,4,7168]{2,1,0:T(4,128)(2,1)} %reshape.33), calls=%async_computation.1 | async-start | bytes 1835008 | tf_op jit(solution)/shard_map/all_to_all | solution.py:309
  (18 other events, 213.0 us)

commit v4 on v3

--- a/solution.py
+++ b/solution.py
@@ -1,3 +1,4 @@
+import functools
 import math
 
 import jax
@@ -12,7 +13,7 @@
 QW = 640
 D = 7168
 XW = D + 128
-KC = 2560
+KC = 1792
 SCALE2 = 192.0 ** (-0.5) * math.log2(math.e)
 AXES = ("seq", "exp")
 bf16 = jnp.bfloat16
@@ -49,8 +50,8 @@
 
 
 def attend_kernel(core_ref, *refs):
-    qs, own, near, far, outs = refs[0:2], refs[2], refs[3], refs[4], refs[5:7]
-    q_ref, k_ref, s_ref, o_ref, sems = refs[7:12]
+    qs, own, near, far, outs = refs[0:2], refs[2], refs[3:6], refs[6:8], refs[8:10]
+    q_ref, k_ref, s_ref, o_ref, sems = refs[10:15]
     core = core_ref[0]
     coref = core.astype(f32)
     cps = []
@@ -58,56 +59,62 @@
     def load(src, dst):
         cps.append(pltpu.make_async_copy(src, dst, sems.at[len(cps) + 2]))
 
-    load(qs[0], q_ref.at[0])
-    load(qs[1], q_ref.at[1])
-    for g, (mine, got) in enumerate(((own.at[core], near), (own.at[1 - core], far))):
-        load(mine, k_ref.at[g, 0])
-        load(got, k_ref.at[g, 1:4])
+    load(qs[0], q_ref.at[0:256])
+    load(qs[1], q_ref.at[256:512])
+    load(own.at[core], k_ref.at[0, 0])
+    for i in range(3):
+        load(near[i], k_ref.at[0, i + 1])
+    load(own.at[1 - core], k_ref.at[1, 0])
+    load(far[0], k_ref.at[1, 1:3])
+    load(far[1], k_ref.at[1, 3])
     for cp in cps:
         cp.start()
-    for cp in cps:
-        cp.wait()
-    lane = lax.broadcasted_iota(jnp.int32, (256, QW - LAT), 1)
+    cps[0].wait()
+    cps[1].wait()
+    needs = [(2, 6), (3, 7), (4,), (5, 8)]
+    lane = lax.broadcasted_iota(jnp.int32, (512, QW - LAT), 1)
     stores = []
-    for step in range(2):
-        q = q_ref[step, :, 0:KDIM]
-        is_a = q_ref[step, :, KDIM : KDIM + 1].astype(f32) == coref
-        best = []
-        for g in range(2):
-            m = None
-            for t in range(4):
-                s = jnp.dot(q, k_ref[g, t], preferred_element_type=f32)
-                s_ref[g * 4 + t] = s
-                ms = jnp.max(s, axis=1, keepdims=True)
-                m = ms if m is None else jnp.maximum(m, ms)
-            best.append(m)
-        mu = jnp.where(is_a, best[0], best[1]) * SCALE2
-        hi = mu.astype(bf16).astype(f32)
-        lo = (mu - hi).astype(bf16).astype(f32)
-        top = hi + lo
-        total = jnp.zeros((256, 1), f32)
-        acc = jnp.zeros((256, LAT), f32)
-        for g in range(2):
-            off = jnp.where(is_a if g == 0 else jnp.logical_not(is_a), -top, -1e30)
-            for t in range(4):
-                w = jnp.exp2(s_ref[g * 4 + t] * SCALE2 + off).astype(bf16)
-                total = total + jnp.sum(w.astype(f32), axis=1, keepdims=True)
-                acc = acc + lax.dot_general(
-                    w,
-                    k_ref[g, t, 0:LAT, :],
-                    (((1,), (1,)), ((), ())),
-                    preferred_element_type=f32,
-                )
-        o_ref[step, :, 0:LAT] = acc.astype(bf16)
-        l_hi = total.astype(bf16).astype(f32)
-        l_lo = total - l_hi
-        tail = jnp.where(
-            lane == 0,
-            hi,
-            jnp.where(lane == 1, lo, jnp.where(lane == 2, l_hi, jnp.where(lane == 3, l_lo, 0.0))),
-        )
-        o_ref[step, :, LAT:QW] = tail.astype(bf16)
-        cp = pltpu.make_async_copy(o_ref.at[step], outs[step], sems.at[step])
+    q = q_ref[:, 0:KDIM]
+    is_a = q_ref[:, KDIM : KDIM + 1].astype(f32) == coref
+    in_a = jnp.where(is_a, 1.0, 0.0).astype(bf16)
+    in_b = jnp.where(is_a, 0.0, 1.0).astype(bf16)
+    best = None
+    for t in range(4):
+        for i in needs[t]:
+            cps[i].wait()
+        sa = jnp.dot(q, k_ref[0, t], preferred_element_type=f32)
+        sb = jnp.dot(q, k_ref[1, t], preferred_element_type=f32)
+        s = jnp.where(is_a, sa, sb)
+        s_ref[t] = s
+        m = jnp.max(s, axis=1, keepdims=True)
+        best = m if best is None else jnp.maximum(best, m)
+    mu = best * SCALE2
+    hi = mu.astype(bf16).astype(f32)
+    lo = (mu - hi).astype(bf16).astype(f32)
+    top = hi + lo
+    total = jnp.zeros((512, 1), f32)
+    acc = jnp.zeros((512, LAT), f32)
+    for t in range(4):
+        w = jnp.exp2(s_ref[t] * SCALE2 - top).astype(bf16)
+        total = total + jnp.sum(w.astype(f32), axis=1, keepdims=True)
+        for g, mask in enumerate((in_a, in_b)):
+            acc = acc + lax.dot_general(
+                w * mask,
+                k_ref[g, t, 0:LAT, :],
+                (((1,), (1,)), ((), ())),
+                preferred_element_type=f32,
+            )
+    o_ref[:, 0:LAT] = acc.astype(bf16)
+    l_hi = total.astype(bf16).astype(f32)
+    l_lo = total - l_hi
+    tail = jnp.where(
+        lane == 0,
+        hi,
+        jnp.where(lane == 1, lo, jnp.where(lane == 2, l_hi, jnp.where(lane == 3, l_lo, 0.0))),
+    )
+    o_ref[:, LAT:QW] = tail.astype(bf16)
+    for i in range(2):
+        cp = pltpu.make_async_copy(o_ref.at[i * 256 : i * 256 + 256], outs[i], sems.at[i])
         cp.start()
         stores.append(cp)
     for cp in stores:
@@ -119,21 +126,21 @@
     return pl.pallas_call(
         attend_kernel,
         out_shape=[pltpu.HBM((256, QW), bf16)] * 2,
-        in_specs=[pl.BlockSpec(memory_space=pltpu.SMEM)] + [hbm] * 5,
+        in_specs=[pl.BlockSpec(memory_space=pltpu.SMEM)] + [hbm] * 8,
         out_specs=[hbm] * 2,
         scratch_shapes=[
-            pltpu.VMEM((2, 256, QW), bf16),
+            pltpu.VMEM((512, QW), bf16),
             pltpu.VMEM((2, 4, KDIM, 512), bf16),
-            pltpu.VMEM((8, 256, 512), f32),
-            pltpu.VMEM((2, 256, QW), bf16),
-            pltpu.SemaphoreType.DMA((8,)),
+            pltpu.VMEM((4, 512, 512), f32),
+            pltpu.VMEM((512, QW), bf16),
+            pltpu.SemaphoreType.DMA((11,)),
         ],
         compiler_params=pltpu.CompilerParams(vmem_limit_bytes=40 << 20),
         cost_estimate=pl.CostEstimate(
             flops=4_500_000_000, transcendentals=2_000_000, bytes_accessed=6_000_000
         ),
         name="attend",
-    )(core, *in_hbm(*qs, own, near.reshape(3, KDIM, 512), far.reshape(3, KDIM, 512)))
+    )(core, *in_hbm(*qs, own, *near, *far))
 
 
 def merge_kernel(q_ref, lat_ref, *refs):
@@ -168,9 +175,17 @@
     )(q, lat, *parts)
 
 
-def expert_kernel(e_ref, *refs):
-    xs, (wg, wu, wd, wg2, wu2, wd2), outs = refs[0:5], refs[5:11], refs[11:16]
-    x_ref, w_ref, d_ref, acc_ref, o_ref, sems = refs[16:22]
+def expert_kernel(e_ref, *refs, count_x, fresh):
+    xs, refs = refs[:count_x], refs[count_x:]
+    if fresh:
+        (wg, wu, wd, wg2, wu2, wd2), refs = refs[:6], refs[6:]
+    else:
+        (w_ref, d_ref), refs = refs[:2], refs[2:]
+    outs, refs = refs[:count_x], refs[count_x:]
+    if fresh:
+        (w_ref, d_ref), refs = refs[:2], refs[2:]
+    x_ref, acc_ref, o_ref, sems = refs
+    height = x_ref.shape[0]
     bounds = [(k, min(k + KC, D)) for k in range(0, D, KC)]
     count = [0]
 
@@ -183,15 +198,18 @@
     steps = []
     for k0, k1 in bounds:
         cps = []
-        for j, w in enumerate((wg, wu, wg2, wu2)):
-            cps.append(copy(w.at[k0:k1, :], w_ref.at[k0:k1, j * 128 : j * 128 + 128]))
+        if fresh:
+            for j, w in enumerate((wg, wu, wg2, wu2)):
+                cps.append(copy(w.at[k0:k1, :], w_ref.at[k0:k1, j * 128 : j * 128 + 128]))
         end = XW if k1 == D else k1
         r = 0
         for x in xs:
             cps.append(copy(x.at[:, k0:end], x_ref.at[r : r + x.shape[0], k0:end]))
             r += x.shape[0]
         steps.append(cps)
-    down = [copy(wd, d_ref.at[0:128, :]), copy(wd2, d_ref.at[128:256, :])]
+    down = []
+    if fresh:
+        down = [copy(wd, d_ref.at[0:128, :]), copy(wd2, d_ref.at[128:256, :])]
     for i, (k0, k1) in enumerate(bounds):
         for cp in steps[i]:
             cp.wait()
@@ -201,7 +219,7 @@
         else:
             acc_ref[...] += part
     gates = x_ref[:, D:XW].astype(f32)
-    lane = lax.broadcasted_iota(jnp.int32, (256, 128), 1)
+    lane = lax.broadcasted_iota(jnp.int32, (height, 128), 1)
     halves = []
     for j in range(2):
         e = e_ref[j]
@@ -227,27 +245,37 @@
         cp.wait()
 
 
-def experts(e, xs, weights):
+def experts(e, xs, weights, fresh):
     hbm = pl.BlockSpec(memory_space=pltpu.HBM)
+    vmem = pl.BlockSpec(memory_space=pltpu.VMEM)
+    height = sum(x.shape[0] for x in xs)
+    out_shape = [pltpu.HBM((x.shape[0], D), bf16) for x in xs]
+    if fresh:
+        out_shape += [pltpu.VMEM((D, 512), bf16), pltpu.VMEM((256, D), bf16)]
+        weights = in_hbm(*weights)
+    else:
+        weights = [pltpu.with_memory_space_constraint(w, pltpu.VMEM) for w in weights]
     return pl.pallas_call(
-        expert_kernel,
-        out_shape=[pltpu.HBM((n, D), bf16) for n in (64, 64, 32, 32, 64)],
-        in_specs=[pl.BlockSpec(memory_space=pltpu.SMEM)] + [hbm] * 11,
-        out_specs=[hbm] * 5,
+        functools.partial(expert_kernel, count_x=len(xs), fresh=fresh),
+        out_shape=out_shape,
+        in_specs=[pl.BlockSpec(memory_space=pltpu.SMEM)]
+        + [hbm] * len(xs)
+        + [hbm if fresh else vmem] * len(weights),
+        out_specs=[hbm] * len(xs) + [vmem, vmem] * fresh,
         scratch_shapes=[
-            pltpu.VMEM((256, XW), bf16),
-            pltpu.VMEM((D, 512), bf16),
-            pltpu.VMEM((256, D), bf16),
-            pltpu.VMEM((256, 512), f32),
-            pltpu.VMEM((256, D), bf16),
+            pltpu.VMEM((height, XW), bf16),
+            pltpu.VMEM((height, 512), f32),
+            pltpu.VMEM((height, D), bf16),
             pltpu.SemaphoreType.DMA((72,)),
         ],
-        compiler_params=pltpu.CompilerParams(vmem_limit_bytes=48 << 20),
+        compiler_params=pltpu.CompilerParams(vmem_limit_bytes=32 << 20),
         cost_estimate=pl.CostEstimate(
-            flops=3_000_000_000, transcendentals=65_536, bytes_accessed=18_000_000
+            flops=11_000_000 * height,
+            transcendentals=256 * height,
+            bytes_accessed=11_000_000 * fresh + 30_000 * height,
         ),
         name="experts",
-    )(e, *in_hbm(*xs, *weights))
+    )(e, *in_hbm(*xs), *weights)
 
 
 def body(
@@ -285,19 +313,23 @@
 
     z1, z3 = shift(rows, "z", 1), shift(rows, "z", 3)
     k1, k3, q1 = shift(half, "x", 1), shift(half, "x", 3), shift(query, "y", 1)
-    z1, z3, k1, k3, q1, half, query = after(z1, z3, k1, k3, q1, half, query)
-    xs = [rows, z1, shift(z1[:32], "z", 1), shift(z3[32:], "z", 3), z3]
+    k1, k3, q1, half, query = after(k1, k3, q1, half, query)
+    mine = [rows, z1, z3]
+    last = [shift(z1[:32], "z", 1), shift(z3[32:], "z", 3)]
     k2, q3, q2 = shift(half, "x", 2), shift(query, "y", 3), shift(query, "y", 2)
-    xs, k2, q3 = after(xs, k2, q3)
-    near = jnp.concatenate([k1, k2, k3], axis=0)
-    far = shift(near, "c", 1)
-
-    out0, out1, low, high, out3 = experts(jnp.stack([place, place ^ 1]), xs, weights)
+    far = shift(jnp.stack([k1, k3]), "c", 1)
+    near = [k1, k3, k2]
+    numbers = jnp.stack([place, place ^ 1])
+    *mine, w_all, d_all = experts(numbers, mine, weights, True)
+    last, mine, k2, q3, far = after(last, mine, k2, q3, far)
+    far = [far, shift(k2, "c", 1)]
+    out0, out1, out3 = mine
+    low, high = experts(numbers, last, [w_all, d_all], False)
     low, high = shift(low, "z", -1), shift(high, "z", 1)
     p1, p3 = attend(core[None], (q1, q3), keys, near, far)
     low, high, p1, p3 = after(low, high, p1, p3)
-    s1 = jnp.concatenate([add(out1[:32], low), out1[32:]], axis=0)
-    s3 = jnp.concatenate([out3[:32], add(out3[32:], high)], axis=0)
+    s1 = add(out1, jnp.pad(low, ((0, 32), (0, 0))))
+    s3 = add(out3, jnp.pad(high, ((32, 0), (0, 0))))
     s1, s3, q2, again = after(s1, s3, q2, query)
     r1, r3 = shift(s1, "z", -1), shift(s3, "z", 1)
     v1, v3 = shift(p1, "y", -1), shift(p3, "y", 1)

time: 145 us -> 138 us (0.952)
  waiting for transfers between devices: 59.1 us -> 52.8 us
  Pallas kernels: 32.1 us -> 36.3 us
  starting transfers between devices: 39.7 us -> 36.5 us
  local copies, waits for them, and re-layouts: 10.2 us -> 7.59 us
    ppermute x21 -> x22, waiting for transfers between devices: 32.8 us -> 26.4 us  [shift(): return lax.ppermute(a, AXES, pairs)]
    pallas_call x1 -> x2, Pallas kernels: 8.63 us -> 13.2 us  [experts(): pl.pallas_call(functools.partial(expert_kernel, count_x=len(xs), fresh=fr...]
    ppermute x21 -> x22, starting transfers between devices: 26.5 us -> 24.3 us  [shift(): return lax.ppermute(a, AXES, pairs)]
  transfers between devices with their start and end apart: 23 -> 24, of which waited for: 10 -> 8; matrix products, arithmetic and copies ran while one was open for 6% -> 5% of each run, Pallas kernels for 22% -> 26%
where the time goes in v4:
time: 138 us
  waiting for transfers between devices  52.8 us (38%)
  starting transfers between devices  36.5 us (26%)
  Pallas kernels  36.3 us (26%)
  local copies, waits for them, and re-layouts  7.59 us (6%)
  other arithmetic  3.78 us (3%)
    ppermute x22, waiting for transfers between devices, shift(): return lax.ppermute(a, AXES, pairs)  26.4 us
    ppermute x22, starting transfers between devices, shift(): return lax.ppermute(a, AXES, pairs)  24.3 us
    pallas_call x2, Pallas kernels, attend(): pl.pallas_call(attend_kernel, out_shape=[pltpu.HBM((256, QW), bf16)] * 2,...  20.1 us
    all_to_all x1, waiting for transfers between devices, body(): lax.all_to_all(jnp.broadcast_to(row[None], (16, 4, XW)), 'seq', 0, 0, til...  15.6 us
    pallas_call x2, Pallas kernels, experts(): pl.pallas_call(functools.partial(expert_kernel, count_x=len(xs), fresh=fr...  13.2 us
    all_to_all x1, waiting for transfers between devices, body(): moe = lax.all_to_all(own, 'seq', 0, 0, tiled=True)  10.8 us
    all_to_all x1, starting transfers between devices, body(): lax.all_to_all(jnp.broadcast_to(row[None], (16, 4, XW)), 'seq', 0, 0, til...  7.12 us
    all_to_all x1, starting transfers between devices, body(): moe = lax.all_to_all(own, 'seq', 0, 0, tiled=True)  5.17 us
  transfers between devices with their start and end apart: 24, of which 8 were waited for; matrix products, arithmetic and copies ran while one was open for 5% of the time, Pallas kernels for 26%

profile of v4, /device:TPU:0, one launch (start us, length us, event | category | flops | bytes accessed | tf_op | source)
XLA Modules:
  0.0 138.0 jit_solution(3152055838480732907)
XLA Ops:
  4.2 7.1 %all-to-all-start = ((bf16[16,4,7296]{2,1,0:T(4,128)(2,1)}), bf16[16,4,7296]{2,1,0:T(4,128)(2,1)S(1)}, u32[]{:S(2)}, u32[]{:S(2)}) async-start(bf16[16,4,7296]{2,1,0:T(4,128)(2,1)} %broadcast_in_dim.9), calls=%async_computation | async-start | bytes 1867776 | tf_op jit(solution)/shard_map/all_to_all | solution.py:301
  12.6 15.6 %all-to-all-done = bf16[16,4,7296]{2,1,0:T(4,128)(2,1)S(1)} async-done(((bf16[16,4,7296]{2,1,0:T(4,128)(2,1)}), bf16[16,4,7296]{2,1,0:T(4,128)(2,1)S(1)}, u32[]{:S(2)}, u32[]{:S(2)}) %all-to-all-start) | async-done | bytes 933920 | tf_op jit(solution)/shard_map/all_to_all | solution.py:301
  28.8 2.9 %collective-permute-start.4 = (bf16[576,512]{1,0:T(8,128)(2,1)}, bf16[576,512]{1,0:T(8,128)(2,1)S(1)}, u32[]{:S(2)}, u32[]{:S(2)}) collective-permute-start(bf16[576,512]{1,0:T(8,128)(2,1)} %dynamic-slice_bitcast_fusion), channel_id=1, source_target_pairs={{0,24},{1,25},{2,26},{3,27},{4,28},{5,29},{6,30},{7,31},{8,0},{9,1... | collective-permute-start | bytes 1769480 | tf_op jit(solution)/shard_map/ppermute | solution.py:34
  31.7 1.9 %collective-permute-start.6 = (bf16[64,7296]{1,0:T(8,128)(2,1)S(1)}, bf16[64,7296]{1,0:T(8,128)(2,1)S(1)}, u32[]{:S(2)}, u32[]{:S(2)}) collective-permute-start(bf16[64,7296]{1,0:T(8,128)(2,1)S(1)} %reshape.20.refs_0_), channel_id=1, source_target_pairs={{0,2},{1,3},{2,4},{3,5},{4,6},{5,7},{6,0},{7,1},{8,10},{9,11},{10,... | collective-permute-start | bytes 2801672 | tf_op jit(solution)/shard_map/ppermute | solution.py:34
  33.6 2.1 %collective-permute-start.8 = (bf16[64,7296]{1,0:T(8,128)(2,1)S(1)}, bf16[64,7296]{1,0:T(8,128)(2,1)S(1)}, u32[]{:S(2)}, u32[]{:S(2)}) collective-permute-start(bf16[64,7296]{1,0:T(8,128)(2,1)S(1)} %reshape.20.refs_0_), channel_id=1, source_target_pairs={{0,6},{1,7},{2,0},{3,1},{4,2},{5,3},{6,4},{7,5},{8,14},{9,15},{10,... | collective-permute-start | bytes 2801672 | tf_op jit(solution)/shard_map/ppermute | solution.py:34
  35.7 5.1 %collective-permute-done.5.refs_0_ = bf16[256,640]{1,0:T(8,128)(2,1)S(1)} collective-permute-done((bf16[256,640]{1,0:T(8,128)(2,1)S(1)}, bf16[256,640]{1,0:T(8,128)(2,1)S(1)}, u32[]{:S(2)}, u32[]{:S(2)}) %collective-permute-start.5) | collective-permute-done | bytes 327712 | tf_op jit(solution)/shard_map/ppermute | solution.py:34
  40.8 3.1 %collective-permute-done.3.refs_3_ = bf16[576,512]{1,0:T(8,128)(2,1)S(1)} collective-permute-done((bf16[576,512]{1,0:T(8,128)(2,1)}, bf16[576,512]{1,0:T(8,128)(2,1)S(1)}, u32[]{:S(2)}, u32[]{:S(2)}) %collective-permute-start.3) | collective-permute-done | bytes 589856 | tf_op jit(solution)/shard_map/ppermute | solution.py:34
  45.2 1.5 %collective-permute-start.10 = (bf16[576,512]{1,0:T(8,128)(2,1)}, bf16[576,512]{1,0:T(8,128)(2,1)}, u32[]{:S(2)}, u32[]{:S(2)}) collective-permute-start(bf16[576,512]{1,0:T(8,128)(2,1)} %dynamic-slice_bitcast_fusion), channel_id=1, source_target_pairs={{0,16},{1,17},{2,18},{3,19},{4,20},{5,21},{6,22},{7,23},{8,24},{9,... | collective-permute-start | bytes 1769480 | tf_op jit(solution)/shard_map/ppermute | solution.py:34
  46.7 8.2 %collective-permute-done.6.refs_1_ = bf16[64,7296]{1,0:T(8,128)(2,1)S(1)} collective-permute-done((bf16[64,7296]{1,0:T(8,128)(2,1)S(1)}, bf16[64,7296]{1,0:T(8,128)(2,1)S(1)}, u32[]{:S(2)}, u32[]{:S(2)}) %collective-permute-start.6) | collective-permute-done | bytes 933920 | tf_op jit(solution)/shard_map/ppermute | solution.py:34
  56.6 3.3 %collective-permute-start.9 = (bf16[32,7296]{1,0:T(8,128)(2,1)}, bf16[32,7296]{1,0:T(8,128)(2,1)}, u32[]{:S(2)}, u32[]{:S(2)}) collective-permute-start(bf16[32,7296]{1,0:T(8,128)(2,1)} %slice.9), channel_id=1, source_target_pairs={{0,6},{1,7},{2,0},{3,1},{4,2},{5,3},{6,4},{7,5},{8,14},{9,15},{10,... | collective-permute-start | bytes 1400840 | tf_op jit(solution)/shard_map/ppermute | solution.py:34
  59.9 3.0 %collective-permute-start.11 = (bf16[256,640]{1,0:T(8,128)(2,1)S(1)}, bf16[256,640]{1,0:T(8,128)(2,1)S(1)}, u32[]{:S(2)}, u32[]{:S(2)}) collective-permute-start(bf16[256,640]{1,0:T(8,128)(2,1)S(1)} %bitcast.22), channel_id=1, source_target_pairs={{0,96},{1,97},{2,98},{3,99},{4,100},{5,101},{6,102},{7,103},{8,104... | collective-permute-start | bytes 983048 | tf_op jit(solution)/shard_map/ppermute | solution.py:34
  62.9 8.1 %experts.2 = (bf16[64,7168]{1,0:T(8,128)(2,1)}, bf16[64,7168]{1,0:T(8,128)(2,1)}, bf16[64,7168]{1,0:T(8,128)(2,1)}, bf16[7168,512]{1,0:T(8,128)(2,1)S(1)}, bf16[256,7168]{1,0:T(8,128)(2,1)S(1)}) custom-call(s32[2]{0:T(128)S(1)} %pad_add_fusion.e_ref, bf16[64,7296]{1,0:T(8,128)(2,1)} %copy-done, bf16[64,7296]{1,0:T(8,128)(2,1)} %copy-done.1, ...), custom_call_target="tpu_custom_call" | custom-call | flops 2112000000 | bytes 16760000 | tf_op jit(solution)/shard_map/experts/pallas_call | solution.py:258
  71.3 5.0 %experts.3 = (bf16[32,7168]{1,0:T(8,128)(2,1)}, bf16[32,7168]{1,0:T(8,128)(2,1)}) custom-call(s32[2]{0:T(128)S(1)} %pad_add_fusion.e_ref, bf16[32,7296]{1,0:T(8,128)(2,1)} %collective-permute-done.7.refs_0_, bf16[32,7296]{1,0:T(8,128)(2,1)} %collective-permute-done.9.refs_1_, bf16[7168,512]{1,0:T(8,128)(2,1)S(1)} %get-tuple-element.64.refs_2_, ...), custom_call_target="tpu_custom_call" | custom-call | flops 704000000 | bytes 1920000 | tf_op jit(solution)/shard_map/experts/pallas_call | solution.py:258
  76.9 1.5 %collective-permute-start.14 = (bf16[32,7168]{1,0:T(8,128)(2,1)}, bf16[32,7168]{1,0:T(8,128)(2,1)S(1)}, u32[]{:S(2)}, u32[]{:S(2)}) collective-permute-start(bf16[32,7168]{1,0:T(8,128)(2,1)} %get-tuple-element.67), channel_id=1, source_target_pairs={{0,2},{1,3},{2,4},{3,5},{4,6},{5,7},{6,0},{7,1},{8,10},{9,11},{10,... | collective-permute-start | bytes 1376264 | tf_op jit(solution)/shard_map/ppermute | solution.py:34
  79.4 10.1 %attend.2 = (bf16[256,640]{1,0:T(8,128)(2,1)}, bf16[256,640]{1,0:T(8,128)(2,1)}) custom-call(s32[1]{0:T(128)} %bitcast.10.core_ref, bf16[256,640]{1,0:T(8,128)(2,1)} %copy-done.15, bf16[256,640]{1,0:T(8,128)(2,1)} %copy-done.16, bf16[2,576,512]{2,1,0:T(8,128)(2,1)} %bitcast.28, bf16[576,512]{1,0:T(8,128)(2,1)} %copy-done.7, bf16[576,512]{1,0:T(8,128)(2,1)} %copy-done.8, ...), custom_call_target="tpu_custom_call" | custom-call | flops 4499999744 | bytes 6000000 | tf_op jit(solution)/shard_map/attend/pallas_call | solution.py:126
  91.2 1.9 %collective-permute-start.17 = (bf16[64,7168]{1,0:T(8,128)(2,1)S(1)}, bf16[64,7168]{1,0:T(8,128)(2,1)S(1)}, u32[]{:S(2)}, u32[]{:S(2)}) collective-permute-start(bf16[64,7168]{1,0:T(8,128)(2,1)S(1)} %get-tuple-element.77), channel_id=1, source_target_pairs={{0,6},{1,7},{2,0},{3,1},{4,2},{5,3},{6,4},{7,5},{8,14},{9,15},{10,... | collective-permute-start | bytes 2752520 | tf_op jit(solution)/shard_map/ppermute | solution.py:34
  93.3 2.4 %collective-permute-start.19 = (bf16[256,640]{1,0:T(8,128)(2,1)S(1)}, bf16[256,640]{1,0:T(8,128)(2,1)S(1)}, u32[]{:S(2)}, u32[]{:S(2)}) collective-permute-start(bf16[256,640]{1,0:T(8,128)(2,1)S(1)} %copy-done.19), channel_id=1, source_target_pairs={{0,96},{1,97},{2,98},{3,99},{4,100},{5,101},{6,102},{7,103},{8,104... | collective-permute-start | bytes 983048 | tf_op jit(solution)/shard_map/ppermute | solution.py:34
  95.8 10.0 %attend.3 = (bf16[256,640]{1,0:T(8,128)(2,1)}, bf16[256,640]{1,0:T(8,128)(2,1)}) custom-call(s32[1]{0:T(128)} %bitcast.10.core_ref, bf16[256,640]{1,0:T(8,128)(2,1)} %copy-done.18, bf16[256,640]{1,0:T(8,128)(2,1)} %bitcast.24, bf16[2,576,512]{2,1,0:T(8,128)(2,1)} %bitcast.29, bf16[576,512]{1,0:T(8,128)(2,1)} %copy-done.7, bf16[576,512]{1,0:T(8,128)(2,1)} %copy-done.8, ...), custom_call_target="tpu_custom_call" | custom-call | flops 4499999744 | bytes 6000000 | tf_op jit(solution)/shard_map/attend/pallas_call | solution.py:126
  105.8 1.6 %collective-permute-start.21 = (bf16[256,640]{1,0:T(8,128)(2,1)}, bf16[256,640]{1,0:T(8,128)(2,1)S(1)}, u32[]{:S(2)}, u32[]{:S(2)}) collective-permute-start(bf16[256,640]{1,0:T(8,128)(2,1)} %get-tuple-element.88), channel_id=1, source_target_pairs={{0,64},{1,65},{2,66},{3,67},{4,68},{5,69},{6,70},{7,71},{8,72},{9,... | collective-permute-start | bytes 983048 | tf_op jit(solution)/shard_map/ppermute | solution.py:34
  107.4 5.5 %collective-permute-done.17 = bf16[64,7168]{1,0:T(8,128)(2,1)S(1)} collective-permute-done((bf16[64,7168]{1,0:T(8,128)(2,1)S(1)}, bf16[64,7168]{1,0:T(8,128)(2,1)S(1)}, u32[]{:S(2)}, u32[]{:S(2)}) %collective-permute-start.17) | collective-permute-done | bytes 917536 | tf_op jit(solution)/shard_map/ppermute | solution.py:34
  113.0 3.0 %collective-permute-done.18 = bf16[64,7168]{1,0:T(8,128)(2,1)S(1)} collective-permute-done((bf16[64,7168]{1,0:T(8,128)(2,1)S(1)}, bf16[64,7168]{1,0:T(8,128)(2,1)S(1)}, u32[]{:S(2)}, u32[]{:S(2)}) %collective-permute-start.18) | collective-permute-done | bytes 917536 | tf_op jit(solution)/shard_map/ppermute | solution.py:34
  118.0 5.2 %all-to-all-start.1 = ((bf16[16,4,7168]{2,1,0:T(4,128)(2,1)}), bf16[16,4,7168]{2,1,0:T(4,128)(2,1)S(1)}, u32[]{:S(2)}, u32[]{:S(2)}) async-start(bf16[16,4,7168]{2,1,0:T(4,128)(2,1)} %reshape.23), calls=%async_computation.1 | async-start | bytes 1835008 | tf_op jit(solution)/shard_map/all_to_all | solution.py:341
  123.2 3.0 %merge.1 = bf16[256,512]{1,0:T(8,128)(2,1)} custom-call(bf16[256,640]{1,0:T(8,128)(2,1)} %bitcast.25, bf16[4,576]{1,0:T(4,128)(2,1)} %lat_ref.1, bf16[256,640]{1,0:T(8,128)(2,1)} %get-tuple-element.84.refs_0_, bf16[256,640]{1,0:T(8,128)(2,1)} %copy-done.9, bf16[256,640]{1,0:T(8,128)(2,1)} %copy-done.11, bf16[256,640]{1,0:T(8,128)(2,1)} %copy-done.10), custom_call_target="tpu_custom_call" | custom-call | tf_op jit(solution)/shard_map/merge/pallas_call | solution.py:169
  126.2 10.8 %all-to-all-done.1 = bf16[16,4,7168]{2,1,0:T(4,128)(2,1)S(1)} async-done(((bf16[16,4,7168]{2,1,0:T(4,128)(2,1)}), bf16[16,4,7168]{2,1,0:T(4,128)(2,1)S(1)}, u32[]{:S(2)}, u32[]{:S(2)}) %all-to-all-start.1) | async-done | bytes 917536 | tf_op jit(solution)/shard_map/all_to_all | solution.py:341
  (89 shorter events, 15.0 us)
Async XLA Ops:
  0.7 27.7 %collective-permute-start = (bf16[7168,128]{1,0:T(8,128)(2,1)}, bf16[7168,128]{1,0:T(8,128)(2,1)}, u32[]{:S(2)}, u32[]{:S(2)}) collective-permute-start(bf16[7168,128]{1,0:T(8,128)(2,1)} %bitcast.15), channel_id=1, source_target_pairs={{0,1},{1,0},{2,3},{3,2},{4,5},{5,4},{6,7},{7,6},{8,9},{9,8},{10,11... | collective-permute-start | bytes 5505032 | tf_op jit(solution)/shard_map/ppermute | solution.py:34
  0.7 27.6 %collective-permute-start.1 = (bf16[7168,128]{1,0:T(8,128)(2,1)}, bf16[7168,128]{1,0:T(8,128)(2,1)}, u32[]{:S(2)}, u32[]{:S(2)}) collective-permute-start(bf16[7168,128]{1,0:T(8,128)(2,1)} %bitcast.17), channel_id=1, source_target_pairs={{0,1},{1,0},{2,3},{3,2},{4,5},{5,4},{6,7},{7,6},{8,9},{9,8},{10,11... | collective-permute-start | bytes 5505032 | tf_op jit(solution)/shard_map/ppermute | solution.py:34
  1.2 27.1 %collective-permute-start.2 = (bf16[128,7168]{1,0:T(8,128)(2,1)}, bf16[128,7168]{1,0:T(8,128)(2,1)}, u32[]{:S(2)}, u32[]{:S(2)}) collective-permute-start(bf16[128,7168]{1,0:T(8,128)(2,1)} %bitcast.19), channel_id=1, source_target_pairs={{0,1},{1,0},{2,3},{3,2},{4,5},{5,4},{6,7},{7,6},{8,9},{9,8},{10,11... | collective-permute-start | bytes 5505032 | tf_op jit(solution)/shard_map/ppermute | solution.py:34
  4.2 23.9 %all-to-all-start = ((bf16[16,4,7296]{2,1,0:T(4,128)(2,1)}), bf16[16,4,7296]{2,1,0:T(4,128)(2,1)S(1)}, u32[]{:S(2)}, u32[]{:S(2)}) async-start(bf16[16,4,7296]{2,1,0:T(4,128)(2,1)} %broadcast_in_dim.9), calls=%async_computation | async-start | bytes 1867776 | tf_op jit(solution)/shard_map/all_to_all | solution.py:301
  28.4 15.6 %collective-permute-start.3 = (bf16[576,512]{1,0:T(8,128)(2,1)}, bf16[576,512]{1,0:T(8,128)(2,1)S(1)}, u32[]{:S(2)}, u32[]{:S(2)}) collective-permute-start(bf16[576,512]{1,0:T(8,128)(2,1)} %dynamic-slice_bitcast_fusion), channel_id=1, source_target_pairs={{0,8},{1,9},{2,10},{3,11},{4,12},{5,13},{6,14},{7,15},{8,16},{9,17... | collective-permute-start | bytes 1769480 | tf_op jit(solution)/shard_map/ppermute | solution.py:34
  28.8 15.2 %collective-permute-start.4 = (bf16[576,512]{1,0:T(8,128)(2,1)}, bf16[576,512]{1,0:T(8,128)(2,1)S(1)}, u32[]{:S(2)}, u32[]{:S(2)}) collective-permute-start(bf16[576,512]{1,0:T(8,128)(2,1)} %dynamic-slice_bitcast_fusion), channel_id=1, source_target_pairs={{0,24},{1,25},{2,26},{3,27},{4,28},{5,29},{6,30},{7,31},{8,0},{9,1... | collective-permute-start | bytes 1769480 | tf_op jit(solution)/shard_map/ppermute | solution.py:34
  31.7 9.1 %collective-permute-start.5 = (bf16[256,640]{1,0:T(8,128)(2,1)S(1)}, bf16[256,640]{1,0:T(8,128)(2,1)S(1)}, u32[]{:S(2)}, u32[]{:S(2)}) collective-permute-start(bf16[256,640]{1,0:T(8,128)(2,1)S(1)} %bitcast.21), channel_id=1, source_target_pairs={{0,32},{1,33},{2,34},{3,35},{4,36},{5,37},{6,38},{7,39},{8,40},{9,... | collective-permute-start | bytes 983048 | tf_op jit(solution)/shard_map/ppermute | solution.py:34
  31.7 23.2 %collective-permute-start.6 = (bf16[64,7296]{1,0:T(8,128)(2,1)S(1)}, bf16[64,7296]{1,0:T(8,128)(2,1)S(1)}, u32[]{:S(2)}, u32[]{:S(2)}) collective-permute-start(bf16[64,7296]{1,0:T(8,128)(2,1)S(1)} %reshape.20.refs_0_), channel_id=1, source_target_pairs={{0,2},{1,3},{2,4},{3,5},{4,6},{5,7},{6,0},{7,1},{8,10},{9,11},{10,... | collective-permute-start | bytes 2801672 | tf_op jit(solution)/shard_map/ppermute | solution.py:34
  33.6 22.1 %collective-permute-start.8 = (bf16[64,7296]{1,0:T(8,128)(2,1)S(1)}, bf16[64,7296]{1,0:T(8,128)(2,1)S(1)}, u32[]{:S(2)}, u32[]{:S(2)}) collective-permute-start(bf16[64,7296]{1,0:T(8,128)(2,1)S(1)} %reshape.20.refs_0_), channel_id=1, source_target_pairs={{0,6},{1,7},{2,0},{3,1},{4,2},{5,3},{6,4},{7,5},{8,14},{9,15},{10,... | collective-permute-start | bytes 2801672 | tf_op jit(solution)/shard_map/ppermute | solution.py:34
  45.2 25.9 %collective-permute-start.12 = (bf16[2,576,512]{2,1,0:T(8,128)(2,1)}, bf16[2,576,512]{2,1,0:T(8,128)(2,1)}, u32[]{:S(2)}, u32[]{:S(2)}) collective-permute-start(bf16[2,576,512]{2,1,0:T(8,128)(2,1)} %pad_maximum_fusion), channel_id=1, source_target_pairs={{0,1},{1,0},{2,3},{3,2},{4,5},{5,4},{6,7},{7,6},{8,9},{9,8},{10,11... | collective-permute-start | bytes 3538952 | tf_op jit(solution)/shard_map/ppermute | solution.py:34
  45.2 25.9 %collective-permute-start.10 = (bf16[576,512]{1,0:T(8,128)(2,1)}, bf16[576,512]{1,0:T(8,128)(2,1)}, u32[]{:S(2)}, u32[]{:S(2)}) collective-permute-start(bf16[576,512]{1,0:T(8,128)(2,1)} %dynamic-slice_bitcast_fusion), channel_id=1, source_target_pairs={{0,16},{1,17},{2,18},{3,19},{4,20},{5,21},{6,22},{7,23},{8,24},{9,... | collective-permute-start | bytes 1769480 | tf_op jit(solution)/shard_map/ppermute | solution.py:34
  55.7 15.4 %collective-permute-start.7 = (bf16[32,7296]{1,0:T(8,128)(2,1)}, bf16[32,7296]{1,0:T(8,128)(2,1)}, u32[]{:S(2)}, u32[]{:S(2)}) collective-permute-start(bf16[32,7296]{1,0:T(8,128)(2,1)} %slice.8), channel_id=1, source_target_pairs={{0,2},{1,3},{2,4},{3,5},{4,6},{5,7},{6,0},{7,1},{8,10},{9,11},{10,... | collective-permute-start | bytes 1400840 | tf_op jit(solution)/shard_map/ppermute | solution.py:34
  56.6 14.5 %collective-permute-start.9 = (bf16[32,7296]{1,0:T(8,128)(2,1)}, bf16[32,7296]{1,0:T(8,128)(2,1)}, u32[]{:S(2)}, u32[]{:S(2)}) collective-permute-start(bf16[32,7296]{1,0:T(8,128)(2,1)} %slice.9), channel_id=1, source_target_pairs={{0,6},{1,7},{2,0},{3,1},{4,2},{5,3},{6,4},{7,5},{8,14},{9,15},{10,... | collective-permute-start | bytes 1400840 | tf_op jit(solution)/shard_map/ppermute | solution.py:34
  59.9 11.2 %collective-permute-start.11 = (bf16[256,640]{1,0:T(8,128)(2,1)S(1)}, bf16[256,640]{1,0:T(8,128)(2,1)S(1)}, u32[]{:S(2)}, u32[]{:S(2)}) collective-permute-start(bf16[256,640]{1,0:T(8,128)(2,1)S(1)} %bitcast.22), channel_id=1, source_target_pairs={{0,96},{1,97},{2,98},{3,99},{4,100},{5,101},{6,102},{7,103},{8,104... | collective-permute-start | bytes 983048 | tf_op jit(solution)/shard_map/ppermute | solution.py:34
  71.2 7.4 %collective-permute-start.15 = (bf16[576,512]{1,0:T(8,128)(2,1)}, bf16[576,512]{1,0:T(8,128)(2,1)S(1)}, u32[]{:S(2)}, u32[]{:S(2)}) collective-permute-start(bf16[576,512]{1,0:T(8,128)(2,1)} %collective-permute-done.10.refs_5_), channel_id=1, source_target_pairs={{0,1},{1,0},{2,3},{3,2},{4,5},{5,4},{6,7},{7,6},{8,9},{9,8},{10,11... | collective-permute-start | bytes 1769480 | tf_op jit(solution)/shard_map/ppermute | solution.py:34
  76.3 13.2 %collective-permute-start.13 = (bf16[32,7168]{1,0:T(8,128)(2,1)}, bf16[32,7168]{1,0:T(8,128)(2,1)S(1)}, u32[]{:S(2)}, u32[]{:S(2)}) collective-permute-start(bf16[32,7168]{1,0:T(8,128)(2,1)} %get-tuple-element.66), channel_id=1, source_target_pairs={{0,6},{1,7},{2,0},{3,1},{4,2},{5,3},{6,4},{7,5},{8,14},{9,15},{10,... | collective-permute-start | bytes 1376264 | tf_op jit(solution)/shard_map/ppermute | solution.py:34
  76.9 14.1 %collective-permute-start.14 = (bf16[32,7168]{1,0:T(8,128)(2,1)}, bf16[32,7168]{1,0:T(8,128)(2,1)S(1)}, u32[]{:S(2)}, u32[]{:S(2)}) collective-permute-start(bf16[32,7168]{1,0:T(8,128)(2,1)} %get-tuple-element.67), channel_id=1, source_target_pairs={{0,2},{1,3},{2,4},{3,5},{4,6},{5,7},{6,0},{7,1},{8,10},{9,11},{10,... | collective-permute-start | bytes 1376264 | tf_op jit(solution)/shard_map/ppermute | solution.py:34
  78.4 12.8 %collective-permute-start.16 = (bf16[256,640]{1,0:T(8,128)(2,1)S(1)}, bf16[256,640]{1,0:T(8,128)(2,1)S(1)}, u32[]{:S(2)}, u32[]{:S(2)}) collective-permute-start(bf16[256,640]{1,0:T(8,128)(2,1)S(1)} %bitcast.23), channel_id=1, source_target_pairs={{0,64},{1,65},{2,66},{3,67},{4,68},{5,69},{6,70},{7,71},{8,72},{9,... | collective-permute-start | bytes 983048 | tf_op jit(solution)/shard_map/ppermute | solution.py:34
  91.2 21.7 %collective-permute-start.17 = (bf16[64,7168]{1,0:T(8,128)(2,1)S(1)}, bf16[64,7168]{1,0:T(8,128)(2,1)S(1)}, u32[]{:S(2)}, u32[]{:S(2)}) collective-permute-start(bf16[64,7168]{1,0:T(8,128)(2,1)S(1)} %get-tuple-element.77), channel_id=1, source_target_pairs={{0,6},{1,7},{2,0},{3,1},{4,2},{5,3},{6,4},{7,5},{8,14},{9,15},{10,... | collective-permute-start | bytes 2752520 | tf_op jit(solution)/shard_map/ppermute | solution.py:34
  93.1 22.8 %collective-permute-start.18 = (bf16[64,7168]{1,0:T(8,128)(2,1)S(1)}, bf16[64,7168]{1,0:T(8,128)(2,1)S(1)}, u32[]{:S(2)}, u32[]{:S(2)}) collective-permute-start(bf16[64,7168]{1,0:T(8,128)(2,1)S(1)} %get-tuple-element.78), channel_id=1, source_target_pairs={{0,2},{1,3},{2,4},{3,5},{4,6},{5,7},{6,0},{7,1},{8,10},{9,11},{10,... | collective-permute-start | bytes 2752520 | tf_op jit(solution)/shard_map/ppermute | solution.py:34
  93.3 14.1 %collective-permute-start.19 = (bf16[256,640]{1,0:T(8,128)(2,1)S(1)}, bf16[256,640]{1,0:T(8,128)(2,1)S(1)}, u32[]{:S(2)}, u32[]{:S(2)}) collective-permute-start(bf16[256,640]{1,0:T(8,128)(2,1)S(1)} %copy-done.19), channel_id=1, source_target_pairs={{0,96},{1,97},{2,98},{3,99},{4,100},{5,101},{6,102},{7,103},{8,104... | collective-permute-start | bytes 983048 | tf_op jit(solution)/shard_map/ppermute | solution.py:34
  95.7 11.7 %collective-permute-start.20 = (bf16[256,640]{1,0:T(8,128)(2,1)S(1)}, bf16[256,640]{1,0:T(8,128)(2,1)S(1)}, u32[]{:S(2)}, u32[]{:S(2)}) collective-permute-start(bf16[256,640]{1,0:T(8,128)(2,1)S(1)} %copy-done.17), channel_id=1, source_target_pairs={{0,32},{1,33},{2,34},{3,35},{4,36},{5,37},{6,38},{7,39},{8,40},{9,... | collective-permute-start | bytes 983048 | tf_op jit(solution)/shard_map/ppermute | solution.py:34
  105.8 10.2 %collective-permute-start.21 = (bf16[256,640]{1,0:T(8,128)(2,1)}, bf16[256,640]{1,0:T(8,128)(2,1)S(1)}, u32[]{:S(2)}, u32[]{:S(2)}) collective-permute-start(bf16[256,640]{1,0:T(8,128)(2,1)} %get-tuple-element.88), channel_id=1, source_target_pairs={{0,64},{1,65},{2,66},{3,67},{4,68},{5,69},{6,70},{7,71},{8,72},{9,... | collective-permute-start | bytes 983048 | tf_op jit(solution)/shard_map/ppermute | solution.py:34
  118.0 19.0 %all-to-all-start.1 = ((bf16[16,4,7168]{2,1,0:T(4,128)(2,1)}), bf16[16,4,7168]{2,1,0:T(4,128)(2,1)S(1)}, u32[]{:S(2)}, u32[]{:S(2)}) async-start(bf16[16,4,7168]{2,1,0:T(4,128)(2,1)} %reshape.23), calls=%async_computation.1 | async-start | bytes 1835008 | tf_op jit(solution)/shard_map/all_to_all | solution.py:341
  (21 other events, 280.2 us)

commit v5 on v4

--- a/solution.py
+++ b/solution.py
@@ -13,7 +13,7 @@
 QW = 640
 D = 7168
 XW = D + 128
-KC = 1792
+KC = 1024
 SCALE2 = 192.0 ** (-0.5) * math.log2(math.e)
 AXES = ("seq", "exp")
 bf16 = jnp.bfloat16
@@ -266,7 +266,7 @@
             pltpu.VMEM((height, XW), bf16),
             pltpu.VMEM((height, 512), f32),
             pltpu.VMEM((height, D), bf16),
-            pltpu.SemaphoreType.DMA((72,)),
+            pltpu.SemaphoreType.DMA((80,)),
         ],
         compiler_params=pltpu.CompilerParams(vmem_limit_bytes=32 << 20),
         cost_estimate=pl.CostEstimate(

time: 138 us -> 138 us (level)
  transfers between devices with their start and end apart: 24 -> 24, of which waited for: 8 -> 9; matrix products, arithmetic and copies ran while one was open for 5% -> 5% of each run, Pallas kernels for 26% -> 26%
where the time goes in v5:
time: 138 us
  waiting for transfers between devices  52.8 us (38%)
  starting transfers between devices  36.5 us (26%)
  Pallas kernels  36.4 us (26%)
  local copies, waits for them, and re-layouts  7.59 us (6%)
  other arithmetic  3.78 us (3%)
    ppermute x22, waiting for transfers between devices, shift(): return lax.ppermute(a, AXES, pairs)  26.5 us
    ppermute x22, starting transfers between devices, shift(): return lax.ppermute(a, AXES, pairs)  24.2 us
    pallas_call x2, Pallas kernels, attend(): pl.pallas_call(attend_kernel, out_shape=[pltpu.HBM((256, QW), bf16)] * 2,...  20.1 us
    all_to_all x1, waiting for transfers between devices, body(): lax.all_to_all(jnp.broadcast_to(row[None], (16, 4, XW)), 'seq', 0, 0, til...  15.6 us
    pallas_call x2, Pallas kernels, experts(): pl.pallas_call(functools.partial(expert_kernel, count_x=len(xs), fresh=fr...  13.3 us
    all_to_all x1, waiting for transfers between devices, body(): moe = lax.all_to_all(own, 'seq', 0, 0, tiled=True)  10.8 us
    all_to_all x1, starting transfers between devices, body(): lax.all_to_all(jnp.broadcast_to(row[None], (16, 4, XW)), 'seq', 0, 0, til...  7.12 us
    all_to_all x1, starting transfers between devices, body(): moe = lax.all_to_all(own, 'seq', 0, 0, tiled=True)  5.15 us
  transfers between devices with their start and end apart: 24, of which 9 were waited for; matrix products, arithmetic and copies ran while one was open for 5% of the time, Pallas kernels for 26%

profile of v5, /device:TPU:0, one launch (start us, length us, event | category | flops | bytes accessed | tf_op | source)
XLA Modules:
  0.0 138.0 jit_solution(13125790610222510667)
XLA Ops:
  4.2 7.1 %all-to-all-start = ((bf16[16,4,7296]{2,1,0:T(4,128)(2,1)}), bf16[16,4,7296]{2,1,0:T(4,128)(2,1)S(1)}, u32[]{:S(2)}, u32[]{:S(2)}) async-start(bf16[16,4,7296]{2,1,0:T(4,128)(2,1)} %broadcast_in_dim.9), calls=%async_computation | async-start | bytes 1867776 | tf_op jit(solution)/shard_map/all_to_all | solution.py:301
  12.6 15.6 %all-to-all-done = bf16[16,4,7296]{2,1,0:T(4,128)(2,1)S(1)} async-done(((bf16[16,4,7296]{2,1,0:T(4,128)(2,1)}), bf16[16,4,7296]{2,1,0:T(4,128)(2,1)S(1)}, u32[]{:S(2)}, u32[]{:S(2)}) %all-to-all-start) | async-done | bytes 933920 | tf_op jit(solution)/shard_map/all_to_all | solution.py:301
  28.8 2.9 %collective-permute-start.4 = (bf16[576,512]{1,0:T(8,128)(2,1)}, bf16[576,512]{1,0:T(8,128)(2,1)S(1)}, u32[]{:S(2)}, u32[]{:S(2)}) collective-permute-start(bf16[576,512]{1,0:T(8,128)(2,1)} %dynamic-slice_bitcast_fusion), channel_id=1, source_target_pairs={{0,24},{1,25},{2,26},{3,27},{4,28},{5,29},{6,30},{7,31},{8,0},{9,1... | collective-permute-start | bytes 1769480 | tf_op jit(solution)/shard_map/ppermute | solution.py:34
  31.7 1.9 %collective-permute-start.6 = (bf16[64,7296]{1,0:T(8,128)(2,1)S(1)}, bf16[64,7296]{1,0:T(8,128)(2,1)S(1)}, u32[]{:S(2)}, u32[]{:S(2)}) collective-permute-start(bf16[64,7296]{1,0:T(8,128)(2,1)S(1)} %reshape.20.refs_0_), channel_id=1, source_target_pairs={{0,2},{1,3},{2,4},{3,5},{4,6},{5,7},{6,0},{7,1},{8,10},{9,11},{10,... | collective-permute-start | bytes 2801672 | tf_op jit(solution)/shard_map/ppermute | solution.py:34
  33.6 2.1 %collective-permute-start.8 = (bf16[64,7296]{1,0:T(8,128)(2,1)S(1)}, bf16[64,7296]{1,0:T(8,128)(2,1)S(1)}, u32[]{:S(2)}, u32[]{:S(2)}) collective-permute-start(bf16[64,7296]{1,0:T(8,128)(2,1)S(1)} %reshape.20.refs_0_), channel_id=1, source_target_pairs={{0,6},{1,7},{2,0},{3,1},{4,2},{5,3},{6,4},{7,5},{8,14},{9,15},{10,... | collective-permute-start | bytes 2801672 | tf_op jit(solution)/shard_map/ppermute | solution.py:34
  35.7 5.1 %collective-permute-done.5.refs_0_ = bf16[256,640]{1,0:T(8,128)(2,1)S(1)} collective-permute-done((bf16[256,640]{1,0:T(8,128)(2,1)S(1)}, bf16[256,640]{1,0:T(8,128)(2,1)S(1)}, u32[]{:S(2)}, u32[]{:S(2)}) %collective-permute-start.5) | collective-permute-done | bytes 327712 | tf_op jit(solution)/shard_map/ppermute | solution.py:34
  40.8 3.1 %collective-permute-done.3.refs_3_ = bf16[576,512]{1,0:T(8,128)(2,1)S(1)} collective-permute-done((bf16[576,512]{1,0:T(8,128)(2,1)}, bf16[576,512]{1,0:T(8,128)(2,1)S(1)}, u32[]{:S(2)}, u32[]{:S(2)}) %collective-permute-start.3) | collective-permute-done | bytes 589856 | tf_op jit(solution)/shard_map/ppermute | solution.py:34
  45.2 1.5 %collective-permute-start.10 = (bf16[576,512]{1,0:T(8,128)(2,1)}, bf16[576,512]{1,0:T(8,128)(2,1)}, u32[]{:S(2)}, u32[]{:S(2)}) collective-permute-start(bf16[576,512]{1,0:T(8,128)(2,1)} %dynamic-slice_bitcast_fusion), channel_id=1, source_target_pairs={{0,16},{1,17},{2,18},{3,19},{4,20},{5,21},{6,22},{7,23},{8,24},{9,... | collective-permute-start | bytes 1769480 | tf_op jit(solution)/shard_map/ppermute | solution.py:34
  46.7 8.2 %collective-permute-done.6.refs_1_ = bf16[64,7296]{1,0:T(8,128)(2,1)S(1)} collective-permute-done((bf16[64,7296]{1,0:T(8,128)(2,1)S(1)}, bf16[64,7296]{1,0:T(8,128)(2,1)S(1)}, u32[]{:S(2)}, u32[]{:S(2)}) %collective-permute-start.6) | collective-permute-done | bytes 933920 | tf_op jit(solution)/shard_map/ppermute | solution.py:34
  56.6 3.3 %collective-permute-start.9 = (bf16[32,7296]{1,0:T(8,128)(2,1)}, bf16[32,7296]{1,0:T(8,128)(2,1)}, u32[]{:S(2)}, u32[]{:S(2)}) collective-permute-start(bf16[32,7296]{1,0:T(8,128)(2,1)} %slice.9), channel_id=1, source_target_pairs={{0,6},{1,7},{2,0},{3,1},{4,2},{5,3},{6,4},{7,5},{8,14},{9,15},{10,... | collective-permute-start | bytes 1400840 | tf_op jit(solution)/shard_map/ppermute | solution.py:34
  59.9 3.0 %collective-permute-start.11 = (bf16[256,640]{1,0:T(8,128)(2,1)S(1)}, bf16[256,640]{1,0:T(8,128)(2,1)S(1)}, u32[]{:S(2)}, u32[]{:S(2)}) collective-permute-start(bf16[256,640]{1,0:T(8,128)(2,1)S(1)} %bitcast.22), channel_id=1, source_target_pairs={{0,96},{1,97},{2,98},{3,99},{4,100},{5,101},{6,102},{7,103},{8,104... | collective-permute-start | bytes 983048 | tf_op jit(solution)/shard_map/ppermute | solution.py:34
  62.9 8.2 %experts.2 = (bf16[64,7168]{1,0:T(8,128)(2,1)}, bf16[64,7168]{1,0:T(8,128)(2,1)}, bf16[64,7168]{1,0:T(8,128)(2,1)}, bf16[7168,512]{1,0:T(8,128)(2,1)S(1)}, bf16[256,7168]{1,0:T(8,128)(2,1)S(1)}) custom-call(s32[2]{0:T(128)S(1)} %pad_add_fusion.e_ref, bf16[64,7296]{1,0:T(8,128)(2,1)} %copy-done, bf16[64,7296]{1,0:T(8,128)(2,1)} %copy-done.1, ...), custom_call_target="tpu_custom_call" | custom-call | flops 2112000000 | bytes 16760000 | tf_op jit(solution)/shard_map/experts/pallas_call | solution.py:258
  71.3 5.0 %experts.3 = (bf16[32,7168]{1,0:T(8,128)(2,1)}, bf16[32,7168]{1,0:T(8,128)(2,1)}) custom-call(s32[2]{0:T(128)S(1)} %pad_add_fusion.e_ref, bf16[32,7296]{1,0:T(8,128)(2,1)} %collective-permute-done.7.refs_0_, bf16[32,7296]{1,0:T(8,128)(2,1)} %collective-permute-done.9.refs_1_, bf16[7168,512]{1,0:T(8,128)(2,1)S(1)} %get-tuple-element.64.refs_2_, ...), custom_call_target="tpu_custom_call" | custom-call | flops 704000000 | bytes 1920000 | tf_op jit(solution)/shard_map/experts/pallas_call | solution.py:258
  77.0 1.5 %collective-permute-start.14 = (bf16[32,7168]{1,0:T(8,128)(2,1)}, bf16[32,7168]{1,0:T(8,128)(2,1)S(1)}, u32[]{:S(2)}, u32[]{:S(2)}) collective-permute-start(bf16[32,7168]{1,0:T(8,128)(2,1)} %get-tuple-element.67), channel_id=1, source_target_pairs={{0,2},{1,3},{2,4},{3,5},{4,6},{5,7},{6,0},{7,1},{8,10},{9,11},{10,... | collective-permute-start | bytes 1376264 | tf_op jit(solution)/shard_map/ppermute | solution.py:34
  79.4 10.1 %attend.2 = (bf16[256,640]{1,0:T(8,128)(2,1)}, bf16[256,640]{1,0:T(8,128)(2,1)}) custom-call(s32[1]{0:T(128)} %bitcast.10.core_ref, bf16[256,640]{1,0:T(8,128)(2,1)} %copy-done.15, bf16[256,640]{1,0:T(8,128)(2,1)} %copy-done.16, bf16[2,576,512]{2,1,0:T(8,128)(2,1)} %bitcast.28, bf16[576,512]{1,0:T(8,128)(2,1)} %copy-done.7, bf16[576,512]{1,0:T(8,128)(2,1)} %copy-done.8, ...), custom_call_target="tpu_custom_call" | custom-call | flops 4499999744 | bytes 6000000 | tf_op jit(solution)/shard_map/attend/pallas_call | solution.py:126
  91.3 1.8 %collective-permute-start.17 = (bf16[64,7168]{1,0:T(8,128)(2,1)S(1)}, bf16[64,7168]{1,0:T(8,128)(2,1)S(1)}, u32[]{:S(2)}, u32[]{:S(2)}) collective-permute-start(bf16[64,7168]{1,0:T(8,128)(2,1)S(1)} %get-tuple-element.77), channel_id=1, source_target_pairs={{0,6},{1,7},{2,0},{3,1},{4,2},{5,3},{6,4},{7,5},{8,14},{9,15},{10,... | collective-permute-start | bytes 2752520 | tf_op jit(solution)/shard_map/ppermute | solution.py:34
  93.4 2.3 %collective-permute-start.19 = (bf16[256,640]{1,0:T(8,128)(2,1)S(1)}, bf16[256,640]{1,0:T(8,128)(2,1)S(1)}, u32[]{:S(2)}, u32[]{:S(2)}) collective-permute-start(bf16[256,640]{1,0:T(8,128)(2,1)S(1)} %copy-done.19), channel_id=1, source_target_pairs={{0,96},{1,97},{2,98},{3,99},{4,100},{5,101},{6,102},{7,103},{8,104... | collective-permute-start | bytes 983048 | tf_op jit(solution)/shard_map/ppermute | solution.py:34
  95.8 10.0 %attend.3 = (bf16[256,640]{1,0:T(8,128)(2,1)}, bf16[256,640]{1,0:T(8,128)(2,1)}) custom-call(s32[1]{0:T(128)} %bitcast.10.core_ref, bf16[256,640]{1,0:T(8,128)(2,1)} %copy-done.18, bf16[256,640]{1,0:T(8,128)(2,1)} %bitcast.24, bf16[2,576,512]{2,1,0:T(8,128)(2,1)} %bitcast.29, bf16[576,512]{1,0:T(8,128)(2,1)} %copy-done.7, bf16[576,512]{1,0:T(8,128)(2,1)} %copy-done.8, ...), custom_call_target="tpu_custom_call" | custom-call | flops 4499999744 | bytes 6000000 | tf_op jit(solution)/shard_map/attend/pallas_call | solution.py:126
  105.8 1.7 %collective-permute-start.21 = (bf16[256,640]{1,0:T(8,128)(2,1)}, bf16[256,640]{1,0:T(8,128)(2,1)S(1)}, u32[]{:S(2)}, u32[]{:S(2)}) collective-permute-start(bf16[256,640]{1,0:T(8,128)(2,1)} %get-tuple-element.88), channel_id=1, source_target_pairs={{0,64},{1,65},{2,66},{3,67},{4,68},{5,69},{6,70},{7,71},{8,72},{9,... | collective-permute-start | bytes 983048 | tf_op jit(solution)/shard_map/ppermute | solution.py:34
  107.5 5.5 %collective-permute-done.17 = bf16[64,7168]{1,0:T(8,128)(2,1)S(1)} collective-permute-done((bf16[64,7168]{1,0:T(8,128)(2,1)S(1)}, bf16[64,7168]{1,0:T(8,128)(2,1)S(1)}, u32[]{:S(2)}, u32[]{:S(2)}) %collective-permute-start.17) | collective-permute-done | bytes 917536 | tf_op jit(solution)/shard_map/ppermute | solution.py:34
  113.1 2.9 %collective-permute-done.18 = bf16[64,7168]{1,0:T(8,128)(2,1)S(1)} collective-permute-done((bf16[64,7168]{1,0:T(8,128)(2,1)S(1)}, bf16[64,7168]{1,0:T(8,128)(2,1)S(1)}, u32[]{:S(2)}, u32[]{:S(2)}) %collective-permute-start.18) | collective-permute-done | bytes 917536 | tf_op jit(solution)/shard_map/ppermute | solution.py:34
  118.0 5.2 %all-to-all-start.1 = ((bf16[16,4,7168]{2,1,0:T(4,128)(2,1)}), bf16[16,4,7168]{2,1,0:T(4,128)(2,1)S(1)}, u32[]{:S(2)}, u32[]{:S(2)}) async-start(bf16[16,4,7168]{2,1,0:T(4,128)(2,1)} %reshape.23), calls=%async_computation.1 | async-start | bytes 1835008 | tf_op jit(solution)/shard_map/all_to_all | solution.py:341
  123.2 3.0 %merge.1 = bf16[256,512]{1,0:T(8,128)(2,1)} custom-call(bf16[256,640]{1,0:T(8,128)(2,1)} %bitcast.25, bf16[4,576]{1,0:T(4,128)(2,1)} %lat_ref.1, bf16[256,640]{1,0:T(8,128)(2,1)} %get-tuple-element.84.refs_0_, bf16[256,640]{1,0:T(8,128)(2,1)} %copy-done.9, bf16[256,640]{1,0:T(8,128)(2,1)} %copy-done.11, bf16[256,640]{1,0:T(8,128)(2,1)} %copy-done.10), custom_call_target="tpu_custom_call" | custom-call | tf_op jit(solution)/shard_map/merge/pallas_call | solution.py:169
  126.2 10.8 %all-to-all-done.1 = bf16[16,4,7168]{2,1,0:T(4,128)(2,1)S(1)} async-done(((bf16[16,4,7168]{2,1,0:T(4,128)(2,1)}), bf16[16,4,7168]{2,1,0:T(4,128)(2,1)S(1)}, u32[]{:S(2)}, u32[]{:S(2)}) %all-to-all-start.1) | async-done | bytes 917536 | tf_op jit(solution)/shard_map/all_to_all | solution.py:341
  (89 shorter events, 15.1 us)
Async XLA Ops:
  0.7 27.7 %collective-permute-start = (bf16[7168,128]{1,0:T(8,128)(2,1)}, bf16[7168,128]{1,0:T(8,128)(2,1)}, u32[]{:S(2)}, u32[]{:S(2)}) collective-permute-start(bf16[7168,128]{1,0:T(8,128)(2,1)} %bitcast.15), channel_id=1, source_target_pairs={{0,1},{1,0},{2,3},{3,2},{4,5},{5,4},{6,7},{7,6},{8,9},{9,8},{10,11... | collective-permute-start | bytes 5505032 | tf_op jit(solution)/shard_map/ppermute | solution.py:34
  0.7 27.6 %collective-permute-start.1 = (bf16[7168,128]{1,0:T(8,128)(2,1)}, bf16[7168,128]{1,0:T(8,128)(2,1)}, u32[]{:S(2)}, u32[]{:S(2)}) collective-permute-start(bf16[7168,128]{1,0:T(8,128)(2,1)} %bitcast.17), channel_id=1, source_target_pairs={{0,1},{1,0},{2,3},{3,2},{4,5},{5,4},{6,7},{7,6},{8,9},{9,8},{10,11... | collective-permute-start | bytes 5505032 | tf_op jit(solution)/shard_map/ppermute | solution.py:34
  1.2 27.1 %collective-permute-start.2 = (bf16[128,7168]{1,0:T(8,128)(2,1)}, bf16[128,7168]{1,0:T(8,128)(2,1)}, u32[]{:S(2)}, u32[]{:S(2)}) collective-permute-start(bf16[128,7168]{1,0:T(8,128)(2,1)} %bitcast.19), channel_id=1, source_target_pairs={{0,1},{1,0},{2,3},{3,2},{4,5},{5,4},{6,7},{7,6},{8,9},{9,8},{10,11... | collective-permute-start | bytes 5505032 | tf_op jit(solution)/shard_map/ppermute | solution.py:34
  4.2 23.9 %all-to-all-start = ((bf16[16,4,7296]{2,1,0:T(4,128)(2,1)}), bf16[16,4,7296]{2,1,0:T(4,128)(2,1)S(1)}, u32[]{:S(2)}, u32[]{:S(2)}) async-start(bf16[16,4,7296]{2,1,0:T(4,128)(2,1)} %broadcast_in_dim.9), calls=%async_computation | async-start | bytes 1867776 | tf_op jit(solution)/shard_map/all_to_all | solution.py:301
  28.4 15.6 %collective-permute-start.3 = (bf16[576,512]{1,0:T(8,128)(2,1)}, bf16[576,512]{1,0:T(8,128)(2,1)S(1)}, u32[]{:S(2)}, u32[]{:S(2)}) collective-permute-start(bf16[576,512]{1,0:T(8,128)(2,1)} %dynamic-slice_bitcast_fusion), channel_id=1, source_target_pairs={{0,8},{1,9},{2,10},{3,11},{4,12},{5,13},{6,14},{7,15},{8,16},{9,17... | collective-permute-start | bytes 1769480 | tf_op jit(solution)/shard_map/ppermute | solution.py:34
  28.8 15.2 %collective-permute-start.4 = (bf16[576,512]{1,0:T(8,128)(2,1)}, bf16[576,512]{1,0:T(8,128)(2,1)S(1)}, u32[]{:S(2)}, u32[]{:S(2)}) collective-permute-start(bf16[576,512]{1,0:T(8,128)(2,1)} %dynamic-slice_bitcast_fusion), channel_id=1, source_target_pairs={{0,24},{1,25},{2,26},{3,27},{4,28},{5,29},{6,30},{7,31},{8,0},{9,1... | collective-permute-start | bytes 1769480 | tf_op jit(solution)/shard_map/ppermute | solution.py:34
  31.7 9.1 %collective-permute-start.5 = (bf16[256,640]{1,0:T(8,128)(2,1)S(1)}, bf16[256,640]{1,0:T(8,128)(2,1)S(1)}, u32[]{:S(2)}, u32[]{:S(2)}) collective-permute-start(bf16[256,640]{1,0:T(8,128)(2,1)S(1)} %bitcast.21), channel_id=1, source_target_pairs={{0,32},{1,33},{2,34},{3,35},{4,36},{5,37},{6,38},{7,39},{8,40},{9,... | collective-permute-start | bytes 983048 | tf_op jit(solution)/shard_map/ppermute | solution.py:34
  31.7 23.2 %collective-permute-start.6 = (bf16[64,7296]{1,0:T(8,128)(2,1)S(1)}, bf16[64,7296]{1,0:T(8,128)(2,1)S(1)}, u32[]{:S(2)}, u32[]{:S(2)}) collective-permute-start(bf16[64,7296]{1,0:T(8,128)(2,1)S(1)} %reshape.20.refs_0_), channel_id=1, source_target_pairs={{0,2},{1,3},{2,4},{3,5},{4,6},{5,7},{6,0},{7,1},{8,10},{9,11},{10,... | collective-permute-start | bytes 2801672 | tf_op jit(solution)/shard_map/ppermute | solution.py:34
  33.6 22.1 %collective-permute-start.8 = (bf16[64,7296]{1,0:T(8,128)(2,1)S(1)}, bf16[64,7296]{1,0:T(8,128)(2,1)S(1)}, u32[]{:S(2)}, u32[]{:S(2)}) collective-permute-start(bf16[64,7296]{1,0:T(8,128)(2,1)S(1)} %reshape.20.refs_0_), channel_id=1, source_target_pairs={{0,6},{1,7},{2,0},{3,1},{4,2},{5,3},{6,4},{7,5},{8,14},{9,15},{10,... | collective-permute-start | bytes 2801672 | tf_op jit(solution)/shard_map/ppermute | solution.py:34
  45.2 26.0 %collective-permute-start.12 = (bf16[2,576,512]{2,1,0:T(8,128)(2,1)}, bf16[2,576,512]{2,1,0:T(8,128)(2,1)}, u32[]{:S(2)}, u32[]{:S(2)}) collective-permute-start(bf16[2,576,512]{2,1,0:T(8,128)(2,1)} %pad_maximum_fusion), channel_id=1, source_target_pairs={{0,1},{1,0},{2,3},{3,2},{4,5},{5,4},{6,7},{7,6},{8,9},{9,8},{10,11... | collective-permute-start | bytes 3538952 | tf_op jit(solution)/shard_map/ppermute | solution.py:34
  45.2 26.0 %collective-permute-start.10 = (bf16[576,512]{1,0:T(8,128)(2,1)}, bf16[576,512]{1,0:T(8,128)(2,1)}, u32[]{:S(2)}, u32[]{:S(2)}) collective-permute-start(bf16[576,512]{1,0:T(8,128)(2,1)} %dynamic-slice_bitcast_fusion), channel_id=1, source_target_pairs={{0,16},{1,17},{2,18},{3,19},{4,20},{5,21},{6,22},{7,23},{8,24},{9,... | collective-permute-start | bytes 1769480 | tf_op jit(solution)/shard_map/ppermute | solution.py:34
  55.7 15.5 %collective-permute-start.7 = (bf16[32,7296]{1,0:T(8,128)(2,1)}, bf16[32,7296]{1,0:T(8,128)(2,1)}, u32[]{:S(2)}, u32[]{:S(2)}) collective-permute-start(bf16[32,7296]{1,0:T(8,128)(2,1)} %slice.8), channel_id=1, source_target_pairs={{0,2},{1,3},{2,4},{3,5},{4,6},{5,7},{6,0},{7,1},{8,10},{9,11},{10,... | collective-permute-start | bytes 1400840 | tf_op jit(solution)/shard_map/ppermute | solution.py:34
  56.6 14.6 %collective-permute-start.9 = (bf16[32,7296]{1,0:T(8,128)(2,1)}, bf16[32,7296]{1,0:T(8,128)(2,1)}, u32[]{:S(2)}, u32[]{:S(2)}) collective-permute-start(bf16[32,7296]{1,0:T(8,128)(2,1)} %slice.9), channel_id=1, source_target_pairs={{0,6},{1,7},{2,0},{3,1},{4,2},{5,3},{6,4},{7,5},{8,14},{9,15},{10,... | collective-permute-start | bytes 1400840 | tf_op jit(solution)/shard_map/ppermute | solution.py:34
  59.9 11.3 %collective-permute-start.11 = (bf16[256,640]{1,0:T(8,128)(2,1)S(1)}, bf16[256,640]{1,0:T(8,128)(2,1)S(1)}, u32[]{:S(2)}, u32[]{:S(2)}) collective-permute-start(bf16[256,640]{1,0:T(8,128)(2,1)S(1)} %bitcast.22), channel_id=1, source_target_pairs={{0,96},{1,97},{2,98},{3,99},{4,100},{5,101},{6,102},{7,103},{8,104... | collective-permute-start | bytes 983048 | tf_op jit(solution)/shard_map/ppermute | solution.py:34
  71.2 7.3 %collective-permute-start.15 = (bf16[576,512]{1,0:T(8,128)(2,1)}, bf16[576,512]{1,0:T(8,128)(2,1)S(1)}, u32[]{:S(2)}, u32[]{:S(2)}) collective-permute-start(bf16[576,512]{1,0:T(8,128)(2,1)} %collective-permute-done.10.refs_5_), channel_id=1, source_target_pairs={{0,1},{1,0},{2,3},{3,2},{4,5},{5,4},{6,7},{7,6},{8,9},{9,8},{10,11... | collective-permute-start | bytes 1769480 | tf_op jit(solution)/shard_map/ppermute | solution.py:34
  76.4 13.2 %collective-permute-start.13 = (bf16[32,7168]{1,0:T(8,128)(2,1)}, bf16[32,7168]{1,0:T(8,128)(2,1)S(1)}, u32[]{:S(2)}, u32[]{:S(2)}) collective-permute-start(bf16[32,7168]{1,0:T(8,128)(2,1)} %get-tuple-element.66), channel_id=1, source_target_pairs={{0,6},{1,7},{2,0},{3,1},{4,2},{5,3},{6,4},{7,5},{8,14},{9,15},{10,... | collective-permute-start | bytes 1376264 | tf_op jit(solution)/shard_map/ppermute | solution.py:34
  77.0 14.1 %collective-permute-start.14 = (bf16[32,7168]{1,0:T(8,128)(2,1)}, bf16[32,7168]{1,0:T(8,128)(2,1)S(1)}, u32[]{:S(2)}, u32[]{:S(2)}) collective-permute-start(bf16[32,7168]{1,0:T(8,128)(2,1)} %get-tuple-element.67), channel_id=1, source_target_pairs={{0,2},{1,3},{2,4},{3,5},{4,6},{5,7},{6,0},{7,1},{8,10},{9,11},{10,... | collective-permute-start | bytes 1376264 | tf_op jit(solution)/shard_map/ppermute | solution.py:34
  78.5 12.8 %collective-permute-start.16 = (bf16[256,640]{1,0:T(8,128)(2,1)S(1)}, bf16[256,640]{1,0:T(8,128)(2,1)S(1)}, u32[]{:S(2)}, u32[]{:S(2)}) collective-permute-start(bf16[256,640]{1,0:T(8,128)(2,1)S(1)} %bitcast.23), channel_id=1, source_target_pairs={{0,64},{1,65},{2,66},{3,67},{4,68},{5,69},{6,70},{7,71},{8,72},{9,... | collective-permute-start | bytes 983048 | tf_op jit(solution)/shard_map/ppermute | solution.py:34
  91.3 21.7 %collective-permute-start.17 = (bf16[64,7168]{1,0:T(8,128)(2,1)S(1)}, bf16[64,7168]{1,0:T(8,128)(2,1)S(1)}, u32[]{:S(2)}, u32[]{:S(2)}) collective-permute-start(bf16[64,7168]{1,0:T(8,128)(2,1)S(1)} %get-tuple-element.77), channel_id=1, source_target_pairs={{0,6},{1,7},{2,0},{3,1},{4,2},{5,3},{6,4},{7,5},{8,14},{9,15},{10,... | collective-permute-start | bytes 2752520 | tf_op jit(solution)/shard_map/ppermute | solution.py:34
  93.2 22.8 %collective-permute-start.18 = (bf16[64,7168]{1,0:T(8,128)(2,1)S(1)}, bf16[64,7168]{1,0:T(8,128)(2,1)S(1)}, u32[]{:S(2)}, u32[]{:S(2)}) collective-permute-start(bf16[64,7168]{1,0:T(8,128)(2,1)S(1)} %get-tuple-element.78), channel_id=1, source_target_pairs={{0,2},{1,3},{2,4},{3,5},{4,6},{5,7},{6,0},{7,1},{8,10},{9,11},{10,... | collective-permute-start | bytes 2752520 | tf_op jit(solution)/shard_map/ppermute | solution.py:34
  93.4 14.1 %collective-permute-start.19 = (bf16[256,640]{1,0:T(8,128)(2,1)S(1)}, bf16[256,640]{1,0:T(8,128)(2,1)S(1)}, u32[]{:S(2)}, u32[]{:S(2)}) collective-permute-start(bf16[256,640]{1,0:T(8,128)(2,1)S(1)} %copy-done.19), channel_id=1, source_target_pairs={{0,96},{1,97},{2,98},{3,99},{4,100},{5,101},{6,102},{7,103},{8,104... | collective-permute-start | bytes 983048 | tf_op jit(solution)/shard_map/ppermute | solution.py:34
  95.8 11.7 %collective-permute-start.20 = (bf16[256,640]{1,0:T(8,128)(2,1)S(1)}, bf16[256,640]{1,0:T(8,128)(2,1)S(1)}, u32[]{:S(2)}, u32[]{:S(2)}) collective-permute-start(bf16[256,640]{1,0:T(8,128)(2,1)S(1)} %copy-done.17), channel_id=1, source_target_pairs={{0,32},{1,33},{2,34},{3,35},{4,36},{5,37},{6,38},{7,39},{8,40},{9,... | collective-permute-start | bytes 983048 | tf_op jit(solution)/shard_map/ppermute | solution.py:34
  105.8 10.2 %collective-permute-start.21 = (bf16[256,640]{1,0:T(8,128)(2,1)}, bf16[256,640]{1,0:T(8,128)(2,1)S(1)}, u32[]{:S(2)}, u32[]{:S(2)}) collective-permute-start(bf16[256,640]{1,0:T(8,128)(2,1)} %get-tuple-element.88), channel_id=1, source_target_pairs={{0,64},{1,65},{2,66},{3,67},{4,68},{5,69},{6,70},{7,71},{8,72},{9,... | collective-permute-start | bytes 983048 | tf_op jit(solution)/shard_map/ppermute | solution.py:34
  118.0 19.0 %all-to-all-start.1 = ((bf16[16,4,7168]{2,1,0:T(4,128)(2,1)}), bf16[16,4,7168]{2,1,0:T(4,128)(2,1)S(1)}, u32[]{:S(2)}, u32[]{:S(2)}) async-start(bf16[16,4,7168]{2,1,0:T(4,128)(2,1)} %reshape.23), calls=%async_computation.1 | async-start | bytes 1835008 | tf_op jit(solution)/shard_map/all_to_all | solution.py:341
  (21 other events, 280.2 us)
